TPU v7x, 32 devices: a whole 2x2x4 slice. The times are simulated.
32 devices in a mesh: ctx: 16 (over z, x, core), fsdp: 2 (over y).
Axes of the slice: x: 2, y: 2, z: 4, core: 2. Of those that a mesh axis runs over, the one named last changes fastest.
Arguments:
- tokens: bfloat16 [2, 2048, 2048], P('fsdp', 'ctx'), may hold values from -6 to 6
- doc_lengths: int32 [2, 8], P('fsdp'), may hold values from 1 to 1024, 2048 in all within a row
- ln1_gain: bfloat16 [2048], P(('ctx', 'fsdp')), may hold values from 0.099609375 to 1.8984375
- ln1_bias: bfloat16 [2048], P(('ctx', 'fsdp')), may hold values from -1.75 to 1.75
- w_qkv: bfloat16 [2048, 6144], P(('ctx', 'fsdp')), may hold values from -0.125 to 0.125
- bias_q: bfloat16 [2048], P(('ctx', 'fsdp')), may hold values from -3 to 3
- bias_v: bfloat16 [2048], P(('ctx', 'fsdp')), may hold values from -3 to 3
- w_out: bfloat16 [2048, 2048], P(('ctx', 'fsdp')), may hold values from -0.25 to 0.25
- b_out: bfloat16 [2048], P(('ctx', 'fsdp')), may hold values from -1.75 to 1.75
- ln2_gain: bfloat16 [2048], P(('ctx', 'fsdp')), may hold values from 0.099609375 to 1.8984375
- ln2_bias: bfloat16 [2048], P(('ctx', 'fsdp')), may hold values from -1.75 to 1.75
- w_up: bfloat16 [2048, 8192], P(('ctx', 'fsdp')), may hold values from -0.125 to 0.125
- b_up: bfloat16 [8192], P(('ctx', 'fsdp')), may hold values from -3 to 3
- w_down: bfloat16 [8192, 2048], P(('ctx', 'fsdp')), may hold values from -0.0625 to 0.0625
- b_down: bfloat16 [2048], P(('ctx', 'fsdp')), may hold values from -1.75 to 1.75
- cotangent: bfloat16 [2, 2048, 2048], P('fsdp', 'ctx'), may hold values from -6 to 6
Outputs:
- outputs: bfloat16 [2, 2048, 2048], P('fsdp', 'ctx')
- grad_tokens: float32 [2, 2048, 2048], P('fsdp', 'ctx')
- grad_ln1_gain: float32 [2048], P(('ctx', 'fsdp'))
- grad_ln1_bias: float32 [2048], P(('ctx', 'fsdp'))
- grad_w_qkv: float32 [2048, 6144], P(('ctx', 'fsdp'))
- grad_bias_q: float32 [2048], P(('ctx', 'fsdp'))
- grad_bias_v: float32 [2048], P(('ctx', 'fsdp'))
- grad_w_out: float32 [2048, 2048], P(('ctx', 'fsdp'))
- grad_b_out: float32 [2048], P(('ctx', 'fsdp'))
- grad_ln2_gain: float32 [2048], P(('ctx', 'fsdp'))
- grad_ln2_bias: float32 [2048], P(('ctx', 'fsdp'))
- grad_w_up: float32 [2048, 8192], P(('ctx', 'fsdp'))
- grad_b_up: float32 [8192], P(('ctx', 'fsdp'))
- grad_w_down: float32 [8192, 2048], P(('ctx', 'fsdp'))
- grad_b_down: float32 [2048], P(('ctx', 'fsdp'))
Inputs may be any that keep to these rules, and one draw needn't show every extreme that they name: `doc_lengths`: each row lists the lengths of 8 documents that together fill one sequence of 2048 positions in order; in every row the longest is exactly 1024.
All inputs are finite; a program needn't handle non-finite values.
Results may differ from a plain program's by a relative error of at most 0.015.
Values may be sent and summed in bfloat16 or wider, within the bound.
A program may use at most 576 MiB of HBM per device.

v0:
```python
import math

import jax
import jax.numpy as jnp
from jax import lax
from jax.sharding import PartitionSpec as P

HEAD_DIM = 64


epsilon = 1e-05


def layer_norm(values, gain, shift):
    mean_value = jnp.mean(values, axis=-1, keepdims=True)
    centred = values - mean_value
    variance = jnp.mean(centred * centred, axis=-1, keepdims=True)
    return centred * lax.rsqrt(variance + epsilon) * gain + shift


def gelu_exact(pre_activation):
    return jax.nn.gelu(pre_activation, approximate=False)


def head_slopes(head_count):
    return 2.0 ** (-8.0 * (jnp.arange(head_count, dtype=jnp.float32) + 1.0) / head_count)


def layout_position(row_index, tok_rows, ctx_count):
    half_rows = tok_rows // 2
    device_index = row_index // tok_rows
    within = row_index % tok_rows
    block_index = jnp.where(within < half_rows, device_index, 2 * ctx_count - 1 - device_index)
    return block_index * half_rows + within % half_rows


def segment_of(positions, doc_starts):
    return jnp.sum((doc_starts[None, :] <= positions[:, None]).astype(jnp.int32), axis=1) - 1


def masked_scores(query_heads, key_block, key_index, query_pos, query_seg, context):
    doc_starts, tok_rows, ctx_count, slopes = context
    rows_count = key_block.shape[0]
    head_count = query_heads.shape[1]
    head_dim = query_heads.shape[2]
    key_heads = key_block.reshape(rows_count, head_count, head_dim)
    raw = jnp.einsum(
        "qhd,khd->hqk", query_heads, key_heads, preferred_element_type=jnp.float32
    ) * head_dim ** (-0.5)
    key_pos = layout_position(key_index, tok_rows, ctx_count)
    key_seg = segment_of(key_pos, doc_starts)
    distance = (query_pos[:, None] - key_pos[None, :]).astype(jnp.float32)
    allowed = (query_seg[:, None] == key_seg[None, :]) & (distance >= 0)
    return jnp.where(allowed[None], raw - slopes[:, None, None] * distance[None], -1e30)


def on_device(
    tokens,
    doc_lengths,
    ln1_gain,
    ln1_bias,
    w_qkv,
    bias_q,
    bias_v,
    w_out,
    b_out,
    ln2_gain,
    ln2_bias,
    w_up,
    b_up,
    w_down,
    b_down,
    cotangent,
):
    ctx_count = lax.axis_size("ctx")
    ctx_rank = lax.axis_index("ctx")
    tok_rows = tokens.shape[1]
    model_width = tokens.shape[2]
    head_count = model_width // HEAD_DIM
    seq_len = tok_rows * ctx_count
    block_rows = math.gcd(512, seq_len)
    block_count = seq_len // block_rows
    lengths = doc_lengths[0]
    doc_starts = jnp.cumsum(lengths) - lengths
    query_index = ctx_rank * tok_rows + jnp.arange(tok_rows, dtype=jnp.int32)
    query_pos = layout_position(query_index, tok_rows, ctx_count)
    query_seg = segment_of(query_pos, doc_starts)
    context = (doc_starts, tok_rows, ctx_count, head_slopes(head_count))
    block_ids = jnp.arange(block_count, dtype=jnp.int32)
    block_offsets = jnp.arange(block_rows, dtype=jnp.int32)
    attn_set = (
        lax.all_gather(ln1_gain, ("ctx", "fsdp"), axis=0, tiled=True),
        lax.all_gather(ln1_bias, ("ctx", "fsdp"), axis=0, tiled=True),
        lax.all_gather(w_qkv, ("ctx", "fsdp"), axis=0, tiled=True),
        lax.all_gather(bias_q, ("ctx", "fsdp"), axis=0, tiled=True),
        lax.all_gather(bias_v, ("ctx", "fsdp"), axis=0, tiled=True),
        lax.all_gather(w_out, ("ctx", "fsdp"), axis=0, tiled=True),
        lax.all_gather(b_out, ("ctx", "fsdp"), axis=0, tiled=True),
    )
    gain_one = attn_set[0].astype(jnp.float32)
    shift_one = attn_set[1].astype(jnp.float32)
    inputs = tokens[0].astype(jnp.float32)
    normed = layer_norm(inputs, gain_one, shift_one).astype(jnp.bfloat16)
    projected = jnp.dot(normed, attn_set[2], preferred_element_type=jnp.float32)
    queries = (projected[:, :model_width] + attn_set[3].astype(jnp.float32)).astype(jnp.bfloat16)
    key_rows = projected[:, model_width : 2 * model_width].astype(jnp.bfloat16)
    value_rows = (projected[:, 2 * model_width :] + attn_set[4].astype(jnp.float32)).astype(
        jnp.bfloat16
    )
    all_keys, all_values = (
        lax.all_gather(key_rows, "ctx", axis=0, tiled=True),
        lax.all_gather(value_rows, "ctx", axis=0, tiled=True),
    )
    query_heads = queries.reshape(tok_rows, head_count, HEAD_DIM)
    key_stack = all_keys.reshape(block_count, block_rows, model_width)
    value_stack = all_values.reshape(block_count, block_rows, model_width)

    def total_step(carried, pieces):
        running_top, running_sum = carried
        key_block, block_id = pieces
        scores = masked_scores(
            query_heads,
            key_block,
            block_id * block_rows + block_offsets,
            query_pos,
            query_seg,
            context,
        )
        new_top = jnp.maximum(running_top, jnp.max(scores, axis=-1))
        running_sum = running_sum * jnp.exp(running_top - new_top) + jnp.sum(
            jnp.exp(scores - new_top[:, :, None]), axis=-1
        )
        return ((new_top, running_sum), None)

    initial = (
        jnp.full((head_count, tok_rows), -1e30, jnp.float32),
        jnp.zeros((head_count, tok_rows), jnp.float32),
    )
    (final_top, final_sum), unused_total = lax.scan(total_step, initial, (key_stack, block_ids))
    log_total = final_top + jnp.log(final_sum)

    def output_step(accum, pieces):
        key_block, value_block, block_id = pieces
        scores = masked_scores(
            query_heads,
            key_block,
            block_id * block_rows + block_offsets,
            query_pos,
            query_seg,
            context,
        )
        probs = jnp.exp(scores - log_total[:, :, None]).astype(jnp.bfloat16)
        value_heads = value_block.reshape(block_rows, head_count, HEAD_DIM)
        return (
            accum
            + jnp.einsum("hqk,khd->qhd", probs, value_heads, preferred_element_type=jnp.float32),
            None,
        )

    attended_heads, unused_output = lax.scan(
        output_step,
        jnp.zeros((tok_rows, head_count, HEAD_DIM), jnp.float32),
        (key_stack, value_stack, block_ids),
    )
    attended = attended_heads.reshape(tok_rows, model_width).astype(jnp.bfloat16)
    middle = (
        inputs
        + jnp.dot(attended, attn_set[5], preferred_element_type=jnp.float32)
        + attn_set[6].astype(jnp.float32)
    )
    mlp_set = (
        lax.all_gather(ln2_gain, ("ctx", "fsdp"), axis=0, tiled=True),
        lax.all_gather(ln2_bias, ("ctx", "fsdp"), axis=0, tiled=True),
        lax.all_gather(w_up, ("ctx", "fsdp"), axis=0, tiled=True),
        lax.all_gather(b_up, ("ctx", "fsdp"), axis=0, tiled=True),
        lax.all_gather(w_down, ("ctx", "fsdp"), axis=0, tiled=True),
        lax.all_gather(b_down, ("ctx", "fsdp"), axis=0, tiled=True),
    )
    gain_two = mlp_set[0].astype(jnp.float32)
    shift_two = mlp_set[1].astype(jnp.float32)
    normed_two = layer_norm(middle, gain_two, shift_two).astype(jnp.bfloat16)
    hidden = jnp.dot(normed_two, mlp_set[2], preferred_element_type=jnp.float32) + mlp_set[
        3
    ].astype(jnp.float32)
    activated = gelu_exact(hidden).astype(jnp.bfloat16)
    outputs = (
        middle
        + jnp.dot(activated, mlp_set[4], preferred_element_type=jnp.float32)
        + mlp_set[5].astype(jnp.float32)
    ).astype(jnp.bfloat16)
    mlp_back = (
        lax.all_gather(ln2_gain, ("ctx", "fsdp"), axis=0, tiled=True),
        lax.all_gather(ln2_bias, ("ctx", "fsdp"), axis=0, tiled=True),
        lax.all_gather(w_up, ("ctx", "fsdp"), axis=0, tiled=True),
        lax.all_gather(b_up, ("ctx", "fsdp"), axis=0, tiled=True),
        lax.all_gather(w_down, ("ctx", "fsdp"), axis=0, tiled=True),
        lax.all_gather(b_down, ("ctx", "fsdp"), axis=0, tiled=True),
    )
    grad_out = cotangent[0]
    grad_out_full = grad_out.astype(jnp.float32)
    grad_b_down = jnp.sum(grad_out_full, axis=0)
    grad_w_down = jnp.einsum("tf,td->fd", activated, grad_out, preferred_element_type=jnp.float32)
    grad_activated = jnp.einsum(
        "td,fd->tf", grad_out, mlp_back[4], preferred_element_type=jnp.float32
    )
    unused_gelu, gelu_pull = jax.vjp(gelu_exact, hidden)
    grad_hidden = gelu_pull(grad_activated)[0].astype(jnp.bfloat16)
    grad_b_up = jnp.sum(grad_hidden.astype(jnp.float32), axis=0)
    grad_w_up = jnp.einsum("td,tf->df", normed_two, grad_hidden, preferred_element_type=jnp.float32)
    grad_normed_two = jnp.einsum(
        "tf,df->td", grad_hidden, mlp_back[2], preferred_element_type=jnp.float32
    )
    unused_norm, second_pull = jax.vjp(
        layer_norm, middle, mlp_back[0].astype(jnp.float32), mlp_back[1].astype(jnp.float32)
    )
    grad_mid_norm, grad_gain_two, grad_shift_two = second_pull(grad_normed_two)
    grad_middle = grad_out_full + grad_mid_norm
    mlp_grads = (
        lax.psum_scatter(grad_gain_two, ("ctx", "fsdp"), scatter_dimension=0, tiled=True),
        lax.psum_scatter(grad_shift_two, ("ctx", "fsdp"), scatter_dimension=0, tiled=True),
        lax.psum_scatter(grad_w_up, ("ctx", "fsdp"), scatter_dimension=0, tiled=True),
        lax.psum_scatter(grad_b_up, ("ctx", "fsdp"), scatter_dimension=0, tiled=True),
        lax.psum_scatter(grad_w_down, ("ctx", "fsdp"), scatter_dimension=0, tiled=True),
        lax.psum_scatter(grad_b_down, ("ctx", "fsdp"), scatter_dimension=0, tiled=True),
    )
    attn_back = (
        lax.all_gather(ln1_gain, ("ctx", "fsdp"), axis=0, tiled=True),
        lax.all_gather(ln1_bias, ("ctx", "fsdp"), axis=0, tiled=True),
        lax.all_gather(w_qkv, ("ctx", "fsdp"), axis=0, tiled=True),
        lax.all_gather(bias_q, ("ctx", "fsdp"), axis=0, tiled=True),
        lax.all_gather(bias_v, ("ctx", "fsdp"), axis=0, tiled=True),
        lax.all_gather(w_out, ("ctx", "fsdp"), axis=0, tiled=True),
        lax.all_gather(b_out, ("ctx", "fsdp"), axis=0, tiled=True),
    )
    grad_branch = grad_middle.astype(jnp.bfloat16)
    grad_b_out = jnp.sum(grad_branch.astype(jnp.float32), axis=0)
    grad_w_out = jnp.einsum("td,te->de", attended, grad_branch, preferred_element_type=jnp.float32)
    grad_attended = jnp.einsum(
        "te,de->td", grad_branch, attn_back[5], preferred_element_type=jnp.float32
    ).astype(jnp.bfloat16)
    grad_heads = grad_attended.reshape(tok_rows, head_count, HEAD_DIM)
    row_delta = jnp.sum(grad_heads.astype(jnp.float32) * attended_heads, axis=-1).T
    back_keys, back_values = (
        lax.all_gather(key_rows, "ctx", axis=0, tiled=True),
        lax.all_gather(value_rows, "ctx", axis=0, tiled=True),
    )
    back_key_stack = back_keys.reshape(block_count, block_rows, model_width)
    back_value_stack = back_values.reshape(block_count, block_rows, model_width)

    def query_step(accum, pieces):
        key_block, value_block, block_id = pieces
        scores = masked_scores(
            query_heads,
            key_block,
            block_id * block_rows + block_offsets,
            query_pos,
            query_seg,
            context,
        )
        probs = jnp.exp(scores - log_total[:, :, None])
        value_heads = value_block.reshape(block_rows, head_count, HEAD_DIM)
        grad_probs = jnp.einsum(
            "qhd,khd->hqk", grad_heads, value_heads, preferred_element_type=jnp.float32
        )
        grad_scores = (probs * (grad_probs - row_delta[:, :, None])).astype(jnp.bfloat16)
        key_heads = key_block.reshape(block_rows, head_count, HEAD_DIM)
        return (
            accum
            + jnp.einsum(
                "hqk,khd->qhd", grad_scores, key_heads, preferred_element_type=jnp.float32
            ),
            None,
        )

    grad_query_heads, unused_query = lax.scan(
        query_step,
        jnp.zeros((tok_rows, head_count, HEAD_DIM), jnp.float32),
        (back_key_stack, back_value_stack, block_ids),
    )
    grad_queries = (
        (grad_query_heads * HEAD_DIM ** (-0.5)).reshape(tok_rows, model_width).astype(jnp.bfloat16)
    )
    piece_rows = math.gcd(512, tok_rows * lax.axis_size("ctx"))
    piece_offsets = jnp.arange(piece_rows, dtype=jnp.int32)

    def one_piece(offset):
        first_row = offset * piece_rows
        key_block = lax.dynamic_slice_in_dim(back_keys, first_row, piece_rows, 0)
        value_block = lax.dynamic_slice_in_dim(back_values, first_row, piece_rows, 0)
        scores = masked_scores(
            query_heads, key_block, first_row + piece_offsets, query_pos, query_seg, context
        )
        probs = jnp.exp(scores - log_total[:, :, None])
        value_heads = value_block.reshape(piece_rows, head_count, HEAD_DIM)
        grad_probs = jnp.einsum(
            "qhd,khd->hqk", grad_heads, value_heads, preferred_element_type=jnp.float32
        )
        grad_scores = (probs * (grad_probs - row_delta[:, :, None])).astype(jnp.bfloat16)
        grad_key_part = jnp.einsum(
            "hqk,qhd->khd", grad_scores, query_heads, preferred_element_type=jnp.float32
        ) * HEAD_DIM ** (-0.5)
        grad_value_part = jnp.einsum(
            "hqk,qhd->khd",
            probs.astype(jnp.bfloat16),
            grad_heads,
            preferred_element_type=jnp.float32,
        )
        return jnp.concatenate(
            [
                grad_key_part.reshape(piece_rows, model_width),
                grad_value_part.reshape(piece_rows, model_width),
            ],
            axis=1,
        )

    terms = lax.map(
        one_piece, jnp.arange(tok_rows * lax.axis_size("ctx") // piece_rows, dtype=jnp.int32)
    )
    key_value_sum = lax.psum_scatter(
        terms.reshape(tok_rows * lax.axis_size("ctx"), 2 * model_width),
        "ctx",
        scatter_dimension=0,
        tiled=True,
    )
    grad_keys = key_value_sum[:, :model_width].astype(jnp.bfloat16)
    grad_values = key_value_sum[:, model_width:].astype(jnp.bfloat16)
    grad_qkv = jnp.concatenate([grad_queries, grad_keys, grad_values], axis=1)
    grad_bias_q = jnp.sum(grad_queries.astype(jnp.float32), axis=0)
    grad_bias_v = jnp.sum(grad_values.astype(jnp.float32), axis=0)
    grad_w_qkv = jnp.einsum("td,te->de", normed, grad_qkv, preferred_element_type=jnp.float32)
    grad_normed = jnp.einsum(
        "te,de->td", grad_qkv, attn_back[2], preferred_element_type=jnp.float32
    )
    unused_first, first_pull = jax.vjp(
        layer_norm, inputs, attn_back[0].astype(jnp.float32), attn_back[1].astype(jnp.float32)
    )
    grad_in_norm, grad_gain_one, grad_shift_one = first_pull(grad_normed)
    grad_inputs = grad_middle + grad_in_norm
    attn_grads = (
        lax.psum_scatter(grad_gain_one, ("ctx", "fsdp"), scatter_dimension=0, tiled=True),
        lax.psum_scatter(grad_shift_one, ("ctx", "fsdp"), scatter_dimension=0, tiled=True),
        lax.psum_scatter(grad_w_qkv, ("ctx", "fsdp"), scatter_dimension=0, tiled=True),
        lax.psum_scatter(grad_bias_q, ("ctx", "fsdp"), scatter_dimension=0, tiled=True),
        lax.psum_scatter(grad_bias_v, ("ctx", "fsdp"), scatter_dimension=0, tiled=True),
        lax.psum_scatter(grad_w_out, ("ctx", "fsdp"), scatter_dimension=0, tiled=True),
        lax.psum_scatter(grad_b_out, ("ctx", "fsdp"), scatter_dimension=0, tiled=True),
    )
    return (
        outputs[None],
        grad_inputs[None],
        attn_grads[0],
        attn_grads[1],
        attn_grads[2],
        attn_grads[3],
        attn_grads[4],
        attn_grads[5],
        attn_grads[6],
        mlp_grads[0],
        mlp_grads[1],
        mlp_grads[2],
        mlp_grads[3],
        mlp_grads[4],
        mlp_grads[5],
    )


def solution(mesh):
    placed = (
        P("fsdp", "ctx", None),
        P("fsdp", None),
        P(("ctx", "fsdp")),
        P(("ctx", "fsdp")),
        P(("ctx", "fsdp"), None),
        P(("ctx", "fsdp")),
        P(("ctx", "fsdp")),
        P(("ctx", "fsdp"), None),
        P(("ctx", "fsdp")),
        P(("ctx", "fsdp")),
        P(("ctx", "fsdp")),
        P(("ctx", "fsdp"), None),
        P(("ctx", "fsdp")),
        P(("ctx", "fsdp"), None),
        P(("ctx", "fsdp")),
        P("fsdp", "ctx", None),
    )
    return jax.shard_map(
        on_device,
        mesh=mesh,
        in_specs=placed,
        out_specs=(
            P("fsdp", "ctx", None),
            P("fsdp", "ctx", None),
            P(("ctx", "fsdp")),
            P(("ctx", "fsdp")),
            P(("ctx", "fsdp"), None),
            P(("ctx", "fsdp")),
            P(("ctx", "fsdp")),
            P(("ctx", "fsdp"), None),
            P(("ctx", "fsdp")),
            P(("ctx", "fsdp")),
            P(("ctx", "fsdp")),
            P(("ctx", "fsdp"), None),
            P(("ctx", "fsdp")),
            P(("ctx", "fsdp"), None),
            P(("ctx", "fsdp")),
        ),
        check_vma=False,
    )
```

profile of v0, /device:TPU:0, one launch (start us, length us, event | category | flops | bytes accessed | tf_op | source)
XLA Modules:
  0.0 5170.2 jit_solution(13428341154890801328)
XLA Ops:
  14.8 44.5 all-reduce.18
  61.8 107.3 %all-gather.8.cloned.1.call-done = bf16[2048,6144]{1,0:T(8,128)(2,1)} async-done(((bf16[64,6144]{1,0:T(8,128)(2,1)}), bf16[2048,6144]{1,0:T(8,128)(2,1)}) %all-gather.8.cloned.1.call-update) | async-done | bytes 25165840 | tf_op jit(solution)/shard_map/all_gather | solution.py:94
  169.1 10.3 fusion.164
  183.7 67.7 %all-gather = bf16[32,1,256]{2,1,0:T(2,128)(2,1)S(1)} all-gather(bf16[1,1,256]{2,1,0:T(2,128)(2,1)S(1)} %reshape.921), channel_id=1, replica_groups=mesh['ctx'=16,'fsdp'=2] {'ctx','fsdp'}, dimensions={0}, use_global_device_ids=true | all-gather | bytes 16896 | tf_op jit(solution)/shard_map/all_gather | solution.py:175
  253.1 11.5 copy.95
  264.6 64.2 %all-gather.10.cloned.1.call-done = bf16[2048,2048]{1,0:T(8,128)(2,1)} async-done(((bf16[128,2048]{1,0:T(8,128)(2,1)}), bf16[2048,2048]{1,0:T(8,128)(2,1)}) %all-gather.10.cloned.1.call-update) | async-done | bytes 8388624 | tf_op jit(solution)/shard_map/all_gather | solution.py:112
  328.7 11.4 copy.94
  340.2 36.6 while.59
  377.3 54.1 %while.60 = (s32[]{:T(128)}, f32[128,32,64]{0,2,1:T(8,128)}, bf16[4,512,2048]{1,2,0:T(8,128)(2,1)}, s32[128]{0:T(128)S(1)}, s32[8]{0:T(128)S(1)}, /*index=5*/s32...) while((s32[]{:T(128)}, f32[128,32,64]{0,2,1:T(8,128)}, ...), condition=%wide.region_11.12_spmd.clone, body=%wide.region_9.11_spmd.clone.sunk | while | flops 550472256 | bytes 15894995 | solution.py:160
  384.0 6.5 fusion.264
  397.3 6.8 fusion.264
  410.8 6.8 fusion.264
  424.4 6.8 fusion.264
  432.7 4.9 fusion.171
  438.0 165.3 %all-gather.16.cloned.1.call-done = bf16[2048,8192]{1,0:T(8,128)(2,1)} async-done(((bf16[64,8192]{1,0:T(8,128)(2,1)}), bf16[2048,8192]{1,0:T(8,128)(2,1)}) %all-gather.16.cloned.1.call-update) | async-done | bytes 33554448 | tf_op jit(solution)/shard_map/all_gather | solution.py:174
  603.3 17.9 convolution_add_fusion
  621.2 177.4 %all-gather.18.cloned.1.call-done = bf16[8192,2048]{1,0:T(8,128)(2,1)} async-done(((bf16[256,2048]{1,0:T(8,128)(2,1)}), bf16[8192,2048]{1,0:T(8,128)(2,1)}) %all-gather.18.cloned.1.call-update) | async-done | bytes 33554448 | tf_op jit(solution)/shard_map/all_gather | solution.py:176
  798.6 26.9 convert_reduce_fusion.4
  825.5 19.6 multiply_reduce_fusion
  848.6 7.2 convolution_convert_fusion
  857.3 217.3 %while.58 = (s32[]{:T(128)}, f32[4,512,4096]{2,1,0:T(8,128)}, s32[128]{0:T(128)S(1)}, s32[8]{0:T(128)S(1)}, s32[4]{0:T(128)S(1)}, /*index=5*/bf16[2048,2048]{1,0...) while((s32[]{:T(128)}, f32[4,512,4096]{2,1,0:T(8,128)}, ...), condition=%wide.region_22.23_spmd.clone, body=%wide.region_20.22_spmd.clone.sunk | while | flops 1106741760 | bytes 133171896 | solution.py:316
  869.6 6.3 fusion.248
  875.9 9.7 broadcast_multiply_fusion.4
  885.6 5.4 fusion.251
  895.2 8.9 copy.134
  904.2 7.6 constant_dynamic-update-slice_fusion.2
  923.9 6.3 fusion.248
  930.2 9.7 broadcast_multiply_fusion.4
  939.9 5.4 fusion.251
  949.5 8.9 copy.134
  958.4 7.6 constant_dynamic-update-slice_fusion.2
  978.2 6.3 fusion.248
  984.5 9.7 broadcast_multiply_fusion.4
  994.2 5.4 fusion.251
  1003.8 8.9 copy.134
  1012.7 7.6 constant_dynamic-update-slice_fusion.2
  1032.5 6.3 fusion.248
  1038.7 9.7 broadcast_multiply_fusion.4
  1048.5 5.4 fusion.251
  1058.1 8.9 copy.134
  1067.0 7.6 constant_dynamic-update-slice_fusion.2
  1074.7 87.8 %while.61 = (s32[]{:T(128)}, f32[128,32,64]{0,2,1:T(8,128)}, bf16[4,512,2048]{1,2,0:T(8,128)(2,1)}, s32[128]{0:T(128)S(1)}, s32[8]{0:T(128)S(1)}, /*index=5*/s32...) while((s32[]{:T(128)}, f32[128,32,64]{0,2,1:T(8,128)}, ...), condition=%wide.region_19.20_spmd.clone, body=%wide.region_17.19_spmd.clone.sunk | while | flops 823102016 | bytes 35310048 | solution.py:275
  1076.7 4.4 constant_dynamic-slice_fusion.14
  1081.0 5.9 fusion.271
  1086.9 11.4 fusion.274
  1100.1 4.6 constant_dynamic-slice_fusion.14
  1104.7 5.8 fusion.271
  1110.4 11.8 fusion.274
  1127.8 4.8 fusion.271
  1132.7 9.7 fusion.274
  1148.0 4.6 fusion.271
  1152.6 9.9 fusion.274
  1165.1 238.5 %reduce-scatter.6.cloned.1.call-done = f32[128,4096]{1,0:T(8,128)} async-done(((f32[2048,4096]{1,0:T(8,128)}), f32[128,4096]{1,0:T(8,128)}) %reduce-scatter.6.cloned.1.call-update) | async-done | bytes 2097168 | tf_op jit(solution)/shard_map/reduce_scatter | solution.py:319
  1406.0 15.1 fusion.168
  1427.5 9.2 fusion.174
  1437.7 19.7 fusion.147
  1458.5 28.7 fusion.150
  1489.1 23.3 fusion.167
  1513.1 20.3 fusion.132
  1533.4 20.0 all-reduce.21.cloned.1.call-done
  1564.9 350.0 %reduce-scatter.10.cloned.1.call-done = f32[64,2048]{1,0:T(8,128)} async-done(((f32[2048,2048]{1,0:T(8,128)}), f32[64,2048]{1,0:T(8,128)}) %reduce-scatter.10.cloned.1.call-update) | async-done | bytes 524304 | tf_op jit(solution)/shard_map/reduce_scatter | solution.py:345
  1914.8 437.2 %reduce-scatter.8.cloned.1.call-done = f32[64,6144]{1,0:T(8,128)} async-done(((f32[2048,6144]{1,0:T(8,128)}), f32[64,6144]{1,0:T(8,128)}) %reduce-scatter.8.cloned.1.call-update) | async-done | bytes 1572880 | tf_op jit(solution)/shard_map/reduce_scatter | solution.py:342
  2352.0 1404.6 %reduce-scatter.14.cloned.1.call-done = f32[256,2048]{1,0:T(8,128)} async-done(((f32[8192,2048]{1,0:T(8,128)}), f32[256,2048]{1,0:T(8,128)}) %reduce-scatter.14.cloned.1.call-update) | async-done | bytes 2097168 | tf_op jit(solution)/shard_map/reduce_scatter | solution.py:223
  3756.6 1406.5 %reduce-scatter.12.cloned.1.call-done = f32[64,8192]{1,0:T(8,128)} async-done(((f32[2048,8192]{1,0:T(8,128)}), f32[64,8192]{1,0:T(8,128)}) %reduce-scatter.12.cloned.1.call-update) | async-done | bytes 2097168 | tf_op jit(solution)/shard_map/reduce_scatter | solution.py:221
  (369 shorter events, 182.8 us)
Async XLA Ops:
  7.2 161.9 %all-gather.8.cloned.1.call-start = ((), (), s32[]{:S(2)}) async-start(), calls=%async_computation.5 | async-start | bytes 25952256 | tf_op jit(solution)/shard_map/all_gather | solution.py:94
  7.9 245.2 %all-gather.12.cloned.1.call-start = ((), (), s32[]{:S(2)}) async-start(), calls=%async_computation.7 | async-start | bytes 8912896 | tf_op jit(solution)/shard_map/all_gather | solution.py:111
  59.2 120.2 %copy-start.23 = (f32[2048]{0:T(1024)}, f32[2048]{0:T(1024)S(1)}, u32[]{:S(2)}) copy-start(f32[2048]{0:T(1024)S(1)} %convert_element_type.227) | copy-start | bytes 24580
  59.2 120.2 %copy-start.17 = (f32[2048]{0:T(1024)}, f32[2048]{0:T(1024)S(1)}, u32[]{:S(2)}) copy-start(f32[2048]{0:T(1024)S(1)} %convert_element_type.226) | copy-start | bytes 24580
  60.4 119.0 %copy-start.29 = (f32[128]{0:T(128)}, f32[128]{0:T(128)S(1)}, u32[]{:S(2)}) copy-start(f32[128]{0:T(128)S(1)} %broadcast_multiply_fusion.2) | copy-start | bytes 1540
  61.8 117.6 %copy-start.36 = (f32[128]{0:T(128)}, f32[128]{0:T(128)S(1)}, u32[]{:S(2)}) copy-start(f32[128]{0:T(128)S(1)} %fusion.143) | copy-start | bytes 1540
  61.8 117.6 %copy-start.31 = (f32[128]{0:T(128)}, f32[128]{0:T(128)S(1)}, u32[]{:S(2)}) copy-start(f32[128]{0:T(128)S(1)} %fusion.159) | copy-start | bytes 1540
  179.4 4.0 copy-start.39
  179.4 4.2 copy-start.38
  180.3 148.4 %all-gather.10.cloned.1.call-start = ((), (), s32[]{:S(2)}) async-start(), calls=%async_computation.6 | async-start | bytes 8912896 | tf_op jit(solution)/shard_map/all_gather | solution.py:112
  181.6 251.1 %all-gather.14.cloned.1.call-start = ((), (), s32[]{:S(2)}) async-start(), calls=%async_computation.8 | async-start | bytes 8650752 | tf_op jit(solution)/shard_map/all_gather | solution.py:97
  182.2 421.1 %all-gather.16.cloned.1.call-start = ((), (), s32[]{:S(2)}) async-start(), calls=%async_computation.9 | async-start | bytes 34603008 | tf_op jit(solution)/shard_map/all_gather | solution.py:174
  182.8 615.9 %all-gather.18.cloned.1.call-start = ((), (), s32[]{:S(2)}) async-start(), calls=%async_computation.10 | async-start | bytes 34603008 | tf_op jit(solution)/shard_map/all_gather | solution.py:176
  183.3 1220.2 %reduce-scatter.6.cloned.1.call-start = ((), (), s32[]{:S(2)}) async-start(), calls=%async_computation.11 | async-start | bytes 35651584 | tf_op jit(solution)/shard_map/reduce_scatter | solution.py:319
  183.6 661.6 %copy-start.19 = (f32[2048]{0:T(1024)}, f32[2048]{0:T(1024)S(1)}, u32[]{:S(2)}) copy-start(f32[2048]{0:T(1024)S(1)} %convert_element_type.237) | copy-start | bytes 24580
  183.7 419.6 %copy-start.21 = (f32[2048]{0:T(1024)}, f32[2048]{0:T(1024)S(1)}, u32[]{:S(2)}) copy-start(f32[2048]{0:T(1024)S(1)} %convert_element_type.238) | copy-start | bytes 24580
  377.3 55.5 %copy-start.4 = (bf16[1,128,2048]{2,1,0:T(8,128)(2,1)S(1)}, bf16[1,128,2048]{2,1,0:T(8,128)(2,1)}, u32[]{:S(2)}) copy-start(bf16[1,128,2048]{2,1,0:T(8,128)(2,1)} %param.24) | copy-start | bytes 1572868
  432.7 5.0 copy-start.9
  437.7 407.5 %copy-start.2 = (f32[128,2048]{1,0:T(8,128)}, f32[128,2048]{1,0:T(8,128)S(1)}, u32[]{:S(2)}) copy-start(f32[128,2048]{1,0:T(8,128)S(1)} %get-tuple-element.1335) | copy-start | bytes 3145732
  437.7 407.5 %copy-start.25 = (f32[128]{0:T(128)}, f32[128]{0:T(128)S(1)}, u32[]{:S(2)}) copy-start(f32[128]{0:T(128)S(1)} %broadcast_multiply_fusion.1) | copy-start | bytes 1540
  438.0 407.2 %copy-start.27 = (f32[128]{0:T(128)}, f32[128]{0:T(128)S(1)}, u32[]{:S(2)}) copy-start(f32[128]{0:T(128)S(1)} %fusion.160) | copy-start | bytes 1540
  603.3 195.4 %copy-start.15 = (bf16[1,128,2048]{2,1,0:T(8,128)(2,1)S(1)}, bf16[1,128,2048]{2,1,0:T(8,128)(2,1)}, u32[]{:S(2)}) copy-start(bf16[1,128,2048]{2,1,0:T(8,128)(2,1)} %param.39) | copy-start | bytes 1572868
  846.8 8.9 copy-start.7
  846.8 8.9 copy-start.34
  847.8 0.8 copy-start.11
  848.6 8.5 copy-start.12
  869.6 6.3 copy-start.1
  885.6 5.4 copy-start
  923.9 6.3 copy-start.1
  939.9 5.4 copy-start
  978.2 6.3 copy-start.1
  994.2 5.4 copy-start
  1032.5 6.3 copy-start.1
  1048.5 5.4 copy-start
  1074.6 478.9 %all-reduce.21.cloned.1.call-start = ((), (), s32[]{:S(2)}) async-start(), calls=%async_computation.16 | async-start | bytes 196608
  1162.5 243.4 %copy-start.5 = (bf16[1,128,2048]{2,1,0:T(8,128)(2,1)S(1)}, bf16[1,128,2048]{2,1,0:T(8,128)(2,1)}, u32[]{:S(2)}) copy-start(bf16[1,128,2048]{2,1,0:T(8,128)(2,1)} %param.24) | copy-start | bytes 1572868
  1162.5 243.4 %copy-start.18 = (f32[2048]{0:T(1024)S(1)}, f32[2048]{0:T(1024)}, u32[]{:S(2)}) copy-start(f32[2048]{0:T(1024)} %copy-done.17) | copy-start | bytes 24580
  1162.5 243.4 %copy-start.30 = (f32[128]{0:T(128)S(1)}, f32[128]{0:T(128)}, u32[]{:S(2)}) copy-start(f32[128]{0:T(128)} %copy-done.29) | copy-start | bytes 1540
  1165.0 240.9 %copy-start.13 = (bf16[128,2048]{1,0:T(8,128)(2,1)}, bf16[128,2048]{1,0:T(8,128)(2,1)S(1)}, u32[]{:S(2)}) copy-start(bf16[128,2048]{1,0:T(8,128)(2,1)S(1)} %copy.102) | copy-start | bytes 1572868
  1405.9 15.1 copy-start.37
  1406.0 15.1 copy-start.32
  1406.0 17.5 copy-start.8
  1406.0 17.5 copy-start.35
  1421.1 6.4 copy-start.10
  1427.1 487.8 %reduce-scatter.10.cloned.1.call-start = ((), (), s32[]{:S(2)}) async-start(), calls=%async_computation.13 | async-start | bytes 17301504 | tf_op jit(solution)/shard_map/reduce_scatter | solution.py:345
  1436.7 1.0 copy-start.14
  1436.7 1.0 copy-start.24
  1436.7 915.3 %reduce-scatter.8.cloned.1.call-start = ((), (), s32[]{:S(2)}) async-start(), calls=%async_computation.12 | async-start | bytes 51904512 | tf_op jit(solution)/shard_map/reduce_scatter | solution.py:342
  1457.4 1.0 copy-start.16
  1457.5 2299.2 %reduce-scatter.14.cloned.1.call-start = ((), (), s32[]{:S(2)}) async-start(), calls=%async_computation.15 | async-start | bytes 69206016 | tf_op jit(solution)/shard_map/reduce_scatter | solution.py:223
  1487.2 1.2 copy-start.3
  1487.2 1.9 copy-start.6
  1487.2 1.9 copy-start.20
  1487.2 1.9 copy-start.22
  1487.2 1.9 copy-start.26
  1487.2 1.9 copy-start.28
  1487.3 3675.9 %reduce-scatter.12.cloned.1.call-start = ((), (), s32[]{:S(2)}) async-start(), calls=%async_computation.14 | async-start | bytes 69206016 | tf_op jit(solution)/shard_map/reduce_scatter | solution.py:221
  1512.4 0.7 copy-start.33
Sparse Core Ops, SparseCore 0:
  10.9 158.1 all-gather.7
  180.5 72.5 all-gather.11
  255.8 72.8 all-gather.9
  331.7 75.7 all-gather.13
  410.4 192.8 all-gather.15
  606.2 192.3 all-gather.17
  1074.7 328.7 reduce-scatter.5
  1427.2 126.2 all-reduce.20
  1556.3 358.4 reduce-scatter.9
  1921.7 430.2 reduce-scatter.7
  2354.9 1401.6 reduce-scatter.13
  3759.4 1403.6 reduce-scatter.11
where the time goes:
time: 5180 us; the launch traced here: 5170 us
  waiting for transfers between devices  4370 us (84%)
  matrix products  392 us (8%)
  local copies, waits for them, and re-layouts  210 us (4%)
  blocking collectives  112 us (2%)
  other arithmetic  54.6 us (1%)
    reduce_scatter x1, waiting for transfers between devices, on_device(): lax.psum_scatter(grad_w_up, ('ctx', 'fsdp'), scatter_dimension=0, tiled=T...  1410 us
    reduce_scatter x1, waiting for transfers between devices, on_device(): lax.psum_scatter(grad_w_down, ('ctx', 'fsdp'), scatter_dimension=0, tiled...  1400 us
    reduce_scatter x1, waiting for transfers between devices, on_device(): lax.psum_scatter(grad_w_qkv, ('ctx', 'fsdp'), scatter_dimension=0, tiled=...  437 us
    reduce_scatter x1, waiting for transfers between devices, on_device(): lax.psum_scatter(grad_w_out, ('ctx', 'fsdp'), scatter_dimension=0, tiled=...  350 us
    reduce_scatter x1, waiting for transfers between devices, on_device(): lax.psum_scatter(terms.reshape(tok_rows * lax.axis_size('ctx'), 2 * model...  238 us
    all_gather x1, waiting for transfers between devices, on_device(): lax.all_gather(w_down, ('ctx', 'fsdp'), axis=0, tiled=True)  177 us
    all_gather x1, waiting for transfers between devices, on_device(): lax.all_gather(w_up, ('ctx', 'fsdp'), axis=0, tiled=True)  165 us
    all_gather x1, waiting for transfers between devices, on_device(): lax.all_gather(w_qkv, ('ctx', 'fsdp'), axis=0, tiled=True)  107 us
  transfers between devices with their start and end apart: 12, of which 11 were waited for; matrix products, arithmetic and copies ran while one was open for 7% of the time, Pallas kernels for 0%

commit v1 on v0

v1 whole, which is shorter than its diff:
```python
import functools

import jax
import jax.numpy as jnp
from jax import lax
from jax.experimental import pallas as pl
from jax.experimental.pallas import tpu as pltpu
from jax.sharding import PartitionSpec as P

HEAD_DIM = 64
EPSILON = 1e-05
MASKED = -1e30
BOTH = ("ctx", "fsdp")
NT = (((1,), (1,)), ((), ()))
TN = (((0,), (0,)), ((), ()))
F32 = jnp.float32
BF16 = jnp.bfloat16


def gelu_exact(pre_activation):
    return jax.nn.gelu(pre_activation, approximate=False)


def norm_parts(values):
    centred = values - jnp.mean(values, axis=-1, keepdims=True)
    rate = lax.rsqrt(jnp.mean(centred * centred, axis=-1, keepdims=True) + EPSILON)
    return centred * rate, rate


def norm_back(unit, rate, gain, grad):
    scaled = grad * gain
    return rate * (
        scaled
        - jnp.mean(scaled, axis=-1, keepdims=True)
        - unit * jnp.mean(scaled * unit, axis=-1, keepdims=True)
    )


def block_parts(key_block, query_block, rows):
    key_at = key_block * rows + lax.broadcasted_iota(jnp.int32, (rows, rows), 0)
    query_at = query_block * rows + lax.broadcasted_iota(jnp.int32, (rows, rows), 1)
    return key_at, query_at


def head_mask(values, head):
    lanes = lax.broadcasted_iota(jnp.int32, values.shape, 1)
    return jnp.where(lanes // HEAD_DIM == head, values, jnp.zeros_like(values))


def scores_block(keys, query_head, slope, distance, allowed):
    raw = lax.dot_general(keys, query_head, NT, preferred_element_type=F32)
    return jnp.where(allowed, raw * HEAD_DIM ** (-0.5) - slope * distance, MASKED)


def attend_kernel(rows, heads, low_ref, slope_ref, start_ref, q_ref, k_ref, v_ref, out_ref, total_ref):
    block = pl.program_id(0)
    low = low_ref[block]
    starts = start_ref[...]
    queries = q_ref[...]
    query_heads = [head_mask(queries, head) for head in range(heads)]

    def parts(key_block):
        key_at, query_at = block_parts(key_block, block, rows)
        allowed = (key_at <= query_at) & (key_at >= starts)
        at = pl.ds(pl.multiple_of(key_block * rows, rows), rows)
        return (query_at - key_at).astype(F32), allowed, at

    def total_step(key_block, carried):
        distance, allowed, at = parts(key_block)
        keys = k_ref[at, :]
        following = []
        for head in range(heads):
            top, total = carried[head]
            scores = scores_block(keys, query_heads[head], slope_ref[head], distance, allowed)
            new_top = jnp.maximum(top, jnp.max(scores, axis=0, keepdims=True))
            total = total * jnp.exp(top - new_top) + jnp.sum(
                jnp.exp(scores - new_top), axis=0, keepdims=True
            )
            following.append((new_top, total))
        return following

    begin = [(jnp.full((1, rows), MASKED, F32), jnp.zeros((1, rows), F32))] * heads
    totals = lax.fori_loop(low, block + 1, total_step, begin)
    log_totals = [top + jnp.log(total) for top, total in totals]
    for head in range(heads):
        total_ref[head : head + 1, :] = log_totals[head]

    def output_step(key_block, accum):
        distance, allowed, at = parts(key_block)
        keys = k_ref[at, :]
        values = v_ref[at, :]
        for head in range(heads):
            scores = scores_block(keys, query_heads[head], slope_ref[head], distance, allowed)
            probs = jnp.exp(scores - log_totals[head]).astype(BF16)
            accum = accum + lax.dot_general(
                probs, head_mask(values, head), TN, preferred_element_type=F32
            )
        return accum

    out_ref[...] = lax.fori_loop(low, block + 1, output_step, jnp.zeros(out_ref.shape, F32))


def attend_back_kernel(
    rows, heads, low_ref, slope_ref, start_ref, total_ref, delta_ref, q_ref, g_ref, k_ref, v_ref,
    dq_ref, dk_ref, dv_ref, dk_sum, dv_sum,
):
    block = pl.program_id(0)
    low = low_ref[block]
    starts = start_ref[...]
    query_heads = [head_mask(q_ref[...], head) for head in range(heads)]
    grad_heads = [head_mask(g_ref[...], head) for head in range(heads)]
    log_totals = [total_ref[head : head + 1, :] for head in range(heads)]
    deltas = [delta_ref[head : head + 1, :] for head in range(heads)]

    @pl.when(block == 0)
    def clear():
        dk_sum[...] = jnp.zeros_like(dk_sum)
        dv_sum[...] = jnp.zeros_like(dv_sum)

    def step(key_block, accum):
        key_at, query_at = block_parts(key_block, block, rows)
        allowed = (key_at <= query_at) & (key_at >= starts)
        distance = (query_at - key_at).astype(F32)
        at = pl.ds(pl.multiple_of(key_block * rows, rows), rows)
        keys = k_ref[at, :]
        values = v_ref[at, :]
        dk_part = jnp.zeros(keys.shape, F32)
        dv_part = jnp.zeros(keys.shape, F32)
        for head in range(heads):
            scores = scores_block(keys, query_heads[head], slope_ref[head], distance, allowed)
            probs = jnp.exp(scores - log_totals[head])
            grad_probs = lax.dot_general(values, grad_heads[head], NT, preferred_element_type=F32)
            grad_scores = (probs * (grad_probs - deltas[head])).astype(BF16)
            dv_part = dv_part + jnp.dot(
                probs.astype(BF16), grad_heads[head], preferred_element_type=F32
            )
            dk_part = dk_part + jnp.dot(grad_scores, query_heads[head], preferred_element_type=F32)
            accum = accum + lax.dot_general(
                grad_scores, head_mask(keys, head), TN, preferred_element_type=F32
            )
        dk_sum[at, :] += dk_part
        dv_sum[at, :] += dv_part
        return accum

    grad = lax.fori_loop(low, block + 1, step, jnp.zeros(dq_ref.shape, F32))
    dq_ref[...] = (grad * HEAD_DIM ** (-0.5)).astype(BF16)

    @pl.when(block == pl.num_programs(0) - 1)
    def store():
        dk_ref[...] = (dk_sum[...] * HEAD_DIM ** (-0.5)).astype(BF16)
        dv_ref[...] = dv_sum[...].astype(BF16)


def attend(queries, keys, values, starts, low, slopes, rows):
    seq_len, width = queries.shape
    heads = width // HEAD_DIM
    whole = pl.BlockSpec((seq_len, width), lambda i: (0, 0))
    block = pl.BlockSpec((rows, width), lambda i: (i, 0))
    row = pl.BlockSpec((1, rows), lambda i: (0, i))
    stat = pl.BlockSpec((heads, rows), lambda i: (0, i))
    scalar = pl.BlockSpec(memory_space=pltpu.SMEM)
    return pl.pallas_call(
        functools.partial(attend_kernel, rows, heads),
        grid=(seq_len // rows,),
        in_specs=[scalar, scalar, row, block, whole, whole],
        out_specs=[block, stat],
        out_shape=[
            jax.ShapeDtypeStruct((seq_len, width), F32),
            jax.ShapeDtypeStruct((heads, seq_len), F32),
        ],
        name="attend",
    )(low, slopes, starts, queries, keys, values)


def attend_back(queries, keys, values, grads, starts, low, slopes, log_total, delta, rows):
    seq_len, width = queries.shape
    heads = width // HEAD_DIM
    whole = pl.BlockSpec((seq_len, width), lambda i: (0, 0))
    block = pl.BlockSpec((rows, width), lambda i: (i, 0))
    row = pl.BlockSpec((1, rows), lambda i: (0, i))
    stat = pl.BlockSpec((heads, rows), lambda i: (0, i))
    scalar = pl.BlockSpec(memory_space=pltpu.SMEM)
    return pl.pallas_call(
        functools.partial(attend_back_kernel, rows, heads),
        grid=(seq_len // rows,),
        in_specs=[scalar, scalar, row, stat, stat, block, block, whole, whole],
        out_specs=[block, whole, whole],
        out_shape=[jax.ShapeDtypeStruct((seq_len, width), BF16)] * 3,
        scratch_shapes=[pltpu.VMEM((seq_len, width), F32)] * 2,
        name="attend_back",
    )(low, slopes, starts, log_total, delta, queries, grads, keys, values)


def to_sequence(rows_in, count):
    halves = rows_in.reshape(count, 2, rows_in.shape[0] // (2 * count), -1)
    return jnp.concatenate([halves[:, 0], halves[::-1, 1]], axis=0).reshape(rows_in.shape)


def to_layout(rows_in, count):
    blocks = rows_in.reshape(2, count, rows_in.shape[0] // (2 * count), -1)
    return jnp.stack([blocks[0], blocks[1, ::-1]], axis=1).reshape(rows_in.shape)


def gather_rows(rows_in):
    return lax.all_gather(rows_in, "ctx", axis=0, tiled=True)


def sum_rows(partial):
    return lax.psum_scatter(partial.astype(BF16), "ctx", scatter_dimension=0, tiled=True).astype(F32)


def columns_of_rows(weight, parts):
    count = lax.axis_size("ctx")
    rows = weight.shape[0]
    split = weight.reshape(rows, parts, count, -1).transpose(2, 0, 1, 3)
    mine = lax.all_to_all(split, "ctx", split_axis=0, concat_axis=0)
    both = lax.all_gather(mine, "fsdp", axis=1)
    return both.reshape(count * both.shape[1] * rows, parts, -1)


def rows_of_columns(grad):
    count = lax.axis_size("ctx")
    pair = lax.axis_size("fsdp")
    rows = grad.shape[0] // (count * pair)
    pieces = grad.astype(BF16).reshape(count, pair, rows, *grad.shape[1:])
    summed = lax.psum_scatter(pieces, "fsdp", scatter_dimension=1, tiled=False)
    mine = lax.all_to_all(summed, "ctx", split_axis=0, concat_axis=0)
    return mine.transpose(1, 2, 0, 3).reshape(rows, -1).astype(F32)


def pair_sum(grad):
    return lax.psum_scatter(grad, "fsdp", scatter_dimension=0, tiled=True)


def rows_to_columns(local):
    count = lax.axis_size("ctx")
    rows = local.shape[0]
    split = local.reshape(rows, count, -1).transpose(1, 0, 2)
    mine = lax.all_to_all(split, "ctx", split_axis=0, concat_axis=0)
    return mine.reshape(count * rows, -1)


def columns_to_rows(slice_in):
    count = lax.axis_size("ctx")
    rows = slice_in.shape[0] // count
    mine = lax.all_to_all(slice_in.reshape(count, rows, -1), "ctx", split_axis=0, concat_axis=0)
    return mine.transpose(1, 0, 2).reshape(rows, -1)


def widen(columns, share):
    if share == 1:
        return columns
    count = lax.axis_size("ctx")
    groups = [list(range(first, first + share)) for first in range(0, count, share)]
    return lax.all_gather(
        columns, "ctx", axis=columns.ndim - 1, tiled=True, axis_index_groups=groups
    )


def narrow(columns, share):
    if share == 1:
        return columns
    width = columns.shape[-1] // share
    place = lax.rem(lax.axis_index("ctx"), share)
    return lax.dynamic_slice_in_dim(columns, place * width, width, columns.ndim - 1)


def on_device(
    tokens, doc_lengths, ln1_gain, ln1_bias, w_qkv, bias_q, bias_v, w_out, b_out,
    ln2_gain, ln2_bias, w_up, b_up, w_down, b_down, cotangent,
):
    count = lax.axis_size("ctx")
    rank = lax.axis_index("ctx")
    pair_rank = lax.axis_index("fsdp")
    tok_rows, width = tokens.shape[1:]
    seq_len = tok_rows * count
    own_cols = width // count
    share = max(1, HEAD_DIM // own_cols)
    head_count = width // HEAD_DIM
    heads = own_cols * share // HEAD_DIM
    rows = min(256, seq_len)

    lengths = doc_lengths[0]
    doc_starts = jnp.cumsum(lengths) - lengths
    positions = jnp.arange(seq_len, dtype=jnp.int32)
    starts = jnp.max(
        jnp.where(doc_starts[None, :] <= positions[:, None], doc_starts[None, :], 0), axis=1
    ).astype(jnp.int32)
    low = starts[::rows] // rows
    starts = starts[None, :]
    first_head = (rank // share) * heads
    head_ids = (first_head + jnp.arange(heads)).astype(F32)
    slopes = 2.0 ** (-8.0 * (head_ids + 1.0) / head_count)

    vectors = jnp.stack([ln1_gain, ln1_bias, b_out, ln2_gain, ln2_bias, b_down])
    vectors = lax.all_gather(vectors, BOTH, axis=1, tiled=True).astype(F32)
    gain_one, shift_one, b_out_all, gain_two, shift_two, b_down_all = vectors
    pair_vectors = lax.all_gather(jnp.stack([bias_q, bias_v]), "fsdp", axis=1, tiled=True)
    pair_vectors = widen(pair_vectors.astype(F32), share)
    b_up_own = lax.all_gather(b_up, "fsdp", axis=0, tiled=True).astype(F32)

    w_qkv_own = columns_of_rows(w_qkv, 3)
    w_qkv_head = widen(w_qkv_own, share).reshape(width, -1)
    w_qkv_own = w_qkv_own.reshape(width, -1)
    w_up_own = columns_of_rows(w_up, 1).reshape(width, -1)
    w_down_own = lax.all_gather(w_down, "fsdp", axis=0, tiled=True)
    w_out_all = lax.all_gather(w_out, BOTH, axis=0, tiled=True)

    inputs = tokens[0].astype(F32)
    unit_one, rate_one = norm_parts(inputs)
    normed = (unit_one * gain_one + shift_one).astype(BF16)
    normed_all = gather_rows(normed)
    grad_out = cotangent[0]
    grad_out_all = gather_rows(grad_out)

    projected = jnp.dot(normed_all, w_qkv_head, preferred_element_type=F32)
    head_width = heads * HEAD_DIM
    shift = jnp.concatenate([pair_vectors[0], jnp.zeros(head_width, F32), pair_vectors[1]])
    projected = to_sequence((projected + shift).astype(BF16), count)
    queries, keys, values = (
        projected[:, part * head_width : (part + 1) * head_width] for part in range(3)
    )
    attended_full, log_total = attend(queries, keys, values, starts, low, slopes, rows)
    attended_own = narrow(to_layout(attended_full.astype(BF16), count), share)
    attended = columns_to_rows(attended_own)
    middle = inputs + jnp.dot(attended, w_out_all, preferred_element_type=F32) + b_out_all

    unit_two, rate_two = norm_parts(middle)
    normed_two = (unit_two * gain_two + shift_two).astype(BF16)
    normed_two_all = gather_rows(normed_two)
    hidden = jnp.dot(normed_two_all, w_up_own, preferred_element_type=F32) + b_up_own
    activated, gelu_pull = jax.vjp(gelu_exact, hidden)
    activated = activated.astype(BF16)

    grad_activated = lax.dot_general(grad_out_all, w_down_own, NT, preferred_element_type=F32)
    grad_hidden = gelu_pull(grad_activated)[0].astype(BF16)
    grad_normed_two = sum_rows(
        lax.dot_general(grad_hidden, w_up_own, NT, preferred_element_type=F32)
    )
    branch = sum_rows(jnp.dot(activated, w_down_own, preferred_element_type=F32))
    outputs = (middle + branch + b_down_all).astype(BF16)

    grad_w_down = pair_sum(
        lax.dot_general(activated, grad_out_all, TN, preferred_element_type=F32).astype(BF16)
    ).astype(F32)
    grad_w_up = rows_of_columns(
        lax.dot_general(normed_two_all, grad_hidden, TN, preferred_element_type=F32)[:, None]
    )
    grad_b_up = pair_sum(jnp.sum(grad_hidden.astype(F32), axis=0))
    own = rank * own_cols
    grad_b_down = pair_sum(
        jnp.sum(lax.dynamic_slice_in_dim(grad_out_all, own, own_cols, 1).astype(F32), axis=0)
    )

    grad_middle = grad_out.astype(F32) + norm_back(unit_two, rate_two, gain_two, grad_normed_two)
    grad_branch = grad_middle.astype(BF16)
    grad_attended = lax.dot_general(
        grad_branch, w_out_all, NT, preferred_element_type=F32
    ).astype(BF16)
    grad_heads = to_sequence(widen(rows_to_columns(grad_attended), share), count)
    grad_branch_all = gather_rows(grad_branch)
    grad_w_out = pair_sum(
        lax.dot_general(attended_own, grad_branch_all, TN, preferred_element_type=F32).astype(BF16)
    ).astype(F32)
    grad_b_out = pair_sum(
        jnp.sum(lax.dynamic_slice_in_dim(grad_branch_all, own, own_cols, 1).astype(F32), axis=0)
    )

    delta = (grad_heads.astype(F32) * attended_full).reshape(seq_len, heads, HEAD_DIM)
    delta = jnp.sum(delta, axis=-1).T
    grad_parts = attend_back(
        queries, keys, values, grad_heads, starts, low, slopes, log_total, delta, rows
    )
    grad_qkv = jnp.concatenate(
        [narrow(to_layout(part, count), share) for part in grad_parts], axis=1
    )
    column_sums = jnp.sum(grad_qkv.astype(F32), axis=0)
    grad_bias_q = pair_sum(column_sums[:own_cols])
    grad_bias_v = pair_sum(column_sums[2 * own_cols :])
    grad_normed = sum_rows(lax.dot_general(grad_qkv, w_qkv_own, NT, preferred_element_type=F32))
    grad_w_qkv = rows_of_columns(
        lax.dot_general(normed_all, grad_qkv, TN, preferred_element_type=F32).reshape(
            width, 3, own_cols
        )
    )
    grad_inputs = grad_middle + norm_back(unit_one, rate_one, gain_one, grad_normed)

    norm_sums = jnp.stack(
        [
            jnp.sum(grad_normed * unit_one, axis=0),
            jnp.sum(grad_normed, axis=0),
            jnp.sum(grad_normed_two * unit_two, axis=0),
            jnp.sum(grad_normed_two, axis=0),
        ]
    )
    norm_sums = lax.psum_scatter(norm_sums, BOTH, scatter_dimension=1, tiled=True)
    return (
        outputs[None],
        grad_inputs[None],
        norm_sums[0],
        norm_sums[1],
        grad_w_qkv,
        grad_bias_q,
        grad_bias_v,
        grad_w_out,
        grad_b_out,
        norm_sums[2],
        norm_sums[3],
        grad_w_up,
        grad_b_up,
        grad_w_down,
        grad_b_down,
    )


def solution(mesh):
    spread = P(BOTH)
    matrix = P(BOTH, None)
    rows = P("fsdp", "ctx", None)
    placed = (
        rows, P("fsdp", None), spread, spread, matrix, spread, spread, matrix, spread,
        spread, spread, matrix, spread, matrix, spread, rows,
    )
    results = (
        rows, rows, spread, spread, matrix, spread, spread, matrix, spread,
        spread, spread, matrix, spread, matrix, spread,
    )
    return jax.shard_map(
        on_device, mesh=mesh, in_specs=placed, out_specs=results, check_vma=False
    )
```

time: 5180 us -> 1240 us (0.24)
  waiting for transfers between devices: 4370 us -> 842 us
  matrix products: 392 us -> 111 us
  local copies, waits for them, and re-layouts: 210 us -> 43 us
    reduce_scatter x5 -> x6, waiting for transfers between devices: 3840 us -> 320 us  [the longest x3 299 us: sum_rows(): lax.psum_scatter(partial.astype(BF16), 'ctx', scatter_dimension=0, tiled=...]
    dot_general x40 -> x12, matrix products: 392 us -> 111 us  [the longest x1 18.7 us: on_device(): jnp.dot(normed_two_all, w_up_own, preferred_element_type=F32) + b_up_own]
    all_gather x6 -> x8, waiting for transfers between devices: 514 us -> 373 us  [the longest x4 297 us: gather_rows(): return lax.all_gather(rows_in, 'ctx', axis=0, tiled=True)]
    unnamed x13 -> x18, waiting for transfers between devices: 22.4 us -> 133 us
    dynamic_slice x40 -> x0, local copies, waits for them, and re-layouts: 92.7 us -> none  [the longest x28 51 us: on_device(): lax.scan(total_step, initial, (key_stack, block_ids))]
    dynamic_update_slice x8 -> x0, local copies, waits for them, and re-layouts: 66.1 us -> none  [on_device(): lax.map(one_piece, jnp.arange(tok_rows * lax.axis_size('ctx') // piece_ro...]
  transfers between devices with their start and end apart: 12 -> 21, of which waited for: 11 -> 16; matrix products, arithmetic and copies ran while one was open for 7% -> 11% of each run, Pallas kernels for 0% -> 4%
where the time goes in v1:
time: 1240 us; the launch traced here: 1230 us
  waiting for transfers between devices  842 us (68%)
  blocking collectives  119 us (10%)
  matrix products  111 us (9%)
  Pallas kernels  46.7 us (4%)
  local copies, waits for them, and re-layouts  43 us (3%)
  starting transfers between devices  25.5 us (2%)
  other arithmetic  23.2 us (2%)
  between operations  16.4 us (1%)
    reduce_scatter x3, waiting for transfers between devices, sum_rows(): lax.psum_scatter(partial.astype(BF16), 'ctx', scatter_dimension=0, tiled=...  299 us
    all_gather x4, waiting for transfers between devices, gather_rows(): return lax.all_gather(rows_in, 'ctx', axis=0, tiled=True)  297 us
    unnamed x18, waiting for transfers between devices  133 us
    all_gather x1, blocking collectives, on_device(): vectors = lax.all_gather(vectors, BOTH, axis=1, tiled=True).astype(F32)  75.6 us
    all_gather x2, waiting for transfers between devices, columns_of_rows(): both = lax.all_gather(mine, 'fsdp', axis=1)  32.8 us
    all_to_all x1, blocking collectives, rows_of_columns(): mine = lax.all_to_all(summed, 'ctx', split_axis=0, concat_axis=0)  29.4 us
    all_gather x1, waiting for transfers between devices, on_device(): w_out_all = lax.all_gather(w_out, BOTH, axis=0, tiled=True)  29.2 us
    pallas_call x1, Pallas kernels, attend(): pl.pallas_call(functools.partial(attend_kernel, rows, heads), grid=(seq_l...  26.2 us
  transfers between devices with their start and end apart: 21, of which 16 were waited for; matrix products, arithmetic and copies ran while one was open for 11% of the time, Pallas kernels for 4%

profile of v1, /device:TPU:0, one launch (start us, length us, event | category | flops | bytes accessed | tf_op | source)
XLA Modules:
  0.0 1226.9 jit_solution(9355102518532302585)
XLA Ops:
  7.3 1.3 copy.163
  8.6 1.1 copy.130
  9.7 7.4 all-to-all-start
  17.2 75.6 %all-gather.3 = bf16[32,64,6]{1,2,0:T(8,128)(2,1)S(1)} all-gather(bf16[1,64,6]{1,2,0:T(8,128)(2,1)S(1)} %bitcast.288), channel_id=1, replica_groups=mesh['ctx'=16,'fsdp'=2] {'ctx','fsdp'}, dimensions={0}, use_global_device_ids=true | all-gather | bytes 25344 | tf_op jit(solution)/shard_map/all_gather | solution.py:296
  92.9 1.4 copy.131
  95.0 1.2 fusion.33
  97.3 1.5 copy.138
  98.9 3.7 all-to-all-start.2
  102.6 4.4 all-gather.4
  108.5 10.8 all-gather.25.cloned.1.call-done
  119.3 2.7 copy.132
  122.0 74.4 %all-gather.15.cloned.1.call-done = bf16[2048,2048]{1,0:T(8,128)(2,1)} async-done(((bf16[128,2048]{1,0:T(8,128)(2,1)}), bf16[2048,2048]{1,0:T(8,128)(2,1)}) %all-gather.15.cloned.1.call-update) | async-done | bytes 8388624 | tf_op jit(solution)/shard_map/all_gather | solution.py:205
  196.4 8.0 add_convert_fusion.1
  204.8 1.2 fusion.50
  206.0 26.2 %attend.1 = (f32[2048,128]{1,0:T(8,128)}, f32[2,2048]{1,0:T(2,128)}) custom-call(s32[8]{0:T(128)} %and_select_fusion.low_ref, f32[2]{0:T(128)} %multiply_power_fusion.slope_ref, s32[1,2048]{1,0:T(1,128)} %bitcast.277, bf16[2048,128]{1,0:T(8,128)(2,1)} %get-tuple-element.44.q_ref, bf16[2048,128]{1,0:T(8,128)(2,1)} %get-tuple-element.43.k_ref, ...), custom_call_target="tpu_custom_call" | custom-call | tf_op jit(solution)/shard_map/attend/pallas_call | solution.py:162
  232.2 1.3 convert_element_type.129
  234.4 3.6 all-to-all-start.1
  238.3 1.5 copy.139
  239.9 12.4 %all-to-all-done.1 = bf16[16,128,128]{2,1,0:T(8,128)(2,1)S(1)} async-done(((bf16[16,128,128]{2,1,0:T(8,128)(2,1)}), bf16[16,128,128]{2,1,0:T(8,128)(2,1)S(1)}, u32[]{:S(2)}, u32[]{:S(2)}) %all-to-all-start.1) | async-done | bytes 524320 | tf_op jit(solution)/shard_map/all_to_all | solution.py:246
  252.5 29.2 %all-gather.17.cloned.1.call-done = bf16[2048,2048]{1,0:T(8,128)(2,1)} async-done(((bf16[64,2048]{1,0:T(8,128)(2,1)}), bf16[2048,2048]{1,0:T(8,128)(2,1)}) %all-gather.17.cloned.1.call-update) | async-done | bytes 8388624 | tf_op jit(solution)/shard_map/all_gather | solution.py:307
  281.7 4.7 fusion.58
  289.2 4.2 all-gather.5
  293.5 22.0 %all-gather.27.cloned.1.call-done = bf16[16,128,1,512]{3,0,2,1:T(8,128)(2,1)} async-done(((bf16[16,64,1,512]{3,0,2,1:T(8,128)(2,1)}), bf16[16,128,1,512]{3,0,2,1:T(8,128)(2,1)}) %all-gather.27.cloned.1.call-update) | async-done | bytes 2097168 | tf_op jit(solution)/shard_map/all_gather | solution.py:217
  315.5 4.1 copy.140
  319.6 72.8 %all-gather.19.cloned.1.call-done = bf16[2048,2048]{1,0:T(8,128)(2,1)} async-done(((bf16[128,2048]{1,0:T(8,128)(2,1)}), bf16[2048,2048]{1,0:T(8,128)(2,1)}) %all-gather.19.cloned.1.call-update) | async-done | bytes 8388624 | tf_op jit(solution)/shard_map/all_gather | solution.py:205
  392.4 18.7 %multiply_convert_fusion = (bf16[2048,512]{1,0:T(8,128)(2,1)}, f32[2048,512]{1,0:T(8,128)}, f32[2048,512]{1,0:T(8,128)}) fusion(f32[512]{0:T(512)S(1)} %bitcast.290, bf16[2048,2048]{1,0:T(8,128)(2,1)} %all-gather.19.cloned.1.call-done, bf16[2048,512]{1,0:T(8,128)(2,1)} %bitcast.241), kind=kOutput, calls=%fused_computation.11 | convolution fusion | flops 4364173312 | bytes 20973568 | tf_op jit(solution)/shard_map/dot_general | solution.py:331
  411.0 14.4 %all-gather.21.cloned.1.call-done = bf16[512,2048]{1,0:T(8,128)(2,1)} async-done(((bf16[256,2048]{1,0:T(8,128)(2,1)}), bf16[512,2048]{1,0:T(8,128)(2,1)}) %all-gather.21.cloned.1.call-update) | async-done | bytes 2097168 | tf_op jit(solution)/shard_map/all_gather | solution.py:306
  425.5 76.5 %all-gather.29.cloned.1.call-done = bf16[1,2048,2048]{2,1,0:T(8,128)(2,1)} async-done(((bf16[1,128,2048]{2,1,0:T(8,128)(2,1)}), bf16[1,2048,2048]{2,1,0:T(8,128)(2,1)}) %all-gather.29.cloned.1.call-update) | async-done | bytes 8388624 | tf_op jit(solution)/shard_map/all_gather | solution.py:205
  502.0 12.8 %convert_reduce_fusion = (f32[512]{0:T(512)S(1)}, bf16[2048,512]{1,0:T(8,128)(2,1)S(1)}) fusion(f32[2048,512]{1,0:T(8,128)} %get-tuple-element.41, bf16[512,2048]{1,0:T(8,128)(2,1)} %all-gather.21.cloned.1.call-done, bf16[1,2048,2048]{2,1,0:T(8,128)(2,1)} %all-gather.29.cloned.1.call-done, f32[2048,512]{1,0:T(8,128)} %get-tuple-element.74, f32[512]{0:T(512)S(1)} %bitcast.291), kind=kOutput, calls=%fused_computation.9 | convolution fusion | flops 4312792576 | bytes 20975616 | tf_op jit(solution)/shard_map/dot_general | solution.py:335
  514.8 1.3 copy-done.28
  516.1 6.9 convolution_convert_fusion.1
  523.3 10.4 convolution_convert_fusion.2
  533.7 91.5 %reduce-scatter.15.cloned.1.call-done = bf16[128,2048]{1,0:T(8,128)(2,1)} async-done(((bf16[2048,2048]{1,0:T(8,128)(2,1)}), bf16[128,2048]{1,0:T(8,128)(2,1)}) %reduce-scatter.15.cloned.1.call-update) | async-done | bytes 524304 | tf_op jit(solution)/shard_map/reduce_scatter | solution.py:209
  625.2 1.5 fusion.44
  626.8 105.7 %reduce-scatter.13.cloned.1.call-done = bf16[128,2048]{1,0:T(8,128)(2,1)} async-done(((bf16[2048,2048]{1,0:T(8,128)(2,1)}), bf16[128,2048]{1,0:T(8,128)(2,1)}) %reduce-scatter.13.cloned.1.call-update) | async-done | bytes 524304 | tf_op jit(solution)/shard_map/reduce_scatter | solution.py:209
  732.4 3.0 fusion.47
  735.4 6.5 fusion.31
  742.9 4.3 all-to-all-start.3
  747.3 9.9 convolution_convert_fusion.3
  757.4 4.1 all-to-all-done.3
  762.8 20.5 %attend_back.1 = (bf16[2048,128]{1,0:T(8,128)(2,1)}, bf16[2048,128]{1,0:T(8,128)(2,1)}, bf16[2048,128]{1,0:T(8,128)(2,1)}) custom-call(s32[8]{0:T(128)} %and_select_fusion.low_ref, f32[2]{0:T(128)} %multiply_power_fusion.slope_ref, s32[1,2048]{1,0:T(1,128)} %bitcast.278, f32[2,2048]{1,0:T(2,128)} %get-tuple-element.21.total_ref, f32[2,2048]{1,0:T(2,128)} %bitcast.279, ...), custom_call_target="tpu_custom_call" | custom-call | tf_op jit(solution)/shard_map/attend_back/pallas_call | solution.py:183
  787.7 9.2 convolution_convert_fusion.4
  796.9 4.0 convert_element_type.146
  800.8 1.6 copy.147
  802.5 10.0 fusion.10
  812.9 8.1 convolution_convert_fusion
  822.3 2.0 dynamic-slice_bitcast_fusion
  824.2 29.4 %all_to_all.30 = bf16[16,64,1,512]{3,1,2,0:T(8,128)(2,1)S(1)} all-to-all(bf16[16,64,1,512]{3,1,2,0:T(8,128)(2,1)S(1)} %dynamic-slice_bitcast_fusion), channel_id=1, replica_groups=mesh['ctx'=16,'fsdp'=2] {'ctx'}, dimensions={0} | all-to-all | bytes 2097152 | tf_op jit(solution)/shard_map/all_to_all | solution.py:227
  853.7 5.0 all-to-all-start.4
  860.0 1.3 convert_reduce_fusion.5
  861.7 1.5 copy.167
  863.2 20.8 %reduce-scatter.23.cloned.1.call-done = bf16[256,2048]{1,0:T(8,128)(2,1)} async-done(((bf16[512,2048]{1,0:T(8,128)(2,1)}), bf16[256,2048]{1,0:T(8,128)(2,1)}) %reduce-scatter.23.cloned.1.call-update) | async-done | bytes 1048592 | tf_op jit(solution)/shard_map/reduce_scatter | solution.py:232
  884.1 2.8 convert_element_type.160
  888.4 1.6 copy.180
  890.0 101.6 %reduce-scatter.17.cloned.1.call-done = bf16[128,2048]{1,0:T(8,128)(2,1)} async-done(((bf16[2048,2048]{1,0:T(8,128)(2,1)}), bf16[128,2048]{1,0:T(8,128)(2,1)}) %reduce-scatter.17.cloned.1.call-update) | async-done | bytes 524304 | tf_op jit(solution)/shard_map/reduce_scatter | solution.py:209
  991.6 1.5 fusion.45
  993.2 1.4 copy.151
  994.7 72.9 %all-gather.23.cloned.1.call-done = bf16[2048,2048]{1,0:T(8,128)(2,1)} async-done(((bf16[128,2048]{1,0:T(8,128)(2,1)}), bf16[2048,2048]{1,0:T(8,128)(2,1)}) %all-gather.23.cloned.1.call-update) | async-done | bytes 8388624 | tf_op jit(solution)/shard_map/all_gather | solution.py:205
  1067.6 5.7 convolution_convert_fusion.5
  1073.4 1.4 fusion.37
  1074.8 130.0 %reduce-scatter.25.cloned.1.call-done = f32[64,4]{1,0:T(8,128)} async-done(((f32[2048,4]{1,0:T(8,128)}), f32[64,4]{1,0:T(8,128)}) %reduce-scatter.25.cloned.1.call-update) | async-done | bytes 1040
  1208.1 1.3 convert_reduce_fusion.6
  1209.4 5.1 all-reduce.6
  1218.2 1.8 convert_element_type.152
  (165 shorter events, 25.6 us)
Async XLA Ops:
  7.2 9.9 copy-start.17
  7.2 9.9 copy-start.18
  7.2 9.9 copy-start.19
  7.2 9.9 copy-start.20
  7.2 9.9 copy-start.21
  7.2 9.9 copy-start.22
  7.2 87.1 %copy-start = (bf16[1,128,2048]{2,1,0:T(8,128)(2,1)S(1)}, bf16[1,128,2048]{2,1,0:T(8,128)(2,1)}, u32[]{:S(2)}) copy-start(bf16[1,128,2048]{2,1,0:T(8,128)(2,1)} %param.16) | copy-start | bytes 1572868
  8.6 88.4 %copy-start.15 = (bf16[64,8192]{1,0:T(8,128)(2,1)S(1)}, bf16[64,8192]{1,0:T(8,128)(2,1)}, u32[]{:S(2)}) copy-start(bf16[64,8192]{1,0:T(8,128)(2,1)} %param.27) | copy-start | bytes 3145732
  9.7 83.2 %all-to-all-start = ((bf16[16,64,3,128]{3,1,2,0:T(8,128)(2,1)}), bf16[16,64,3,128]{3,1,2,0:T(8,128)(2,1)S(1)}, u32[]{:S(2)}, u32[]{:S(2)}) async-start(bf16[16,64,3,128]{3,1,2,0:T(8,128)(2,1)} %copy.130), calls=%async_computation | async-start | bytes 1572864 | tf_op jit(solution)/shard_map/all_to_all | solution.py:216
  17.1 102.2 %all-gather.25.cloned.1.call-start = ((), (), s32[]{:S(2)}) async-start(), calls=%async_computation.24 | async-start | bytes 2359296 | tf_op jit(solution)/shard_map/all_gather | solution.py:217
  94.3 102.1 %all-gather.15.cloned.1.call-start = ((), (), s32[]{:S(2)}) async-start(), calls=%async_computation.13 | async-start | bytes 8912896 | tf_op jit(solution)/shard_map/all_gather | solution.py:205
  94.9 7.6 copy-start.23
  94.9 7.6 copy-start.24
  94.9 12.1 copy-start.25
  96.2 185.6 %all-gather.17.cloned.1.call-start = ((), (), s32[]{:S(2)}) async-start(), calls=%async_computation.14 | async-start | bytes 8650752 | tf_op jit(solution)/shard_map/all_gather | solution.py:307
  98.9 135.6 %all-to-all-start.2 = ((bf16[16,64,1,512]{3,1,2,0:T(8,128)(2,1)}), bf16[16,64,1,512]{3,1,2,0:T(8,128)(2,1)S(1)}, u32[]{:S(2)}, u32[]{:S(2)}) async-start(bf16[16,64,1,512]{3,1,2,0:T(8,128)(2,1)} %copy.138), calls=%async_computation.2 | async-start | bytes 2097152 | tf_op jit(solution)/shard_map/all_to_all | solution.py:216
  107.3 97.0 %copy-start.16 = (s32[2048]{0:T(1024)}, s32[2048]{0:T(1024)S(1)}, u32[]{:S(2)}) copy-start(s32[2048]{0:T(1024)S(1)} %select_reduce_fusion) | copy-start | bytes 24580
  122.0 82.3 %copy-start.14 = (bf16[16,128,3,128]{1,0,3,2:T(8,128)(2,1)}, bf16[16,128,3,128]{1,0,3,2:T(8,128)(2,1)S(1)}, u32[]{:S(2)}) copy-start(bf16[16,128,3,128]{1,0,3,2:T(8,128)(2,1)S(1)} %copy.132) | copy-start | bytes 4718596
  234.4 17.8 %all-to-all-start.1 = ((bf16[16,128,128]{2,1,0:T(8,128)(2,1)}), bf16[16,128,128]{2,1,0:T(8,128)(2,1)S(1)}, u32[]{:S(2)}, u32[]{:S(2)}) async-start(bf16[16,128,128]{2,1,0:T(8,128)(2,1)} %bitcast.30), calls=%async_computation.1 | async-start | bytes 1048576 | tf_op jit(solution)/shard_map/all_to_all | solution.py:246
  238.0 77.5 %all-gather.27.cloned.1.call-start = ((), (), s32[]{:S(2)}) async-start(), calls=%async_computation.25 | async-start | bytes 3145728 | tf_op jit(solution)/shard_map/all_gather | solution.py:217
  239.8 152.5 %all-gather.19.cloned.1.call-start = ((), (), s32[]{:S(2)}) async-start(), calls=%async_computation.15 | async-start | bytes 8912896 | tf_op jit(solution)/shard_map/all_gather | solution.py:205
  286.5 2.7 copy-start.26
  287.8 137.6 %all-gather.21.cloned.1.call-start = ((), (), s32[]{:S(2)}) async-start(), calls=%async_computation.16 | async-start | bytes 3145728 | tf_op jit(solution)/shard_map/all_gather | solution.py:306
  288.4 213.5 %all-gather.29.cloned.1.call-start = ((), (), s32[]{:S(2)}) async-start(), calls=%async_computation.26 | async-start | bytes 8912896 | tf_op jit(solution)/shard_map/all_gather | solution.py:205
  289.2 336.1 %reduce-scatter.15.cloned.1.call-start = ((), (), s32[]{:S(2)}) async-start(), calls=%async_computation.18 | async-start | bytes 8912896 | tf_op jit(solution)/shard_map/reduce_scatter | solution.py:209
  502.0 14.1 %copy-start.6 = (bf16[16,128,1,512]{3,1,0,2:T(8,128)(2,1)S(1)}, bf16[16,128,1,512]{3,1,0,2:T(8,128)(2,1)}, u32[]{:S(2)}) copy-start(bf16[16,128,1,512]{3,1,0,2:T(8,128)(2,1)} %copy.140) | copy-start | bytes 6291460
  514.8 1.3 copy-start.28
  523.0 209.4 %reduce-scatter.13.cloned.1.call-start = ((), (), s32[]{:S(2)}) async-start(), calls=%async_computation.17 | async-start | bytes 8912896 | tf_op jit(solution)/shard_map/reduce_scatter | solution.py:209
  533.7 198.8 %copy-start.5 = (bf16[1,128,2048]{2,1,0:T(8,128)(2,1)S(1)}, bf16[1,128,2048]{2,1,0:T(8,128)(2,1)}, u32[]{:S(2)}) copy-start(bf16[1,128,2048]{2,1,0:T(8,128)(2,1)} %param.31) | copy-start | bytes 1572868
  735.4 6.5 copy-start.1
  742.9 18.6 %all-to-all-start.3 = ((bf16[16,128,128]{2,1,0:T(8,128)(2,1)}), bf16[16,128,128]{2,1,0:T(8,128)(2,1)S(1)}, u32[]{:S(2)}, u32[]{:S(2)}) async-start(bf16[16,128,128]{2,1,0:T(8,128)(2,1)} %bitcast.231), calls=%async_computation.5 | async-start | bytes 1048576 | tf_op jit(solution)/shard_map/all_to_all | solution.py:239
  747.2 75.1 %all-reduce.9.cloned.1.call-start = ((), (), s32[]{:S(2)}) async-start(), calls=%async_computation.28 | async-start | bytes 4194304
  757.1 4.5 copy-start.3
  757.1 96.5 %reduce-scatter.19.cloned.1.call-start = ((), (), s32[]{:S(2)}) async-start(), calls=%async_computation.20 | async-start | bytes 2359296 | tf_op jit(solution)/shard_map/reduce_scatter | solution.py:226
  761.6 1.2 copy-start.2
  786.7 0.8 copy-start.7
  786.8 0.9 copy-start.10
  802.5 10.4 copy-start.8
  802.5 10.4 copy-start.11
  802.5 81.6 %reduce-scatter.23.cloned.1.call-start = ((), (), s32[]{:S(2)}) async-start(), calls=%async_computation.23 | async-start | bytes 3145728 | tf_op jit(solution)/shard_map/reduce_scatter | solution.py:232
  812.6 179.0 %reduce-scatter.17.cloned.1.call-start = ((), (), s32[]{:S(2)}) async-start(), calls=%async_computation.19 | async-start | bytes 8912896 | tf_op jit(solution)/shard_map/reduce_scatter | solution.py:209
  821.0 0.7 copy-start.27
  821.1 246.5 %all-gather.23.cloned.1.call-start = ((), (), s32[]{:S(2)}) async-start(), calls=%async_computation.21 | async-start | bytes 8912896 | tf_op jit(solution)/shard_map/all_gather | solution.py:205
  853.7 33.6 %all-to-all-start.4 = ((bf16[16,64,3,128]{3,1,2,0:T(8,128)(2,1)}), bf16[16,64,3,128]{3,1,2,0:T(8,128)(2,1)S(1)}, u32[]{:S(2)}, u32[]{:S(2)}) async-start(bf16[16,64,3,128]{3,1,2,0:T(8,128)(2,1)} %bitcast.268), calls=%async_computation.8 | async-start | bytes 1572864 | tf_op jit(solution)/shard_map/all_to_all | solution.py:227
  858.7 346.1 %reduce-scatter.25.cloned.1.call-start = ((), (), s32[]{:S(2)}) async-start(), calls=%async_computation.27 | async-start | bytes 1081344
  861.7 25.2 %copy-start.9 = (bf16[16,2,64,128]{3,2,1,0:T(8,128)(2,1)S(1)}, bf16[16,2,64,128]{3,2,1,0:T(8,128)(2,1)}, u32[]{:S(2)}) copy-start(bf16[16,2,64,128]{3,2,1,0:T(8,128)(2,1)} %copy-done.7) | copy-start | bytes 1572868
  861.7 25.2 %copy-start.12 = (bf16[16,2,64,128]{3,2,1,0:T(8,128)(2,1)S(1)}, bf16[16,2,64,128]{3,2,1,0:T(8,128)(2,1)}, u32[]{:S(2)}) copy-start(bf16[16,2,64,128]{3,2,1,0:T(8,128)(2,1)} %copy-done.10) | copy-start | bytes 1572868
  994.6 223.5 %reduce-scatter.21.cloned.1.call-start = ((), (), s32[]{:S(2)}) async-start(), calls=%async_computation.22 | async-start | bytes 786432 | tf_op jit(solution)/shard_map/reduce_scatter | solution.py:232
  1067.6 5.8 copy-start.4
  1067.6 5.8 copy-start.13
Sparse Core Ops, SparseCore 0:
  94.4 24.8 all-gather.24
  122.0 74.2 all-gather.14
  199.5 82.2 all-gather.16
  283.7 31.7 all-gather.26
  318.1 74.2 all-gather.18
  393.8 31.6 all-gather.20
  427.6 74.2 all-gather.28
  523.2 102.0 reduce-scatter.14
  629.3 103.0 reduce-scatter.12
  757.3 64.2 all-reduce.8
  823.8 26.1 reduce-scatter.18
  852.1 31.8 reduce-scatter.22
  888.1 103.4 reduce-scatter.16
  993.6 73.9 all-gather.22
  1069.6 135.0 reduce-scatter.24
  1207.4 10.6 reduce-scatter.20

commit v2 on v1

--- a/solution.py
+++ b/solution.py
@@ -201,12 +201,419 @@
     return jnp.stack([blocks[0], blocks[1, ::-1]], axis=1).reshape(rows_in.shape)
 
 
-def gather_rows(rows_in):
+def gather_beside(rows_in):
     return lax.all_gather(rows_in, "ctx", axis=0, tiled=True)
 
 
-def sum_rows(partial):
+def sum_beside(partial):
     return lax.psum_scatter(partial.astype(BF16), "ctx", scatter_dimension=0, tiled=True).astype(F32)
+
+
+def from_pair(mine):
+    return lax.ppermute(mine, "fsdp", [(0, 1), (1, 0)])
+
+
+def pair_gather(mine, axis):
+    other = from_pair(mine)
+    first = lax.axis_index("fsdp") == 0
+    return jnp.where(
+        first, jnp.stack([mine, other], axis=axis), jnp.stack([other, mine], axis=axis)
+    )
+
+
+def pair_reduce(grad, axis):
+    here = lax.axis_index("fsdp")
+    given = lax.dynamic_index_in_dim(grad, 1 - here, axis, keepdims=False).astype(BF16)
+    kept = lax.dynamic_index_in_dim(grad, here, axis, keepdims=False)
+    return kept.astype(F32) + from_pair(given).astype(F32)
+
+
+def exchange(blocks):
+    total, width = blocks.shape
+    tiles = -(-width // 1024) * 8
+    padded = jnp.pad(blocks, ((0, 0), (0, tiles * 128 - width))).reshape(total, tiles, 128)
+    got = lax.all_to_all(padded, BOTH, split_axis=0, concat_axis=0)
+    return got.reshape(total, tiles * 128)[:, :width]
+
+
+MESH_ID = pl.DeviceIdType.MESH
+
+def remote(source, target, send_sem, recv_sem, device):
+    return pltpu.make_async_remote_copy(
+        src_ref=source, dst_ref=target, send_sem=send_sem, recv_sem=recv_sem,
+        device_id=device, device_id_type=MESH_ID,
+    )
+
+
+def place_of(line, side, core):
+    return (line * 2 + side) * 2 + core
+
+
+def own_place():
+    me = lax.axis_index("ctx")
+    return me, me // 4, (me // 2) % 2, me % 2
+
+
+def greet(lines):
+    me, line, side, core = own_place()
+    barrier = pltpu.get_barrier_semaphore()
+
+    def signal(target):
+        pl.semaphore_signal(barrier, inc=1, device_id={"ctx": target}, device_id_type=MESH_ID)
+
+    signal(place_of(line, side, 1 - core))
+    signal(place_of(line, 1 - side, core))
+
+    @pl.when(line > 0)
+    def below():
+        signal(me - 4)
+
+    @pl.when(line < lines - 1)
+    def above():
+        signal(me + 4)
+
+    pl.semaphore_wait(
+        barrier, 2 + jnp.where(line > 0, 1, 0) + jnp.where(line < lines - 1, 1, 0)
+    )
+
+
+def gather_kernel(
+    count, pieces, own_ref, out_ref, keep_sem, up_sem, down_sem, across_sem, chip_sem, recv_sem
+):
+    lines = count // 4
+    me, line, side, core = own_place()
+    partner = place_of(line, side, 1 - core)
+    across = place_of(line, 1 - side, core)
+    rows = own_ref.shape[0] // pieces
+
+    def part(block, k):
+        return out_ref.at[block, pl.ds(pl.multiple_of(k * rows, rows), rows), :]
+
+    def mine(k):
+        return own_ref.at[pl.ds(pl.multiple_of(k * rows, rows), rows), :]
+
+    def to_up(source, block, slot, k):
+        return remote(source, part(block, k), up_sem.at[slot, k], recv_sem.at[block, k], {"ctx": me + 4})
+
+    def to_down(source, block, slot, k):
+        return remote(source, part(block, k), down_sem.at[slot, k], recv_sem.at[block, k], {"ctx": me - 4})
+
+    def to_across(source, block, k):
+        return remote(
+            source, part(block, k), across_sem.at[block // 4, k], recv_sem.at[block, k], {"ctx": across}
+        )
+
+    def to_partner(source, block, k):
+        return remote(
+            source, part(block, k), chip_sem.at[block // 2, k], recv_sem.at[block, k], {"ctx": partner}
+        )
+
+    def arrived(block, k):
+        to_partner(part(block, k), block, k).wait_recv()
+
+    def each_piece(body):
+        def step(k, carried):
+            body(k)
+            return carried
+
+        lax.fori_loop(0, pieces, step, 0)
+
+    greet(lines)
+    keep = pltpu.make_async_copy(own_ref, out_ref.at[me], keep_sem)
+    keep.start()
+
+    def first(k):
+        @pl.when(line < lines - 1)
+        def up():
+            to_up(mine(k), me, 0, k).start()
+
+        @pl.when(line > 0)
+        def down():
+            to_down(mine(k), me, 0, k).start()
+
+        to_across(mine(k), me, k).start()
+        to_partner(mine(k), me, k).start()
+
+    each_piece(first)
+    for hops in range(1, lines):
+        def relay(k, hops=hops):
+            @pl.when(line >= hops)
+            def from_below():
+                block = me - 4 * hops
+                arrived(block, k)
+                if hops < lines - 1:
+                    @pl.when(line < lines - 1)
+                    def up():
+                        to_up(part(block, k), block, hops, k).start()
+
+                to_across(part(block, k), block, k).start()
+                to_partner(part(block, k), block, k).start()
+
+            @pl.when(line < lines - hops)
+            def from_above():
+                block = me + 4 * hops
+                arrived(block, k)
+                if hops < lines - 1:
+                    @pl.when(line > 0)
+                    def down():
+                        to_down(part(block, k), block, hops, k).start()
+
+                to_across(part(block, k), block, k).start()
+                to_partner(part(block, k), block, k).start()
+
+        each_piece(relay)
+
+    def hand_over(block):
+        def one(k):
+            arrived(block, k)
+            to_partner(part(block, k), block, k).start()
+
+        each_piece(one)
+
+    hand_over(across)
+    for hops in range(1, lines):
+        @pl.when(line >= hops)
+        def from_below(hops=hops):
+            hand_over(across - 4 * hops)
+
+        @pl.when(line < lines - hops)
+        def from_above(hops=hops):
+            hand_over(across + 4 * hops)
+
+    def settle(index, carried):
+        def one(k):
+            arrived(index * 2 + 1 - core, k)
+            to_partner(part(me, k), index * 2 + core, k).wait_send()
+
+        each_piece(one)
+        return carried
+
+    lax.fori_loop(0, count // 2, settle, 0)
+
+    def settle_across(index, carried):
+        each_piece(lambda k: to_across(part(me, k), index * 4, k).wait_send())
+        return carried
+
+    lax.fori_loop(0, lines, settle_across, 0)
+    for hops in range(lines - 1):
+        @pl.when((line >= hops) & (line < lines - 1))
+        def up(hops=hops):
+            each_piece(lambda k: to_up(part(me, k), me, hops, k).wait_send())
+
+        @pl.when((line < lines - hops) & (line > 0))
+        def down(hops=hops):
+            each_piece(lambda k: to_down(part(me, k), me, hops, k).wait_send())
+
+    keep.wait()
+
+
+def gather_rows(own, pieces=2):
+    count = lax.axis_size("ctx")
+    lines = count // 4
+    rows, width = own.shape
+    gathered = pl.pallas_call(
+        functools.partial(gather_kernel, count, pieces),
+        out_shape=jax.ShapeDtypeStruct((count, rows, width), own.dtype),
+        in_specs=[pl.BlockSpec(memory_space=pltpu.VMEM)],
+        out_specs=pl.BlockSpec(memory_space=pl.ANY),
+        scratch_shapes=[
+            pltpu.SemaphoreType.DMA,
+            pltpu.SemaphoreType.DMA((lines, pieces)),
+            pltpu.SemaphoreType.DMA((lines, pieces)),
+            pltpu.SemaphoreType.DMA((lines, pieces)),
+            pltpu.SemaphoreType.DMA((count // 2, pieces)),
+            pltpu.SemaphoreType.DMA((count, pieces)),
+        ],
+        compiler_params=pltpu.CompilerParams(collective_id=0, has_side_effects=True),
+        cost_estimate=pl.CostEstimate(flops=0, bytes_accessed=count * rows * width * 16, transcendentals=0),
+        name="gather_rows",
+    )(own)
+    return gathered.reshape(count * rows, width)
+
+
+def sum_kernel(
+    count, pieces, part_ref, out_ref, held, chip_in, across_in, line_in, load_sem,
+    chip_send, chip_recv, across_send, across_recv, line_send, line_recv,
+):
+    lines = count // 4
+    me, line, side, core = own_place()
+    partner = place_of(line, side, 1 - core)
+    across = place_of(line, 1 - side, core)
+    rows = out_ref.shape[0] // pieces
+
+    def at(ref, block, k):
+        return ref.at[block, pl.ds(pl.multiple_of(k * rows, rows), rows), :]
+
+    def to_partner(pair, k):
+        return remote(
+            at(part_ref, pair * 2 + 1 - core, k), at(chip_in, pair, k),
+            chip_send.at[pair, k], chip_recv.at[pair, k], {"ctx": partner},
+        )
+
+    def to_across(goal, k):
+        return remote(
+            at(held, goal * 2 + 1 - side, k), at(across_in, goal, k),
+            across_send.at[goal, k], across_recv.at[goal, k], {"ctx": across},
+        )
+
+    def to_next(goal, target, slot, k):
+        return remote(
+            at(held, goal * 2 + side, k), at(line_in, slot, k),
+            line_send.at[goal, k], line_recv.at[slot, k], {"ctx": target},
+        )
+
+    def each_piece(body):
+        def step(k, carried):
+            body(k)
+            return carried
+
+        lax.fori_loop(0, pieces, step, 0)
+
+    def far_first(visit):
+        for hops in range(lines - 1, 0, -1):
+            @pl.when(line + hops < lines)
+            def ahead(hops=hops):
+                visit(line + hops, 1)
+
+            @pl.when(line >= hops)
+            def behind(hops=hops):
+                visit(line - hops, -1)
+
+    loads = [
+        pltpu.make_async_copy(part_ref.at[pair * 2 + core], held.at[pair], load_sem.at[pair])
+        for pair in range(count // 2)
+    ]
+    for load in loads:
+        load.start()
+    greet(lines)
+
+    def give(goal, way):
+        each_piece(lambda k: to_partner(goal * 2 + 1 - side, k).start())
+
+    def give_same(goal, way):
+        each_piece(lambda k: to_partner(goal * 2 + side, k).start())
+
+    far_first(give)
+    give(line, 0)
+    far_first(give_same)
+    give_same(line, 0)
+    for load in loads:
+        load.wait()
+
+    def read(ref, block, k):
+        return ref[block, pl.ds(pl.multiple_of(k * rows, rows), rows), :].astype(F32)
+
+    def write(block, k, value):
+        held[block, pl.ds(pl.multiple_of(k * rows, rows), rows), :] = value.astype(held.dtype)
+
+    def cross(goal, way):
+        pair = goal * 2 + 1 - side
+
+        def one(k):
+            to_partner(pair, k).wait_recv()
+            write(pair, k, read(held, pair, k) + read(chip_in, pair, k))
+            to_across(goal, k).start()
+
+        each_piece(one)
+
+    far_first(cross)
+    cross(line, 0)
+
+    def two_sums(goal, k):
+        pair = goal * 2 + side
+        to_partner(pair, k).wait_recv()
+        to_across(goal, k).wait_recv()
+        return read(held, pair, k) + read(chip_in, pair, k) + read(across_in, goal, k)
+
+    def along(goal, way):
+        pair = goal * 2 + side
+        target = me + 4 * way
+        arriving = goal
+        if way == 1:
+            slot = goal
+            fed = line > 0
+        else:
+            fed = line < lines - 1
+            slot = jnp.where(goal == line - 1, lines, goal)
+
+        def one(k):
+            total = two_sums(goal, k)
+            write(pair, k, total)
+
+            @pl.when(fed)
+            def add():
+                to_next(goal, target, arriving, k).wait_recv()
+                write(pair, k, total + read(line_in, arriving, k))
+
+            to_next(goal, target, slot, k).start()
+
+        each_piece(one)
+
+    far_first(along)
+
+    def last(k):
+        span = pl.ds(pl.multiple_of(k * rows, rows), rows)
+        out_ref[span, :] = two_sums(line, k)
+
+        @pl.when(line > 0)
+        def from_below():
+            to_next(line, me, line, k).wait_recv()
+            out_ref[span, :] += read(line_in, line, k)
+
+        @pl.when(line < lines - 1)
+        def from_above():
+            to_next(line, me, lines, k).wait_recv()
+            out_ref[span, :] += read(line_in, lines, k)
+
+    each_piece(last)
+
+    def settle(index, carried):
+        each_piece(lambda k: to_partner(index, k).wait_send())
+        return carried
+
+    lax.fori_loop(0, count // 2, settle, 0)
+
+    def settle_line(goal, carried):
+        each_piece(lambda k: to_across(goal, k).wait_send())
+
+        @pl.when(goal != line)
+        def sent():
+            each_piece(lambda k: to_next(goal, me, goal, k).wait_send())
+
+        return carried
+
+    lax.fori_loop(0, lines, settle_line, 0)
+
+
+def sum_rows(partial, pieces=2):
+    count = lax.axis_size("ctx")
+    lines = count // 4
+    width = partial.shape[1]
+    rows = partial.shape[0] // count
+    return pl.pallas_call(
+        functools.partial(sum_kernel, count, pieces),
+        out_shape=jax.ShapeDtypeStruct((rows, width), F32),
+        in_specs=[pl.BlockSpec(memory_space=pl.ANY)],
+        out_specs=pl.BlockSpec(memory_space=pltpu.VMEM),
+        scratch_shapes=[
+            pltpu.VMEM((count // 2, rows, width), BF16),
+            pltpu.VMEM((count // 2, rows, width), BF16),
+            pltpu.VMEM((lines, rows, width), BF16),
+            pltpu.VMEM((lines + 1, rows, width), BF16),
+            pltpu.SemaphoreType.DMA((count // 2,)),
+            pltpu.SemaphoreType.DMA((count // 2, pieces)),
+            pltpu.SemaphoreType.DMA((count // 2, pieces)),
+            pltpu.SemaphoreType.DMA((lines, pieces)),
+            pltpu.SemaphoreType.DMA((lines, pieces)),
+            pltpu.SemaphoreType.DMA((lines, pieces)),
+            pltpu.SemaphoreType.DMA((lines + 1, pieces)),
+        ],
+        compiler_params=pltpu.CompilerParams(
+            collective_id=1, has_side_effects=True, vmem_limit_bytes=63 * 2**20
+        ),
+        cost_estimate=pl.CostEstimate(flops=0, bytes_accessed=count * rows * width * 16, transcendentals=0),
+        name="sum_rows",
+    )(partial.astype(BF16).reshape(count, rows, width))
 
 
 def columns_of_rows(weight, parts):
@@ -214,7 +621,7 @@
     rows = weight.shape[0]
     split = weight.reshape(rows, parts, count, -1).transpose(2, 0, 1, 3)
     mine = lax.all_to_all(split, "ctx", split_axis=0, concat_axis=0)
-    both = lax.all_gather(mine, "fsdp", axis=1)
+    both = pair_gather(mine, 1)
     return both.reshape(count * both.shape[1] * rows, parts, -1)
 
 
@@ -222,14 +629,14 @@
     count = lax.axis_size("ctx")
     pair = lax.axis_size("fsdp")
     rows = grad.shape[0] // (count * pair)
-    pieces = grad.astype(BF16).reshape(count, pair, rows, *grad.shape[1:])
-    summed = lax.psum_scatter(pieces, "fsdp", scatter_dimension=1, tiled=False)
+    pieces = grad.reshape(count, pair, rows, *grad.shape[1:])
+    summed = pair_reduce(pieces, 1).astype(BF16)
     mine = lax.all_to_all(summed, "ctx", split_axis=0, concat_axis=0)
     return mine.transpose(1, 2, 0, 3).reshape(rows, -1).astype(F32)
 
 
 def pair_sum(grad):
-    return lax.psum_scatter(grad, "fsdp", scatter_dimension=0, tiled=True)
+    return pair_reduce(grad.reshape(2, grad.shape[0] // 2, *grad.shape[1:]), 0)
 
 
 def rows_to_columns(local):
@@ -292,18 +699,28 @@
     head_ids = (first_head + jnp.arange(heads)).astype(F32)
     slopes = 2.0 ** (-8.0 * (head_ids + 1.0) / head_count)
 
-    vectors = jnp.stack([ln1_gain, ln1_bias, b_out, ln2_gain, ln2_bias, b_down])
-    vectors = lax.all_gather(vectors, BOTH, axis=1, tiled=True).astype(F32)
-    gain_one, shift_one, b_out_all, gain_two, shift_two, b_down_all = vectors
-    pair_vectors = lax.all_gather(jnp.stack([bias_q, bias_v]), "fsdp", axis=1, tiled=True)
-    pair_vectors = widen(pair_vectors.astype(F32), share)
-    b_up_own = lax.all_gather(b_up, "fsdp", axis=0, tiled=True).astype(F32)
+    vectors = [ln1_gain, ln1_bias, b_out, ln2_gain, ln2_bias, b_down, bias_q, bias_v, b_up]
+    devices = count * lax.axis_size("fsdp")
+    own_vectors = jnp.concatenate([vector.astype(F32) for vector in vectors])
+    everywhere = exchange(jnp.broadcast_to(own_vectors, (devices, own_vectors.shape[0])))
+    at = 0
+    whole_vectors = []
+    for vector in vectors:
+        whole_vectors.append(everywhere[:, at : at + vector.shape[0]].reshape(-1))
+        at += vector.shape[0]
+    gain_one, shift_one, b_out_all, gain_two, shift_two, b_down_all = whole_vectors[:6]
+    head_at = first_head * HEAD_DIM
+    bias_q_own, bias_v_own = (
+        lax.dynamic_slice_in_dim(vector, head_at, heads * HEAD_DIM) for vector in whole_vectors[6:8]
+    )
+    ff_cols = whole_vectors[8].shape[0] // count
+    b_up_own = lax.dynamic_slice_in_dim(whole_vectors[8], rank * ff_cols, ff_cols)
 
     w_qkv_own = columns_of_rows(w_qkv, 3)
     w_qkv_head = widen(w_qkv_own, share).reshape(width, -1)
     w_qkv_own = w_qkv_own.reshape(width, -1)
     w_up_own = columns_of_rows(w_up, 1).reshape(width, -1)
-    w_down_own = lax.all_gather(w_down, "fsdp", axis=0, tiled=True)
+    w_down_own = pair_gather(w_down, 0).reshape(-1, width)
     w_out_all = lax.all_gather(w_out, BOTH, axis=0, tiled=True)
 
     inputs = tokens[0].astype(F32)
@@ -311,11 +728,11 @@
     normed = (unit_one * gain_one + shift_one).astype(BF16)
     normed_all = gather_rows(normed)
     grad_out = cotangent[0]
-    grad_out_all = gather_rows(grad_out)
+    grad_out_all = gather_beside(grad_out)
 
     projected = jnp.dot(normed_all, w_qkv_head, preferred_element_type=F32)
     head_width = heads * HEAD_DIM
-    shift = jnp.concatenate([pair_vectors[0], jnp.zeros(head_width, F32), pair_vectors[1]])
+    shift = jnp.concatenate([bias_q_own, jnp.zeros(head_width, F32), bias_v_own])
     projected = to_sequence((projected + shift).astype(BF16), count)
     queries, keys, values = (
         projected[:, part * head_width : (part + 1) * head_width] for part in range(3)
@@ -337,19 +754,14 @@
     grad_normed_two = sum_rows(
         lax.dot_general(grad_hidden, w_up_own, NT, preferred_element_type=F32)
     )
-    branch = sum_rows(jnp.dot(activated, w_down_own, preferred_element_type=F32))
+    branch = sum_beside(jnp.dot(activated, w_down_own, preferred_element_type=F32))
     outputs = (middle + branch + b_down_all).astype(BF16)
 
     grad_w_down = pair_sum(
-        lax.dot_general(activated, grad_out_all, TN, preferred_element_type=F32).astype(BF16)
-    ).astype(F32)
+        lax.dot_general(activated, grad_out_all, TN, preferred_element_type=F32)
+    )
     grad_w_up = rows_of_columns(
         lax.dot_general(normed_two_all, grad_hidden, TN, preferred_element_type=F32)[:, None]
-    )
-    grad_b_up = pair_sum(jnp.sum(grad_hidden.astype(F32), axis=0))
-    own = rank * own_cols
-    grad_b_down = pair_sum(
-        jnp.sum(lax.dynamic_slice_in_dim(grad_out_all, own, own_cols, 1).astype(F32), axis=0)
     )
 
     grad_middle = grad_out.astype(F32) + norm_back(unit_two, rate_two, gain_two, grad_normed_two)
@@ -358,12 +770,9 @@
         grad_branch, w_out_all, NT, preferred_element_type=F32
     ).astype(BF16)
     grad_heads = to_sequence(widen(rows_to_columns(grad_attended), share), count)
-    grad_branch_all = gather_rows(grad_branch)
+    grad_branch_all = gather_beside(grad_branch)
     grad_w_out = pair_sum(
-        lax.dot_general(attended_own, grad_branch_all, TN, preferred_element_type=F32).astype(BF16)
-    ).astype(F32)
-    grad_b_out = pair_sum(
-        jnp.sum(lax.dynamic_slice_in_dim(grad_branch_all, own, own_cols, 1).astype(F32), axis=0)
+        lax.dot_general(attended_own, grad_branch_all, TN, preferred_element_type=F32)
     )
 
     delta = (grad_heads.astype(F32) * attended_full).reshape(seq_len, heads, HEAD_DIM)
@@ -375,8 +784,6 @@
         [narrow(to_layout(part, count), share) for part in grad_parts], axis=1
     )
     column_sums = jnp.sum(grad_qkv.astype(F32), axis=0)
-    grad_bias_q = pair_sum(column_sums[:own_cols])
-    grad_bias_v = pair_sum(column_sums[2 * own_cols :])
     grad_normed = sum_rows(lax.dot_general(grad_qkv, w_qkv_own, NT, preferred_element_type=F32))
     grad_w_qkv = rows_of_columns(
         lax.dot_general(normed_all, grad_qkv, TN, preferred_element_type=F32).reshape(
@@ -385,27 +792,47 @@
     )
     grad_inputs = grad_middle + norm_back(unit_one, rate_one, gain_one, grad_normed)
 
-    norm_sums = jnp.stack(
+    pair = devices // count
+    full_sums = jnp.stack(
         [
             jnp.sum(grad_normed * unit_one, axis=0),
             jnp.sum(grad_normed, axis=0),
             jnp.sum(grad_normed_two * unit_two, axis=0),
             jnp.sum(grad_normed_two, axis=0),
+            jnp.sum(grad_branch.astype(F32), axis=0),
+            jnp.sum(grad_out.astype(F32), axis=0),
         ]
     )
-    norm_sums = lax.psum_scatter(norm_sums, BOTH, scatter_dimension=1, tiled=True)
+    full_sums = full_sums.reshape(6, devices, -1).transpose(1, 0, 2).reshape(devices, -1)
+    own_sums = jnp.concatenate(
+        [
+            column_sums[:own_cols].reshape(pair, -1),
+            column_sums[2 * own_cols :].reshape(pair, -1),
+            jnp.sum(grad_hidden.astype(F32), axis=0).reshape(pair, -1),
+        ],
+        axis=1,
+    )
+    here = (jnp.arange(count) == rank)[:, None, None]
+    own_sums = jnp.where(here, own_sums[None], 0.0).reshape(devices, -1)
+    sums = jnp.sum(exchange(jnp.concatenate([full_sums, own_sums], axis=1)), axis=0)
+    share_of = width // devices
+    (
+        grad_ln1_gain, grad_ln1_bias, grad_ln2_gain, grad_ln2_bias, grad_b_out, grad_b_down,
+        grad_bias_q, grad_bias_v,
+    ) = sums[: 8 * share_of].reshape(8, share_of)
+    grad_b_up = sums[8 * share_of :]
     return (
         outputs[None],
         grad_inputs[None],
-        norm_sums[0],
-        norm_sums[1],
+        grad_ln1_gain,
+        grad_ln1_bias,
         grad_w_qkv,
         grad_bias_q,
         grad_bias_v,
         grad_w_out,
         grad_b_out,
-        norm_sums[2],
-        norm_sums[3],
+        grad_ln2_gain,
+        grad_ln2_bias,
         grad_w_up,
         grad_b_up,
         grad_w_down,

time: 1240 us -> 738 us (0.60)
  waiting for transfers between devices: 842 us -> 130 us
  Pallas kernels: 46.7 us -> 334 us
  blocking collectives: 119 us -> 0 us
  local copies, waits for them, and re-layouts: 43 us -> 67.9 us
  starting transfers between devices: 25.5 us -> 49 us
  other arithmetic: 23.2 us -> 40.4 us
  matrix products: 111 us -> 96.5 us
    all_gather x7 -> x2, waiting for transfers between devices: 344 us -> 0.01 us  [gather_beside(): return lax.all_gather(rows_in, 'ctx', axis=0, tiled=True)]
    reduce_scatter x6 -> x1, waiting for transfers between devices: 320 us -> 32 us  [sum_beside(): lax.psum_scatter(partial.astype(BF16), 'ctx', scatter_dimension=0, tiled=...]
    pallas_call x0 -> x4, Pallas kernels: none -> 288 us  [the longest x2 155 us: gather_rows(): pl.pallas_call(functools.partial(gather_kernel, count, pieces), out_shape...]
    unnamed x18 -> x4, waiting for transfers between devices: 133 us -> 1.41 us
    all_gather x3 -> x0, blocking collectives: 84.3 us -> none  [the longest x1 75.6 us: on_device(): vectors = lax.all_gather(vectors, BOTH, axis=1, tiled=True).astype(F32)]
    all_to_all x1 -> x0, blocking collectives: 29.4 us -> none  [rows_of_columns(): mine = lax.all_to_all(summed, 'ctx', split_axis=0, concat_axis=0)]
    all_gather x1, waiting for transfers between devices: 29.2 us -> 0.02 us  [on_device(): w_out_all = lax.all_gather(w_out, BOTH, axis=0, tiled=True)]
    dot_general x0 -> x4, local copies, waits for them, and re-layouts: none -> 28.5 us  [the longest x2 14 us: on_device(): lax.dot_general(normed_all, grad_qkv, TN, preferred_element_type=F32)]
  transfers between devices with their start and end apart: 21 -> 19, of which waited for: 16 -> 8; matrix products, arithmetic and copies ran while one was open for 11% -> 26% of each run, Pallas kernels for 4% -> 46%
where the time goes in v2:
time: 738 us; the launch traced here: 732 us
  Pallas kernels  334 us (45%)
  waiting for transfers between devices  130 us (18%)
  matrix products  96.5 us (13%)
  local copies, waits for them, and re-layouts  67.9 us (9%)
  starting transfers between devices  49 us (7%)
  other arithmetic  40.4 us (5%)
  between operations  14.8 us (2%)
    pallas_call x2, Pallas kernels, gather_rows(): pl.pallas_call(functools.partial(gather_kernel, count, pieces), out_shape...  155 us
    pallas_call x2, Pallas kernels, sum_rows(): pl.pallas_call(functools.partial(sum_kernel, count, pieces), out_shape=ja...  133 us
    reduce_scatter x1, waiting for transfers between devices, sum_beside(): lax.psum_scatter(partial.astype(BF16), 'ctx', scatter_dimension=0, tiled=...  32 us
    all_to_all x2, waiting for transfers between devices, rows_of_columns(): mine = lax.all_to_all(summed, 'ctx', split_axis=0, concat_axis=0)  26.4 us
    pallas_call x1, Pallas kernels, attend(): pl.pallas_call(functools.partial(attend_kernel, rows, heads), grid=(seq_l...  26.2 us
    all_to_all x2, waiting for transfers between devices, columns_of_rows(): mine = lax.all_to_all(split, 'ctx', split_axis=0, concat_axis=0)  25.7 us
    ppermute x7, waiting for transfers between devices, from_pair(): return lax.ppermute(mine, 'fsdp', [(0, 1), (1, 0)])  23.2 us
    pallas_call x1, Pallas kernels, attend_back(): pl.pallas_call(functools.partial(attend_back_kernel, rows, heads), grid=(...  20.2 us
  transfers between devices with their start and end apart: 19, of which 8 were waited for; matrix products, arithmetic and copies ran while one was open for 26% of the time, Pallas kernels for 46%

profile of v2, /device:TPU:0, one launch (start us, length us, event | category | flops | bytes accessed | tf_op | source)
XLA Modules:
  0.0 732.3 jit_solution(265707670519460244)
XLA Ops:
  8.7 6.1 concatenate.39
  15.4 7.3 %all-to-all-start = ((f32[32,8,128]{2,1,0:T(8,128)}), f32[32,8,128]{2,1,0:T(8,128)S(1)}, u32[]{:S(2)}, u32[]{:S(2)}) async-start(f32[32,8,128]{2,1,0:T(8,128)} %pad.16), calls=%async_computation | async-start | bytes 262144 | tf_op jit(solution)/shard_map/all_to_all | solution.py:235
  25.2 8.4 %all-to-all-done = f32[32,8,128]{2,1,0:T(8,128)S(1)} async-done(((f32[32,8,128]{2,1,0:T(8,128)}), f32[32,8,128]{2,1,0:T(8,128)S(1)}, u32[]{:S(2)}, u32[]{:S(2)}) %all-to-all-start) | async-done | bytes 131104 | tf_op jit(solution)/shard_map/all_to_all | solution.py:235
  33.6 3.6 all-to-all-start.1
  38.0 1.5 copy.122
  39.6 25.7 %all-to-all-done.1 = bf16[16,64,3,128]{3,1,2,0:T(8,128)(2,1)S(1)} async-done(((bf16[16,64,3,128]{3,1,2,0:T(8,128)(2,1)}), bf16[16,64,3,128]{3,1,2,0:T(8,128)(2,1)S(1)}, u32[]{:S(2)}, u32[]{:S(2)}) %all-to-all-start.1) | async-done | bytes 786464 | tf_op jit(solution)/shard_map/all_to_all | solution.py:623
  65.3 7.0 all-to-all-start.3
  76.2 103.3 %gather_rows.2 = bf16[16,128,2048]{2,1,0:T(8,128)(2,1)} custom-call(bf16[128,2048]{1,0:T(8,128)(2,1)} %fusion.39.own_ref), custom_call_target="tpu_custom_call" | custom-call | bytes 67108864 | tf_op jit(solution)/shard_map/gather_rows/pallas_call | solution.py:414
  179.6 1.4 collective-permute-start.1
  181.0 1.6 maximum_select_fusion.2
  182.6 1.5 copy.117
  184.1 8.8 %add_convert_fusion = bf16[2048,384]{1,0:T(8,128)(2,1)S(1)} fusion(bf16[2048,2048]{1,0:T(8,128)(2,1)} %bitcast.273, f32[384]{0:T(512)S(1)} %pad_maximum_fusion.8, bf16[256,8,3,128]{3,2,1,0:T(4,128)(2,1)S(1)} %bitcast.302), kind=kOutput, calls=%fused_computation.36 | convolution fusion | flops 3222798336 | bytes 11535872 | tf_op jit(solution)/shard_map/dot_general | solution.py:733
  194.6 26.2 %attend.1 = (f32[2048,128]{1,0:T(8,128)}, f32[2,2048]{1,0:T(2,128)}) custom-call(s32[8]{0:T(128)} %and_select_fusion.low_ref, f32[2]{0:T(128)} %multiply_power_fusion.slope_ref, s32[1,2048]{1,0:T(1,128)} %bitcast.331, bf16[2048,128]{1,0:T(8,128)(2,1)} %get-tuple-element.40.q_ref, bf16[2048,128]{1,0:T(8,128)(2,1)} %get-tuple-element.39.k_ref, ...), custom_call_target="tpu_custom_call" | custom-call | tf_op jit(solution)/shard_map/attend/pallas_call | solution.py:162
  223.0 3.6 all-to-all-start.2
  226.9 3.9 maximum_select_fusion.1
  230.8 3.1 maximum_select_fusion
  234.0 6.8 all-to-all-done.2
  241.1 4.7 fusion.66
  247.8 51.6 %gather_rows.3 = bf16[16,128,2048]{2,1,0:T(8,128)(2,1)} custom-call(bf16[128,2048]{1,0:T(8,128)(2,1)} %add_convert_fusion.2.own_ref), custom_call_target="tpu_custom_call" | custom-call | bytes 67108864 | tf_op jit(solution)/shard_map/gather_rows/pallas_call | solution.py:414
  299.5 17.6 %multiply_convert_fusion = (bf16[2048,512]{1,0:T(8,128)(2,1)S(1)}, f32[2048,512]{1,0:T(8,128)}, f32[2048,512]{1,0:T(8,128)}) fusion(f32[512]{0:T(512)S(1)} %dynamic_slice.35, bf16[2048,2048]{1,0:T(8,128)(2,1)} %bitcast.275, bf16[2048,512]{1,0:T(8,128)(2,1)} %bitcast.307), kind=kOutput, calls=%fused_computation.21 | convolution fusion | flops 4364173312 | bytes 20973568 | tf_op jit(solution)/shard_map/dot_general | solution.py:748
  317.1 1.4 copy-done.29
  318.5 6.8 convolution_convert_fusion.2
  325.5 11.6 %convert_reduce_fusion = (f32[512]{0:T(512)S(1)}, bf16[2048,512]{1,0:T(8,128)(2,1)S(1)}) fusion(f32[2048,512]{1,0:T(8,128)} %get-tuple-element.37, bf16[512,2048]{1,0:T(8,128)(2,1)S(1)} %bitcast.306, bf16[1,2048,2048]{2,1,0:T(8,128)(2,1)} %all-gather.9.cloned.1.call-done, f32[2048,512]{1,0:T(8,128)} %get-tuple-element.74, f32[512]{0:T(512)S(1)} %dynamic_slice.35), kind=kOutput, calls=%fused_computation.20 | convolution fusion | flops 4312792576 | bytes 20975616 | tf_op jit(solution)/shard_map/dot_general | solution.py:752
  337.1 6.9 convolution_convert_fusion.1
  344.0 80.1 %sum_rows.2 = f32[128,2048]{1,0:T(8,128)} custom-call(bf16[16,128,2048]{2,1,0:T(8,128)(2,1)} %bitcast.277), custom_call_target="tpu_custom_call" | custom-call | bytes 67108864 | tf_op jit(solution)/shard_map/sum_rows/pallas_call | solution.py:593
  424.1 2.0 multiply_reduce_fusion
  426.1 32.0 %reduce-scatter.2.cloned.1.call-done = bf16[128,2048]{1,0:T(8,128)(2,1)} async-done(((bf16[2048,2048]{1,0:T(8,128)(2,1)}), bf16[128,2048]{1,0:T(8,128)(2,1)}) %reduce-scatter.2.cloned.1.call-update) | async-done | bytes 524304 | tf_op jit(solution)/shard_map/reduce_scatter | solution.py:209
  458.0 3.8 convert_reduce_fusion.4
  461.9 12.4 %copy.135 = bf16[2048,2048]{1,0:T(8,128)(2,1)} copy(bf16[2048,2048]{0,1:T(8,128)(2,1)} %bitcast.276) | data formatting | bytes 16777216 | tf_op jit(solution)/shard_map/dot_general | solution.py:764
  474.3 6.9 fusion.22
  481.2 2.1 copy-done.14
  483.4 1.6 collective-permute-start.5
  485.0 23.1 %collective-permute-done.5 = bf16[16,64,1,512]{3,1,0,2:T(8,128)(2,1)S(1)} collective-permute-done((bf16[16,64,1,512]{3,1,0,2:T(8,128)(2,1)S(1)}, bf16[16,64,1,512]{3,1,0,2:T(8,128)(2,1)S(1)}, u32[]{:S(2)}, u32[]{:S(2)}) %collective-permute-start.5) | collective-permute-done | bytes 1048608 | tf_op jit(solution)/shard_map/ppermute | solution.py:213
  508.1 2.9 fusion.50
  511.1 4.9 all-to-all-start.7
  516.0 7.6 %fusion.2 = f32[512,2048]{1,0:T(8,128)S(1)} fusion(bf16[2048,512]{1,0:T(8,128)(2,1)} %copy-done.29, bf16[1,2048,2048]{2,1,0:T(8,128)(2,1)} %all-gather.9.cloned.1.call-done), kind=kOutput, calls=%fused_computation.2 | convolution fusion | flops 4294967296 | bytes 14680064 | tf_op jit(solution)/shard_map/dot_general | solution.py:761
  523.6 2.0 copy-done.13
  526.7 1.5 collective-permute-start.6
  528.2 6.3 fusion.35
  535.5 15.6 %all-to-all-done.7 = bf16[16,64,1,512]{3,1,2,0:T(8,128)(2,1)S(1)} async-done(((bf16[16,64,1,512]{3,1,2,0:T(8,128)(2,1)}), bf16[16,64,1,512]{3,1,2,0:T(8,128)(2,1)S(1)}, u32[]{:S(2)}, u32[]{:S(2)}) %all-to-all-start.7) | async-done | bytes 1048608 | tf_op jit(solution)/shard_map/all_to_all | solution.py:634
  551.1 7.4 %all-to-all-start.4 = ((bf16[16,128,128]{2,1,0:T(8,128)(2,1)}), bf16[16,128,128]{2,1,0:T(8,128)(2,1)S(1)}, u32[]{:S(2)}, u32[]{:S(2)}) async-start(bf16[16,128,128]{2,1,0:T(8,128)(2,1)} %bitcast.311), calls=%async_computation.5 | async-start | bytes 1048576 | tf_op jit(solution)/shard_map/all_to_all | solution.py:646
  558.8 12.4 %copy.131 = bf16[2048,2048]{1,0:T(8,128)(2,1)} copy(bf16[2048,2048]{0,1:T(8,128)(2,1)} %bitcast.274) | data formatting | bytes 16777216 | tf_op jit(solution)/shard_map/dot_general | solution.py:789
  571.2 2.0 copy.134
  573.5 3.6 bitcast_add_fusion
  577.4 1.5 copy.154
  580.3 1.6 copy.127
  582.5 20.2 %attend_back.1 = (bf16[2048,128]{1,0:T(8,128)(2,1)}, bf16[2048,128]{1,0:T(8,128)(2,1)}, bf16[2048,128]{1,0:T(8,128)(2,1)}) custom-call(s32[8]{0:T(128)} %and_select_fusion.low_ref, f32[2]{0:T(128)} %multiply_power_fusion.slope_ref, s32[1,2048]{1,0:T(1,128)} %bitcast.332, f32[2,2048]{1,0:T(2,128)} %get-tuple-element.21.total_ref, f32[2,2048]{1,0:T(2,128)} %bitcast.333, ...), custom_call_target="tpu_custom_call" | custom-call | tf_op jit(solution)/shard_map/attend_back/pallas_call | solution.py:183
  607.4 1.6 copy.132
  609.0 7.5 %fusion.68 = f32[16,2,64,3,128]{4,2,3,1,0:T(8,128)S(1)} fusion(bf16[16,2,64,2048,1]{3,2,4,1,0:T(8,128)(2,1)} %bitcast.279, bf16[3,128,2048,1,1]{2,1,0,4,3:T(8,128)(2,1)} %bitcast.314), kind=kOutput, calls=%fused_computation.157 | convolution fusion | flops 3221225472 | bytes 13107200 | tf_op jit(solution)/shard_map/dot_general | solution.py:789
  616.6 1.6 copy-done.19
  619.3 1.4 collective-permute-start.3
  620.7 7.0 convolution_convert_fusion
  627.6 52.6 %sum_rows.3 = f32[128,2048]{1,0:T(8,128)} custom-call(bf16[16,128,2048]{2,1,0:T(8,128)(2,1)} %bitcast.278), custom_call_target="tpu_custom_call" | custom-call | bytes 67108864 | tf_op jit(solution)/shard_map/sum_rows/pallas_call | solution.py:593
  680.2 1.7 fusion.45
  682.4 2.0 convert_reduce_fusion.1
  685.4 3.9 all-to-all-start.5
  689.3 2.8 fusion.27
  692.1 5.8 all-to-all-done.5
  697.9 4.3 all-to-all-start.6
  702.2 1.4 fusion.44
  704.8 4.8 fusion
  710.1 10.8 %all-to-all-done.6 = bf16[16,64,3,128]{3,1,2,0:T(8,128)(2,1)} async-done(((bf16[16,64,3,128]{3,1,2,0:T(8,128)(2,1)}), bf16[16,64,3,128]{3,1,2,0:T(8,128)(2,1)}, u32[]{:S(2)}, u32[]{:S(2)}) %all-to-all-start.6) | async-done | bytes 786464 | tf_op jit(solution)/shard_map/all_to_all | solution.py:634
  720.8 1.3 convert_bitcast_fusion.1
  723.1 1.6 copy.168
  (180 shorter events, 31.5 us)
Async XLA Ops:
  7.2 30.3 %copy-start.28 = (s32[1,8]{1,0:T(1,128)S(1)}, s32[1,8]{1,0:T(1,128)}, u32[]{:S(2)}) copy-start(s32[1,8]{1,0:T(1,128)} %param.17) | copy-start | bytes 100
  7.2 30.5 %copy-start.20 = (bf16[64,8192]{1,0:T(8,128)(2,1)S(1)}, bf16[64,8192]{1,0:T(8,128)(2,1)}, u32[]{:S(2)}) copy-start(bf16[64,8192]{1,0:T(8,128)(2,1)} %param.27) | copy-start | bytes 3145732
  7.2 233.9 %all-gather.5.cloned.1.call-start = ((), (), s32[]{:S(2)}) async-start(), calls=%async_computation.9 | async-start | bytes 8650752 | tf_op jit(solution)/shard_map/all_gather | solution.py:724
  7.9 317.5 %all-gather.9.cloned.1.call-start = ((), (), s32[]{:S(2)}) async-start(), calls=%async_computation.12 | async-start | bytes 8912896 | tf_op jit(solution)/shard_map/all_gather | solution.py:205
  15.4 18.1 %all-to-all-start = ((f32[32,8,128]{2,1,0:T(8,128)}), f32[32,8,128]{2,1,0:T(8,128)S(1)}, u32[]{:S(2)}, u32[]{:S(2)}) async-start(f32[32,8,128]{2,1,0:T(8,128)} %pad.16), calls=%async_computation | async-start | bytes 262144 | tf_op jit(solution)/shard_map/all_to_all | solution.py:235
  25.2 47.9 %copy-start.1 = (bf16[1,128,2048]{2,1,0:T(8,128)(2,1)S(1)}, bf16[1,128,2048]{2,1,0:T(8,128)(2,1)}, u32[]{:S(2)}) copy-start(bf16[1,128,2048]{2,1,0:T(8,128)(2,1)} %param.16) | copy-start | bytes 1572868
  33.6 31.7 %all-to-all-start.1 = ((bf16[16,64,3,128]{3,1,2,0:T(8,128)(2,1)}), bf16[16,64,3,128]{3,1,2,0:T(8,128)(2,1)S(1)}, u32[]{:S(2)}, u32[]{:S(2)}) async-start(bf16[16,64,3,128]{3,1,2,0:T(8,128)(2,1)} %copy.116), calls=%async_computation.1 | async-start | bytes 1572864 | tf_op jit(solution)/shard_map/all_to_all | solution.py:623
  37.2 189.7 %collective-permute-start.2 = (bf16[256,2048]{1,0:T(8,128)(2,1)}, bf16[256,2048]{1,0:T(8,128)(2,1)}, u32[]{:S(2)}, u32[]{:S(2)}) collective-permute-start(bf16[256,2048]{1,0:T(8,128)(2,1)} %param.29), channel_id=1, source_target_pairs={{0,1},{1,0},{2,3},{3,2},{4,5},{5,4},{6,7},{7,6},{8,9},{9,8},{10,11... | collective-permute-start | bytes 3145736 | tf_op jit(solution)/shard_map/ppermute | solution.py:213
  65.3 114.3 %all-to-all-start.3 = ((bf16[16,64,1,512]{3,1,2,0:T(8,128)(2,1)}), bf16[16,64,1,512]{3,1,2,0:T(8,128)(2,1)S(1)}, u32[]{:S(2)}, u32[]{:S(2)}) async-start(bf16[16,64,1,512]{3,1,2,0:T(8,128)(2,1)} %copy.122), calls=%async_computation.3 | async-start | bytes 2097152 | tf_op jit(solution)/shard_map/all_to_all | solution.py:623
  72.4 107.1 %copy-start.23 = (s32[2048]{0:T(1024)}, s32[2048]{0:T(1024)S(1)}, u32[]{:S(2)}) copy-start(s32[2048]{0:T(1024)S(1)} %select_reduce_fusion) | copy-start | bytes 24580
  73.2 106.3 %copy-start.24 = (f32[128]{0:T(128)}, f32[128]{0:T(128)S(1)}, u32[]{:S(2)}) copy-start(f32[128]{0:T(128)S(1)} %broadcast_multiply_fusion.5) | copy-start | bytes 1540
  73.5 106.0 %copy-start.26 = (f32[128]{0:T(128)}, f32[128]{0:T(128)S(1)}, u32[]{:S(2)}) copy-start(f32[128]{0:T(128)S(1)} %add_rsqrt_fusion.1) | copy-start | bytes 1540
  74.1 106.9 %collective-permute-start = (bf16[16,64,3,128]{3,1,2,0:T(8,128)(2,1)S(1)}, bf16[16,64,3,128]{3,1,2,0:T(8,128)(2,1)}, u32[]{:S(2)}, u32[]{:S(2)}) collective-permute-start(bf16[16,64,3,128]{3,1,2,0:T(8,128)(2,1)S(1)} %all-to-all-done.1), channel_id=1, source_target_pairs={{0,1},{1,0},{2,3},{3,2},{4,5},{5,4},{6,7},{7,6},{8,9},{9,8},{10,11... | collective-permute-start | bytes 2359304 | tf_op jit(solution)/shard_map/ppermute | solution.py:213
  74.9 104.6 %copy-start.21 = (f32[2048]{0:T(1024)}, f32[2048]{0:T(1024)S(1)}, u32[]{:S(2)}) copy-start(f32[2048]{0:T(1024)S(1)} %mul.141) | copy-start | bytes 24580
  179.6 51.2 %collective-permute-start.1 = (bf16[16,64,1,512]{3,1,0,2:T(8,128)(2,1)S(1)}, bf16[16,64,1,512]{3,1,0,2:T(8,128)(2,1)}, u32[]{:S(2)}, u32[]{:S(2)}) collective-permute-start(bf16[16,64,1,512]{3,1,0,2:T(8,128)(2,1)S(1)} %bitcast.293), channel_id=1, source_target_pairs={{0,1},{1,0},{2,3},{3,2},{4,5},{5,4},{6,7},{7,6},{8,9},{9,8},{10,11... | collective-permute-start | bytes 3145736 | tf_op jit(solution)/shard_map/ppermute | solution.py:213
  184.1 8.8 %copy-start.15 = (bf16[16,2,64,3,128]{4,3,2,1,0:T(4,128)(2,1)}, bf16[16,2,64,3,128]{4,3,2,1,0:T(4,128)(2,1)S(1)}, u32[]{:S(2)}) copy-start(bf16[16,2,64,3,128]{4,3,2,1,0:T(4,128)(2,1)S(1)} %copy.117) | copy-start | bytes 4718596
  223.0 17.8 %all-to-all-start.2 = ((bf16[16,128,128]{2,1,0:T(8,128)(2,1)}), bf16[16,128,128]{2,1,0:T(8,128)(2,1)S(1)}, u32[]{:S(2)}, u32[]{:S(2)}) async-start(bf16[16,128,128]{2,1,0:T(8,128)(2,1)} %bitcast.16), calls=%async_computation.2 | async-start | bytes 1048576 | tf_op jit(solution)/shard_map/all_to_all | solution.py:653
  226.5 231.5 %reduce-scatter.2.cloned.1.call-start = ((), (), s32[]{:S(2)}) async-start(), calls=%async_computation.10 | async-start | bytes 8912896 | tf_op jit(solution)/shard_map/reduce_scatter | solution.py:209
  245.8 1.0 copy-start
  299.5 19.0 %copy-start.17 = (bf16[2,256,2048]{2,1,0:T(8,128)(2,1)S(1)}, bf16[2,256,2048]{2,1,0:T(8,128)(2,1)}, u32[]{:S(2)}) copy-start(bf16[2,256,2048]{2,1,0:T(8,128)(2,1)} %maximum_select_fusion.1) | copy-start | bytes 6291460
  317.1 1.4 copy-start.29
  325.3 379.5 %all-gather.7.cloned.1.call-start = ((), (), s32[]{:S(2)}) async-start(), calls=%async_computation.11 | async-start | bytes 8912896 | tf_op jit(solution)/shard_map/all_gather | solution.py:205
  325.5 11.6 %copy-start.18 = (bf16[16,2,64,1,512]{4,2,1,0,3:T(8,128)(2,1)S(1)}, bf16[16,2,64,1,512]{4,2,1,0,3:T(8,128)(2,1)}, u32[]{:S(2)}) copy-start(bf16[16,2,64,1,512]{4,2,1,0,3:T(8,128)(2,1)} %maximum_select_fusion) | copy-start | bytes 6291460
  337.0 6.9 copy-start.30
  461.9 12.4 %copy-start.31 = (bf16[2048,512]{1,0:T(8,128)(2,1)S(1)}, bf16[2048,512]{1,0:T(8,128)(2,1)}, u32[]{:S(2)}) copy-start(bf16[2048,512]{1,0:T(8,128)(2,1)} %copy-done.30) | copy-start | bytes 6291460
  481.2 2.1 copy-start.14
  483.4 24.7 %collective-permute-start.5 = (bf16[16,64,1,512]{3,1,0,2:T(8,128)(2,1)S(1)}, bf16[16,64,1,512]{3,1,0,2:T(8,128)(2,1)S(1)}, u32[]{:S(2)}, u32[]{:S(2)}) collective-permute-start(bf16[16,64,1,512]{3,1,0,2:T(8,128)(2,1)S(1)} %fusion.48), channel_id=1, source_target_pairs={{0,1},{1,0},{2,3},{3,2},{4,5},{5,4},{6,7},{7,6},{8,9},{9,8},{10,11... | collective-permute-start | bytes 3145736 | tf_op jit(solution)/shard_map/ppermute | solution.py:213
  511.1 40.0 %all-to-all-start.7 = ((bf16[16,64,1,512]{3,1,2,0:T(8,128)(2,1)}), bf16[16,64,1,512]{3,1,2,0:T(8,128)(2,1)S(1)}, u32[]{:S(2)}, u32[]{:S(2)}) async-start(bf16[16,64,1,512]{3,1,2,0:T(8,128)(2,1)} %fusion.50), calls=%async_computation.8 | async-start | bytes 2097152 | tf_op jit(solution)/shard_map/all_to_all | solution.py:634
  516.0 12.2 %copy-start.3 = (bf16[128,2048]{1,0:T(8,128)(2,1)S(1)}, bf16[128,2048]{1,0:T(8,128)(2,1)}, u32[]{:S(2)}) copy-start(bf16[128,2048]{1,0:T(8,128)(2,1)} %get-tuple-element.34) | copy-start | bytes 1572868
  523.6 2.0 copy-start.13
  526.7 31.8 %copy-start.4 = (bf16[1,128,2048]{2,1,0:T(8,128)(2,1)S(1)}, bf16[1,128,2048]{2,1,0:T(8,128)(2,1)}, u32[]{:S(2)}) copy-start(bf16[1,128,2048]{2,1,0:T(8,128)(2,1)} %param.31) | copy-start | bytes 1572868
  526.7 46.7 %collective-permute-start.6 = (bf16[256,2048]{1,0:T(8,128)(2,1)}, bf16[256,2048]{1,0:T(8,128)(2,1)}, u32[]{:S(2)}, u32[]{:S(2)}) collective-permute-start(bf16[256,2048]{1,0:T(8,128)(2,1)} %fusion.49), channel_id=1, source_target_pairs={{0,1},{1,0},{2,3},{3,2},{4,5},{5,4},{6,7},{7,6},{8,9},{9,8},{10,11... | collective-permute-start | bytes 3145736 | tf_op jit(solution)/shard_map/ppermute | solution.py:213
  551.1 27.9 %all-to-all-start.4 = ((bf16[16,128,128]{2,1,0:T(8,128)(2,1)}), bf16[16,128,128]{2,1,0:T(8,128)(2,1)S(1)}, u32[]{:S(2)}, u32[]{:S(2)}) async-start(bf16[16,128,128]{2,1,0:T(8,128)(2,1)} %bitcast.311), calls=%async_computation.5 | async-start | bytes 1048576 | tf_op jit(solution)/shard_map/all_to_all | solution.py:646
  577.3 1.8 copy-start.12
  579.1 3.4 copy-start.5
  606.1 14.6 %copy-start.6 = (bf16[16,2,64,128]{3,2,1,0:T(8,128)(2,1)}, bf16[16,2,64,128]{3,2,1,0:T(8,128)(2,1)S(1)}, u32[]{:S(2)}) copy-start(bf16[16,2,64,128]{3,2,1,0:T(8,128)(2,1)S(1)} %pad_maximum_fusion.4) | copy-start | bytes 1572868
  606.1 0.9 copy-start.7
  606.2 1.0 copy-start.9
  609.0 11.6 %copy-start.8 = (bf16[16,2,64,128]{3,2,1,0:T(8,128)(2,1)S(1)}, bf16[16,2,64,128]{3,2,1,0:T(8,128)(2,1)}, u32[]{:S(2)}) copy-start(bf16[16,2,64,128]{3,2,1,0:T(8,128)(2,1)} %copy-done.7) | copy-start | bytes 1572868
  609.0 11.6 %copy-start.10 = (bf16[16,2,64,128]{3,2,1,0:T(8,128)(2,1)S(1)}, bf16[16,2,64,128]{3,2,1,0:T(8,128)(2,1)}, u32[]{:S(2)}) copy-start(bf16[16,2,64,128]{3,2,1,0:T(8,128)(2,1)} %copy-done.9) | copy-start | bytes 1572868
  609.0 11.6 %copy-start.16 = (bf16[16,2,64,3,128]{4,3,2,1,0:T(4,128)(2,1)S(1)}, bf16[16,2,64,3,128]{4,3,2,1,0:T(4,128)(2,1)}, u32[]{:S(2)}) copy-start(bf16[16,2,64,3,128]{4,3,2,1,0:T(4,128)(2,1)} %copy-done.15) | copy-start | bytes 4718596
  616.6 1.6 copy-start.19
  619.3 70.0 %collective-permute-start.3 = (bf16[16,64,3,128]{3,1,2,0:T(8,128)(2,1)}, bf16[16,64,3,128]{3,1,2,0:T(8,128)(2,1)}, u32[]{:S(2)}, u32[]{:S(2)}) collective-permute-start(bf16[16,64,3,128]{3,1,2,0:T(8,128)(2,1)} %fusion.51), channel_id=1, source_target_pairs={{0,1},{1,0},{2,3},{3,2},{4,5},{5,4},{6,7},{7,6},{8,9},{9,8},{10,11... | collective-permute-start | bytes 2359304 | tf_op jit(solution)/shard_map/ppermute | solution.py:213
  627.6 52.6 %copy-start.22 = (f32[2048]{0:T(1024)S(1)}, f32[2048]{0:T(1024)}, u32[]{:S(2)}) copy-start(f32[2048]{0:T(1024)} %copy-done.21) | copy-start | bytes 24580
  627.6 52.6 %copy-start.25 = (f32[128]{0:T(128)S(1)}, f32[128]{0:T(128)}, u32[]{:S(2)}) copy-start(f32[128]{0:T(128)} %copy-done.24) | copy-start | bytes 1540
  627.6 52.6 %copy-start.27 = (f32[128]{0:T(128)S(1)}, f32[128]{0:T(128)}, u32[]{:S(2)}) copy-start(f32[128]{0:T(128)} %copy-done.26) | copy-start | bytes 1540
  681.9 20.2 %copy-start.2 = (f32[128,2048]{1,0:T(8,128)S(1)}, f32[128,2048]{1,0:T(8,128)}, u32[]{:S(2)}) copy-start(f32[128,2048]{1,0:T(8,128)} %sum_rows.3) | copy-start | bytes 3145732
  681.9 20.2 %copy-start.11 = (f32[128,2048]{1,0:T(8,128)S(1)}, f32[128,2048]{1,0:T(8,128)}, u32[]{:S(2)}) copy-start(f32[128,2048]{1,0:T(8,128)} %get-tuple-element.35) | copy-start | bytes 3145732
  685.4 12.5 %all-to-all-start.5 = ((f32[32,8,128]{2,1,0:T(8,128)}), f32[32,8,128]{2,1,0:T(8,128)S(1)}, u32[]{:S(2)}, u32[]{:S(2)}) async-start(f32[32,8,128]{2,1,0:T(8,128)} %bitcast.121), calls=%async_computation.6 | async-start | bytes 262144 | tf_op jit(solution)/shard_map/all_to_all | solution.py:235
  697.9 23.0 %all-to-all-start.6 = ((bf16[16,64,3,128]{3,1,2,0:T(8,128)(2,1)}), bf16[16,64,3,128]{3,1,2,0:T(8,128)(2,1)}, u32[]{:S(2)}, u32[]{:S(2)}) async-start(bf16[16,64,3,128]{3,1,2,0:T(8,128)(2,1)} %fusion.27), calls=%async_computation.7 | async-start | bytes 1572864 | tf_op jit(solution)/shard_map/all_to_all | solution.py:634
  709.7 15.0 %collective-permute-start.4 = (bf16[64,2048]{1,0:T(8,128)(2,1)S(1)}, bf16[64,2048]{1,0:T(8,128)(2,1)S(1)}, u32[]{:S(2)}, u32[]{:S(2)}) collective-permute-start(bf16[64,2048]{1,0:T(8,128)(2,1)S(1)} %fusion.53), channel_id=1, source_target_pairs={{0,1},{1,0},{2,3},{3,2},{4,5},{5,4},{6,7},{7,6},{8,9},{9,8},{10,11... | collective-permute-start | bytes 786440 | tf_op jit(solution)/shard_map/ppermute | solution.py:213
Sparse Core Ops, SparseCore 0:
  11.1 113.4 all-gather.4
  126.8 84.1 all-gather.8
  325.5 132.5 reduce-scatter.1
  462.0 89.6 all-gather.6

commit v3 on v2

--- a/solution.py
+++ b/solution.py
@@ -15,6 +15,7 @@
 TN = (((0,), (0,)), ((), ()))
 F32 = jnp.float32
 BF16 = jnp.bfloat16
+BUSY = 160 * 2**20
 
 
 def gelu_exact(pre_activation):
@@ -65,39 +66,32 @@
         at = pl.ds(pl.multiple_of(key_block * rows, rows), rows)
         return (query_at - key_at).astype(F32), allowed, at
 
-    def total_step(key_block, carried):
-        distance, allowed, at = parts(key_block)
-        keys = k_ref[at, :]
-        following = []
-        for head in range(heads):
-            top, total = carried[head]
-            scores = scores_block(keys, query_heads[head], slope_ref[head], distance, allowed)
-            new_top = jnp.maximum(top, jnp.max(scores, axis=0, keepdims=True))
-            total = total * jnp.exp(top - new_top) + jnp.sum(
-                jnp.exp(scores - new_top), axis=0, keepdims=True
-            )
-            following.append((new_top, total))
-        return following
-
-    begin = [(jnp.full((1, rows), MASKED, F32), jnp.zeros((1, rows), F32))] * heads
-    totals = lax.fori_loop(low, block + 1, total_step, begin)
-    log_totals = [top + jnp.log(total) for top, total in totals]
-    for head in range(heads):
-        total_ref[head : head + 1, :] = log_totals[head]
-
-    def output_step(key_block, accum):
+    def step(key_block, carried):
         distance, allowed, at = parts(key_block)
         keys = k_ref[at, :]
         values = v_ref[at, :]
+        following = []
         for head in range(heads):
+            top, total, accum = carried[head]
             scores = scores_block(keys, query_heads[head], slope_ref[head], distance, allowed)
-            probs = jnp.exp(scores - log_totals[head]).astype(BF16)
-            accum = accum + lax.dot_general(
-                probs, head_mask(values, head), TN, preferred_element_type=F32
+            new_top = jnp.maximum(top, jnp.max(scores, axis=0, keepdims=True))
+            shrink = jnp.exp(top - new_top)
+            weights = jnp.exp(scores - new_top)
+            total = total * shrink + jnp.sum(weights, axis=0, keepdims=True)
+            accum = accum * shrink + lax.dot_general(
+                values, weights.astype(BF16), TN, preferred_element_type=F32
             )
-        return accum
-
-    out_ref[...] = lax.fori_loop(low, block + 1, output_step, jnp.zeros(out_ref.shape, F32))
+            following.append((new_top, total, accum))
+        return following
+
+    width = out_ref.shape[1]
+    begin = (jnp.full((1, rows), MASKED, F32), jnp.zeros((1, rows), F32), jnp.zeros((width, rows), F32))
+    done = lax.fori_loop(low, block + 1, step, [begin] * heads)
+    for head in range(heads):
+        top, total, accum = done[head]
+        total_ref[head : head + 1, :] = top + jnp.log(total)
+        span = slice(head * HEAD_DIM, (head + 1) * HEAD_DIM)
+        out_ref[:, span] = jnp.transpose(accum[span, :] / total)
 
 
 def attend_back_kernel(
@@ -168,6 +162,7 @@
             jax.ShapeDtypeStruct((seq_len, width), F32),
             jax.ShapeDtypeStruct((heads, seq_len), F32),
         ],
+        cost_estimate=pl.CostEstimate(flops=0, bytes_accessed=BUSY // 3, transcendentals=0),
         name="attend",
     )(low, slopes, starts, queries, keys, values)
 
@@ -187,6 +182,7 @@
         out_specs=[block, whole, whole],
         out_shape=[jax.ShapeDtypeStruct((seq_len, width), BF16)] * 3,
         scratch_shapes=[pltpu.VMEM((seq_len, width), F32)] * 2,
+        cost_estimate=pl.CostEstimate(flops=0, bytes_accessed=BUSY // 3, transcendentals=0),
         name="attend_back",
     )(low, slopes, starts, log_total, delta, queries, grads, keys, values)
 
@@ -213,17 +209,10 @@
     return lax.ppermute(mine, "fsdp", [(0, 1), (1, 0)])
 
 
-def pair_gather(mine, axis):
-    other = from_pair(mine)
-    first = lax.axis_index("fsdp") == 0
-    return jnp.where(
-        first, jnp.stack([mine, other], axis=axis), jnp.stack([other, mine], axis=axis)
-    )
-
-
 def pair_reduce(grad, axis):
     here = lax.axis_index("fsdp")
-    given = lax.dynamic_index_in_dim(grad, 1 - here, axis, keepdims=False).astype(BF16)
+    grad = grad.astype(BF16)
+    given = lax.dynamic_index_in_dim(grad, 1 - here, axis, keepdims=False)
     kept = lax.dynamic_index_in_dim(grad, here, axis, keepdims=False)
     return kept.astype(F32) + from_pair(given).astype(F32)
 
@@ -425,10 +414,327 @@
             pltpu.SemaphoreType.DMA((count, pieces)),
         ],
         compiler_params=pltpu.CompilerParams(collective_id=0, has_side_effects=True),
-        cost_estimate=pl.CostEstimate(flops=0, bytes_accessed=count * rows * width * 16, transcendentals=0),
+        cost_estimate=pl.CostEstimate(flops=0, bytes_accessed=BUSY, transcendentals=0),
         name="gather_rows",
     )(own)
     return gathered.reshape(count * rows, width)
+
+
+def begin_kernel(count, pieces, shared, *refs):
+    inputs = len(shared) + 2
+    own_ref, sources, down_ref = refs[0], refs[1 : inputs - 1], refs[inputs - 1]
+    out_ref, targets, down_out = refs[inputs], refs[inputs + 1 : 2 * inputs - 1], refs[2 * inputs - 1]
+    (
+        keep_sem, up_sem, down_sem, across_sem, chip_sem, recv_sem,
+        give_sem, take_sem, pass_sem, passed_sem, stay_sem, pair_sem,
+    ) = refs[2 * inputs :]
+    lines = count // 4
+    me, line, side, core = own_place()
+    half = lax.axis_index("fsdp")
+    partner = place_of(line, side, 1 - core)
+    across = place_of(line, 1 - side, core)
+    rows = own_ref.shape[0] // pieces
+
+    barrier = pltpu.get_barrier_semaphore()
+
+    def enter(step, carried):
+        pl.semaphore_signal(
+            barrier, inc=1, device_id={"ctx": lax.rem(me + step, count)}, device_id_type=MESH_ID
+        )
+        return carried
+
+    lax.fori_loop(1, count, enter, 0)
+    pl.semaphore_signal(barrier, inc=1, device_id={"fsdp": 1 - half}, device_id_type=MESH_ID)
+    pl.semaphore_wait(barrier, count)
+
+    moves = []
+    for source, target, (parts, kind) in zip(sources, targets, shared):
+        wide = target.shape[2] // parts
+        for part in range(parts):
+            def block(goal, source=source, part=part, kind=kind, wide=wide, parts=parts):
+                if kind == "same":
+                    return source
+                if kind == "blocks":
+                    return source.at[goal]
+                first = part * (source.shape[1] // parts) + goal * wide
+                return source.at[:, pl.ds(pl.multiple_of(first, 128), wide)]
+
+            def place(sender, side_of, target=target, part=part, wide=wide, parts=parts):
+                at = target.at[sender * 2 + side_of]
+                return at if parts == 1 else at.at[:, pl.ds(part * wide, wide)]
+
+            moves.append((block, place))
+
+    def origin(step):
+        return lax.rem(me + count - step, count)
+
+    def give(step, m):
+        goal = lax.rem(me + step, count)
+        block, place = moves[m]
+        return remote(block(goal), place(me, half), give_sem.at[step, m], take_sem.at[step, m], {"ctx": goal})
+
+    def taken(step, m):
+        at = moves[m][1](origin(step), half)
+        return remote(at, at, give_sem.at[step, m], take_sem.at[step, m], {"ctx": origin(step)})
+
+    def hand(step, m, side_of):
+        at = moves[m][1](origin(step), side_of)
+        return remote(at, at, pass_sem.at[step, m], passed_sem.at[step, m], {"fsdp": 1 - half})
+
+    def hand_own(m):
+        block, place = moves[m]
+        return remote(block(me), place(me, half), pass_sem.at[0, m], passed_sem.at[0, m], {"fsdp": 1 - half})
+
+    def stay(m):
+        block, place = moves[m]
+        return pltpu.make_async_copy(block(me), place(me, half), stay_sem.at[m])
+
+    def each_step(first, last, body):
+        def step_body(step, carried):
+            for m in range(len(moves)):
+                body(step, m)
+            return carried
+
+        lax.fori_loop(first, last, step_body, 0)
+
+    down_stay = pltpu.make_async_copy(down_ref, down_out.at[half], stay_sem.at[len(moves)])
+
+    def down_pair(side_of):
+        return remote(down_ref, down_out.at[side_of], pair_sem.at[0], pair_sem.at[1], {"fsdp": 1 - half})
+
+    def part(block, k):
+        return out_ref.at[block, pl.ds(pl.multiple_of(k * rows, rows), rows), :]
+
+    def mine(k):
+        return own_ref.at[pl.ds(pl.multiple_of(k * rows, rows), rows), :]
+
+    def to_up(source, block, slot, k):
+        return remote(source, part(block, k), up_sem.at[slot, k], recv_sem.at[block, k], {"ctx": me + 4})
+
+    def to_down(source, block, slot, k):
+        return remote(source, part(block, k), down_sem.at[slot, k], recv_sem.at[block, k], {"ctx": me - 4})
+
+    def to_across(source, block, k):
+        return remote(
+            source, part(block, k), across_sem.at[block // 4, k], recv_sem.at[block, k], {"ctx": across}
+        )
+
+    def to_partner(source, block, k):
+        return remote(
+            source, part(block, k), chip_sem.at[block // 2, k], recv_sem.at[block, k], {"ctx": partner}
+        )
+
+    def arrived(block, k):
+        to_partner(part(block, k), block, k).wait_recv()
+
+    def each_piece(body):
+        def step(k, carried):
+            body(k)
+            return carried
+
+        lax.fori_loop(0, pieces, step, 0)
+
+    keep = pltpu.make_async_copy(own_ref, out_ref.at[me], keep_sem)
+
+    def first(k):
+        @pl.when(line < lines - 1)
+        def up():
+            to_up(mine(k), me, 0, k).start()
+
+        @pl.when(line > 0)
+        def down():
+            to_down(mine(k), me, 0, k).start()
+
+        to_across(mine(k), me, k).start()
+        to_partner(mine(k), me, k).start()
+
+    each_piece(first)
+    each_step(1, count, lambda step, m: give(step, m).start())
+    down_pair(half).start()
+    for m in range(len(moves)):
+        hand_own(m).start()
+    keep.start()
+    down_stay.start()
+    for m in range(len(moves)):
+        stay(m).start()
+
+    def pass_on(step, m):
+        taken(step, m).wait_recv()
+        hand(step, m, half).start()
+
+    for hops in range(1, lines):
+        def relay(k, hops=hops):
+            @pl.when(line >= hops)
+            def from_below():
+                block = me - 4 * hops
+                arrived(block, k)
+                if hops < lines - 1:
+                    @pl.when(line < lines - 1)
+                    def up():
+                        to_up(part(block, k), block, hops, k).start()
+
+                to_across(part(block, k), block, k).start()
+                to_partner(part(block, k), block, k).start()
+
+            @pl.when(line < lines - hops)
+            def from_above():
+                block = me + 4 * hops
+                arrived(block, k)
+                if hops < lines - 1:
+                    @pl.when(line > 0)
+                    def down():
+                        to_down(part(block, k), block, hops, k).start()
+
+                to_across(part(block, k), block, k).start()
+                to_partner(part(block, k), block, k).start()
+
+        each_piece(relay)
+        each_step(
+            1 + (hops - 1) * (count - 1) // (lines - 1), 1 + hops * (count - 1) // (lines - 1), pass_on
+        )
+
+    def hand_over(block):
+        def one(k):
+            arrived(block, k)
+            to_partner(part(block, k), block, k).start()
+
+        each_piece(one)
+
+    hand_over(across)
+    for hops in range(1, lines):
+        @pl.when(line >= hops)
+        def from_below(hops=hops):
+            hand_over(across - 4 * hops)
+
+        @pl.when(line < lines - hops)
+        def from_above(hops=hops):
+            hand_over(across + 4 * hops)
+
+    def settle(index, carried):
+        def one(k):
+            arrived(index * 2 + 1 - core, k)
+            to_partner(part(me, k), index * 2 + core, k).wait_send()
+
+        each_piece(one)
+        return carried
+
+    lax.fori_loop(0, count // 2, settle, 0)
+
+    def settle_across(index, carried):
+        each_piece(lambda k: to_across(part(me, k), index * 4, k).wait_send())
+        return carried
+
+    lax.fori_loop(0, lines, settle_across, 0)
+    for hops in range(lines - 1):
+        @pl.when((line >= hops) & (line < lines - 1))
+        def up(hops=hops):
+            each_piece(lambda k: to_up(part(me, k), me, hops, k).wait_send())
+
+        @pl.when((line < lines - hops) & (line > 0))
+        def down(hops=hops):
+            each_piece(lambda k: to_down(part(me, k), me, hops, k).wait_send())
+
+    each_step(0, count, lambda step, m: hand(step, m, 1 - half).wait_recv())
+    each_step(1, count, lambda step, m: hand(step, m, half).wait_send())
+    each_step(1, count, lambda step, m: give(step, m).wait_send())
+    for m in range(len(moves)):
+        hand_own(m).wait_send()
+        stay(m).wait()
+    down_pair(1 - half).wait_recv()
+    down_pair(half).wait_send()
+    down_stay.wait()
+    keep.wait()
+
+
+def begin(own, w_qkv, w_up, w_down, vectors, pieces=2):
+    count = lax.axis_size("ctx")
+    lines = count // 4
+    rows, width = own.shape
+    owned = w_qkv.shape[0]
+    qkv_cols = w_qkv.shape[1] // count
+    up_cols = w_up.shape[1] // count
+    if qkv_cols % 384 == 0:
+        shared = [(3, "columns")]
+    else:
+        w_qkv = w_qkv.reshape(owned, 3, count, -1).transpose(2, 0, 1, 3).reshape(count, owned, qkv_cols)
+        shared = [(1, "blocks")]
+    shared += [(1, "columns"), (1, "same")]
+    moves = sum(parts for parts, _ in shared)
+    in_vmem = pl.BlockSpec(memory_space=pltpu.VMEM)
+    anywhere = pl.BlockSpec(memory_space=pl.ANY)
+    rows_all, qkv, up, vectors_all, down = pl.pallas_call(
+        functools.partial(begin_kernel, count, pieces, tuple(shared)),
+        out_shape=[
+            jax.ShapeDtypeStruct((count, rows, width), own.dtype),
+            jax.ShapeDtypeStruct((count * 2, owned, qkv_cols), BF16),
+            jax.ShapeDtypeStruct((count * 2, owned, up_cols), BF16),
+            jax.ShapeDtypeStruct((count * 2, *vectors.shape), F32),
+            jax.ShapeDtypeStruct((2, *w_down.shape), BF16),
+        ],
+        in_specs=[in_vmem] * 5,
+        out_specs=[anywhere] * 5,
+        scratch_shapes=[
+            pltpu.SemaphoreType.DMA,
+            pltpu.SemaphoreType.DMA((lines, pieces)),
+            pltpu.SemaphoreType.DMA((lines, pieces)),
+            pltpu.SemaphoreType.DMA((lines, pieces)),
+            pltpu.SemaphoreType.DMA((count // 2, pieces)),
+            pltpu.SemaphoreType.DMA((count, pieces)),
+            pltpu.SemaphoreType.DMA((count, moves)),
+            pltpu.SemaphoreType.DMA((count, moves)),
+            pltpu.SemaphoreType.DMA((count, moves)),
+            pltpu.SemaphoreType.DMA((count, moves)),
+            pltpu.SemaphoreType.DMA((moves + 1,)),
+            pltpu.SemaphoreType.DMA((2,)),
+        ],
+        compiler_params=pltpu.CompilerParams(collective_id=3, has_side_effects=True),
+        cost_estimate=pl.CostEstimate(flops=0, bytes_accessed=BUSY, transcendentals=0),
+        name="begin",
+    )(own, w_qkv, w_up, vectors, w_down)
+    return (
+        rows_all.reshape(count * rows, width),
+        qkv.reshape(-1, qkv_cols),
+        up.reshape(-1, up_cols),
+        down.reshape(-1, width),
+        vectors_all.reshape(count * 2, -1),
+    )
+
+
+def project_kernel(rows_ref, gain_ref, shift_ref, weight_ref, bias_ref, normed_ref, out_ref):
+    unit, _ = norm_parts(rows_ref[...].astype(F32))
+    normed = (unit * gain_ref[...] + shift_ref[...]).astype(BF16)
+    normed_ref[...] = normed
+    projected = jnp.dot(normed, weight_ref[...], preferred_element_type=F32)
+    out_ref[...] = (projected + bias_ref[...]).astype(BF16)
+
+
+def project(rows_in, gain, shift, weight, bias, block=256):
+    total, width = rows_in.shape
+    columns = weight.shape[1]
+    row = pl.BlockSpec((1, width), lambda i: (0, 0))
+    return pl.pallas_call(
+        project_kernel,
+        grid=(total // block,),
+        in_specs=[
+            pl.BlockSpec((block, width), lambda i: (i, 0)),
+            row,
+            row,
+            pl.BlockSpec((width, columns), lambda i: (0, 0)),
+            pl.BlockSpec((1, columns), lambda i: (0, 0)),
+        ],
+        out_specs=[
+            pl.BlockSpec((block, width), lambda i: (i, 0)),
+            pl.BlockSpec((block, columns), lambda i: (i, 0)),
+        ],
+        out_shape=[
+            jax.ShapeDtypeStruct((total, width), BF16),
+            jax.ShapeDtypeStruct((total, columns), BF16),
+        ],
+        cost_estimate=pl.CostEstimate(
+            flops=2 * total * width * columns, bytes_accessed=6 * total * width, transcendentals=0
+        ),
+        name="project",
+    )(rows_in, gain[None], shift[None], weight, bias[None])
 
 
 def sum_kernel(
@@ -611,18 +917,14 @@
         compiler_params=pltpu.CompilerParams(
             collective_id=1, has_side_effects=True, vmem_limit_bytes=63 * 2**20
         ),
-        cost_estimate=pl.CostEstimate(flops=0, bytes_accessed=count * rows * width * 16, transcendentals=0),
+        cost_estimate=pl.CostEstimate(flops=0, bytes_accessed=BUSY, transcendentals=0),
         name="sum_rows",
     )(partial.astype(BF16).reshape(count, rows, width))
 
 
-def columns_of_rows(weight, parts):
-    count = lax.axis_size("ctx")
-    rows = weight.shape[0]
-    split = weight.reshape(rows, parts, count, -1).transpose(2, 0, 1, 3)
-    mine = lax.all_to_all(split, "ctx", split_axis=0, concat_axis=0)
-    both = pair_gather(mine, 1)
-    return both.reshape(count * both.shape[1] * rows, parts, -1)
+def weight_grad(rows_in, grads):
+    terms = lax.dot_general(rows_in, grads, TN, preferred_element_type=F32).astype(BF16)
+    return lax.optimization_barrier(terms)
 
 
 def rows_of_columns(grad):
@@ -702,7 +1004,11 @@
     vectors = [ln1_gain, ln1_bias, b_out, ln2_gain, ln2_bias, b_down, bias_q, bias_v, b_up]
     devices = count * lax.axis_size("fsdp")
     own_vectors = jnp.concatenate([vector.astype(F32) for vector in vectors])
-    everywhere = exchange(jnp.broadcast_to(own_vectors, (devices, own_vectors.shape[0])))
+    tiles = -(-own_vectors.shape[0] // 1024) * 8
+    own_vectors = jnp.pad(own_vectors, (0, tiles * 128 - own_vectors.shape[0])).reshape(tiles, 128)
+    tokens_all, w_qkv_own, w_up_own, w_down_own, everywhere = begin(
+        tokens[0], w_qkv, w_up, w_down, own_vectors
+    )
     at = 0
     whole_vectors = []
     for vector in vectors:
@@ -716,24 +1022,19 @@
     ff_cols = whole_vectors[8].shape[0] // count
     b_up_own = lax.dynamic_slice_in_dim(whole_vectors[8], rank * ff_cols, ff_cols)
 
-    w_qkv_own = columns_of_rows(w_qkv, 3)
-    w_qkv_head = widen(w_qkv_own, share).reshape(width, -1)
-    w_qkv_own = w_qkv_own.reshape(width, -1)
-    w_up_own = columns_of_rows(w_up, 1).reshape(width, -1)
-    w_down_own = pair_gather(w_down, 0).reshape(-1, width)
+    w_qkv_head = widen(w_qkv_own.reshape(width, 3, -1), share).reshape(width, -1)
     w_out_all = lax.all_gather(w_out, BOTH, axis=0, tiled=True)
 
     inputs = tokens[0].astype(F32)
     unit_one, rate_one = norm_parts(inputs)
-    normed = (unit_one * gain_one + shift_one).astype(BF16)
-    normed_all = gather_rows(normed)
     grad_out = cotangent[0]
-    grad_out_all = gather_beside(grad_out)
-
-    projected = jnp.dot(normed_all, w_qkv_head, preferred_element_type=F32)
+    tokens_all, cotangent_rows = lax.optimization_barrier((tokens_all, grad_out))
+    grad_out_all = gather_beside(cotangent_rows)
+
     head_width = heads * HEAD_DIM
     shift = jnp.concatenate([bias_q_own, jnp.zeros(head_width, F32), bias_v_own])
-    projected = to_sequence((projected + shift).astype(BF16), count)
+    normed_all, projected = project(tokens_all, gain_one, shift_one, w_qkv_head, shift)
+    projected = to_sequence(projected, count)
     queries, keys, values = (
         projected[:, part * head_width : (part + 1) * head_width] for part in range(3)
     )
@@ -754,26 +1055,20 @@
     grad_normed_two = sum_rows(
         lax.dot_general(grad_hidden, w_up_own, NT, preferred_element_type=F32)
     )
-    branch = sum_beside(jnp.dot(activated, w_down_own, preferred_element_type=F32))
-    outputs = (middle + branch + b_down_all).astype(BF16)
-
-    grad_w_down = pair_sum(
-        lax.dot_general(activated, grad_out_all, TN, preferred_element_type=F32)
-    )
-    grad_w_up = rows_of_columns(
-        lax.dot_general(normed_two_all, grad_hidden, TN, preferred_element_type=F32)[:, None]
-    )
+    grad_w_down = pair_sum(weight_grad(activated, grad_out_all))
+    grad_w_up = weight_grad(normed_two_all, grad_hidden)
+    grad_w_up = rows_of_columns(grad_w_up[:, None])
 
     grad_middle = grad_out.astype(F32) + norm_back(unit_two, rate_two, gain_two, grad_normed_two)
     grad_branch = grad_middle.astype(BF16)
     grad_attended = lax.dot_general(
         grad_branch, w_out_all, NT, preferred_element_type=F32
     ).astype(BF16)
+    grad_attended, late = lax.optimization_barrier((grad_attended, activated))
     grad_heads = to_sequence(widen(rows_to_columns(grad_attended), share), count)
     grad_branch_all = gather_beside(grad_branch)
-    grad_w_out = pair_sum(
-        lax.dot_general(attended_own, grad_branch_all, TN, preferred_element_type=F32)
-    )
+    branch = sum_beside(jnp.dot(late, w_down_own, preferred_element_type=F32))
+    grad_w_out = pair_sum(weight_grad(attended_own, grad_branch_all))
 
     delta = (grad_heads.astype(F32) * attended_full).reshape(seq_len, heads, HEAD_DIM)
     delta = jnp.sum(delta, axis=-1).T
@@ -785,11 +1080,10 @@
     )
     column_sums = jnp.sum(grad_qkv.astype(F32), axis=0)
     grad_normed = sum_rows(lax.dot_general(grad_qkv, w_qkv_own, NT, preferred_element_type=F32))
-    grad_w_qkv = rows_of_columns(
-        lax.dot_general(normed_all, grad_qkv, TN, preferred_element_type=F32).reshape(
-            width, 3, own_cols
-        )
-    )
+    grad_w_qkv = weight_grad(normed_all, grad_qkv)
+    grad_w_qkv = rows_of_columns(grad_w_qkv.reshape(width, 3, own_cols))
+    branch, middle, grad_normed = lax.optimization_barrier((branch, middle, grad_normed))
+    outputs = (middle + branch + b_down_all).astype(BF16)
     grad_inputs = grad_middle + norm_back(unit_one, rate_one, gain_one, grad_normed)
 
     pair = devices // count

time: 738 us -> 644 us (0.87)
  waiting for transfers between devices: 130 us -> 47.9 us
  Pallas kernels: 334 us -> 370 us
  local copies, waits for them, and re-layouts: 67.9 us -> 38.3 us
  starting transfers between devices: 49 us -> 38.9 us
    pallas_call x0 -> x2, Pallas kernels: none -> 143 us  [the longest x1 130 us: begin(): pl.pallas_call(functools.partial(begin_kernel, count, pieces, tuple(share...]
    pallas_call x2 -> x1, Pallas kernels: 155 us -> 58.4 us  [gather_rows(): pl.pallas_call(functools.partial(gather_kernel, count, pieces), out_shape...]
    reduce_scatter x1, waiting for transfers between devices: 32 us -> 0.01 us  [sum_beside(): lax.psum_scatter(partial.astype(BF16), 'ctx', scatter_dimension=0, tiled=...]
    dot_general x4 -> x0, local copies, waits for them, and re-layouts: 28.5 us -> none  [the longest x2 14 us: on_device(): lax.dot_general(normed_all, grad_qkv, TN, preferred_element_type=F32)]
    all_to_all x2 -> x0, waiting for transfers between devices: 25.7 us -> none  [columns_of_rows(): mine = lax.all_to_all(split, 'ctx', split_axis=0, concat_axis=0)]
    ppermute x7 -> x4, waiting for transfers between devices: 23.2 us -> 6.28 us  [from_pair(): return lax.ppermute(mine, 'fsdp', [(0, 1), (1, 0)])]
    all_to_all x2, waiting for transfers between devices: 26.4 us -> 10.4 us  [rows_of_columns(): mine = lax.all_to_all(summed, 'ctx', split_axis=0, concat_axis=0)]
    all_to_all x1, waiting for transfers between devices: 6.8 us -> 22.7 us  [columns_to_rows(): lax.all_to_all(slice_in.reshape(count, rows, -1), 'ctx', split_axis=0, co...]
  transfers between devices with their start and end apart: 19 -> 13, of which waited for: 8 -> 5; matrix products, arithmetic and copies ran while one was open for 26% -> 18% of each run, Pallas kernels for 46% -> 50%
where the time goes in v3:
time: 644 us; the launch traced here: 639 us
  Pallas kernels  370 us (57%)
  matrix products  96.2 us (15%)
  waiting for transfers between devices  47.9 us (7%)
  starting transfers between devices  38.9 us (6%)
  local copies, waits for them, and re-layouts  38.3 us (6%)
  other arithmetic  33.6 us (5%)
  between operations  14.8 us (2%)
    pallas_call x1, Pallas kernels, begin(): pl.pallas_call(functools.partial(begin_kernel, count, pieces, tuple(share...  130 us
    pallas_call x2, Pallas kernels, sum_rows(): pl.pallas_call(functools.partial(sum_kernel, count, pieces), out_shape=ja...  128 us
    pallas_call x1, Pallas kernels, gather_rows(): pl.pallas_call(functools.partial(gather_kernel, count, pieces), out_shape...  58.4 us
    dot_general x4, matrix products, weight_grad(): lax.dot_general(rows_in, grads, TN, preferred_element_type=F32).astype(BF16)  33.5 us
    all_to_all x1, waiting for transfers between devices, columns_to_rows(): lax.all_to_all(slice_in.reshape(count, rows, -1), 'ctx', split_axis=0, co...  22.7 us
    all_to_all x2, starting transfers between devices, rows_of_columns(): mine = lax.all_to_all(summed, 'ctx', split_axis=0, concat_axis=0)  20.3 us
    pallas_call x1, Pallas kernels, attend_back(): pl.pallas_call(functools.partial(attend_back_kernel, rows, heads), grid=(...  20.2 us
    pallas_call x1, Pallas kernels, attend(): pl.pallas_call(functools.partial(attend_kernel, rows, heads), grid=(seq_l...  19.8 us
  transfers between devices with their start and end apart: 13, of which 5 were waited for; matrix products, arithmetic and copies ran while one was open for 18% of the time, Pallas kernels for 50%

profile of v3, /device:TPU:0, one launch (start us, length us, event | category | flops | bytes accessed | tf_op | source)
XLA Modules:
  0.0 639.3 jit_solution(13115995836963699661)
XLA Ops:
  8.0 6.1 concatenate.23
  14.7 129.9 %begin.1 = (bf16[16,128,2048]{2,1,0:T(8,128)(2,1)}, bf16[32,64,384]{2,1,0:T(8,128)(2,1)}, bf16[32,64,512]{2,1,0:T(8,128)(2,1)}, f32[32,8,128]{2,1,0:T(8,128)}, bf16[2,256,2048]{2,1,0:T(8,128)(2,1)}) custom-call(bf16[128,2048]{1,0:T(8,128)(2,1)} %bitcast.168, bf16[64,6144]{1,0:T(8,128)(2,1)} %refs_1_.1, bf16[64,8192]{1,0:T(8,128)(2,1)} %refs_2_.1, ...), custom_call_target="tpu_custom_call" | custom-call | bytes 167772160 | tf_op jit(solution)/shard_map/begin/pallas_call | solution.py:665
  145.0 0.9 copy.143
  146.0 0.7 broadcast_in_dim_reshape.4.gain_ref
  148.8 12.9 %project.1 = (bf16[2048,2048]{1,0:T(8,128)(2,1)}, bf16[2048,384]{1,0:T(8,128)(2,1)}) custom-call(bf16[2048,2048]{1,0:T(8,128)(2,1)} %bitcast.216, f32[1,2048]{1,0:T(1,128)} %broadcast_in_dim_reshape.4.gain_ref, f32[1,2048]{1,0:T(1,128)} %broadcast_in_dim_reshape.5.shift_ref, bf16[2048,384]{1,0:T(8,128)(2,1)} %bitcast.221, f32[1,384]{1,0:T(1,128)} %broadcast_in_dim.68.bias_ref), custom_call_target="tpu_custom_call" | custom-call | flops 3221225472 | bytes 25165824 | tf_op jit(solution)/shard_map/project/pallas_call | solution.py:715
  161.7 1.5 slice_bitcast_fusion.1
  164.0 1.2 fusion.24
  165.3 19.8 %attend.1 = (f32[2048,128]{1,0:T(8,128)}, f32[2,2048]{1,0:T(2,128)}) custom-call(s32[8]{0:T(128)} %and_select_fusion.low_ref, f32[2]{0:T(128)} %multiply_power_fusion.slope_ref, s32[1,2048]{1,0:T(1,128)} %bitcast.212, bf16[2048,128]{1,0:T(8,128)(2,1)} %get-tuple-element.71.q_ref, bf16[2048,128]{1,0:T(8,128)(2,1)} %get-tuple-element.70.k_ref, ...), custom_call_target="tpu_custom_call" | custom-call | bytes 55924052 | tf_op jit(solution)/shard_map/attend/pallas_call | solution.py:156
  185.1 1.3 convert_element_type.151
  186.4 0.9 pad_maximum_fusion.2
  187.3 4.8 all-to-all-start
  192.5 22.7 %all-to-all-done = bf16[16,128,128]{2,1,0:T(8,128)(2,1)S(1)} async-done(((bf16[16,128,128]{2,1,0:T(8,128)(2,1)}), bf16[16,128,128]{2,1,0:T(8,128)(2,1)S(1)}, u32[]{:S(2)}, u32[]{:S(2)}) %all-to-all-start) | async-done | bytes 524320 | tf_op jit(solution)/shard_map/all_to_all | solution.py:955
  215.5 4.7 fusion.32
  220.5 0.7 copy-done
  221.2 1.0 add_convert_fusion.2.own_ref
  222.3 58.4 %gather_rows.1 = bf16[16,128,2048]{2,1,0:T(8,128)(2,1)} custom-call(bf16[128,2048]{1,0:T(8,128)(2,1)} %add_convert_fusion.2.own_ref), custom_call_target="tpu_custom_call" | custom-call | bytes 167772160 | tf_op jit(solution)/shard_map/gather_rows/pallas_call | solution.py:403
  280.7 10.4 %fusion.34 = f32[2048,512]{1,0:T(8,128)} fusion(bf16[2048,2048]{1,0:T(8,128)(2,1)} %bitcast.171, bf16[2048,512]{1,0:T(8,128)(2,1)} %bitcast.219), kind=kOutput, calls=%fused_computation.128 | convolution fusion | flops 4294967296 | bytes 14680064 | tf_op jit(solution)/shard_map/dot_general | solution.py:1049
  291.2 17.7 %convert_reduce_fusion = (f32[512]{0:T(512)S(1)}, bf16[2048,512]{1,0:T(8,128)(2,1)S(1)}, f32[2048,512]{1,0:T(8,128)S(1)}) fusion(f32[2048,512]{1,0:T(8,128)} %fusion.34, f32[512]{0:T(512)S(1)} %dynamic_slice.39, bf16[2048,2048]{1,0:T(8,128)(2,1)} %all-gather.6.cloned.1.call-done, bf16[512,2048]{1,0:T(8,128)(2,1)} %bitcast.217), kind=kOutput, calls=%fused_computation.5 | convolution fusion | flops 4373609984 | bytes 20975616 | tf_op jit(solution)/shard_map/dot_general | solution.py:1053
  308.9 2.5 multiply_convert_fusion
  311.7 6.9 %convolution_convert_fusion.2 = bf16[2048,2048]{1,0:T(8,128)(2,1)} fusion(bf16[2048,512]{1,0:T(8,128)(2,1)S(1)} %get-tuple-element.65, bf16[2048,512]{1,0:T(8,128)(2,1)S(1)} %bitcast.220), kind=kOutput, calls=%fused_computation.2 | convolution fusion | flops 4299161600 | bytes 12582912 | tf_op jit(solution)/shard_map/dot_general | solution.py:1056
  318.6 51.7 %sum_rows.2 = f32[128,2048]{1,0:T(8,128)} custom-call(bf16[16,128,2048]{2,1,0:T(8,128)(2,1)} %bitcast.170), custom_call_target="tpu_custom_call" | custom-call | bytes 167772160 | tf_op jit(solution)/shard_map/sum_rows/pallas_call | solution.py:899
  370.3 2.0 multiply_reduce_fusion
  372.3 3.3 convert_reduce_fusion.4
  375.6 6.5 %convolution_convert_fusion.7 = bf16[128,2048]{1,0:T(8,128)(2,1)S(1)} fusion(bf16[128,2048]{1,0:T(8,128)(2,1)S(1)} %get-tuple-element.62, bf16[2048,2048]{1,0:T(8,128)(2,1)} %all-gather.4.cloned.1.call-done), kind=kOutput, calls=%fused_computation.28 | convolution fusion | flops 1074003968 | bytes 9437184 | tf_op jit(solution)/shard_map/dot_general | solution.py:1064
  382.2 6.7 %convolution_convert_fusion.1 = bf16[2048,2048]{1,0:T(8,128)(2,1)} fusion(bf16[2048,512]{1,0:T(8,128)(2,1)S(1)} %copy-done.16, bf16[512,2048]{1,0:T(8,128)(2,1)S(1)} %bitcast.218), kind=kOutput, calls=%fused_computation.1 | convolution fusion | flops 4299161600 | bytes 12582912 | tf_op jit(solution)/shard_map/dot_general | solution.py:1070
  390.3 0.9 bitcast_bitcast_fusion
  391.2 4.5 all-to-all-start.1
  395.8 9.5 %convolution_convert_fusion.4 = bf16[2048,512]{1,0:T(8,128)(2,1)S(1)} fusion(bf16[2048,2048]{1,0:T(8,128)(2,1)} %bitcast.172, bf16[2048,512]{1,0:T(8,128)(2,1)} %copy-done.21), kind=kOutput, calls=%fused_computation.23 | convolution fusion | flops 4296015872 | bytes 12582912 | tf_op jit(solution)/shard_map/dot_general | solution.py:926
  405.3 1.3 copy-done.12
  406.6 1.0 dynamic-slice_bitcast_fusion.1
  407.7 2.3 all-to-all-done.1
  411.3 20.2 %attend_back.1 = (bf16[2048,128]{1,0:T(8,128)(2,1)}, bf16[2048,128]{1,0:T(8,128)(2,1)}, bf16[2048,128]{1,0:T(8,128)(2,1)}) custom-call(s32[8]{0:T(128)} %and_select_fusion.low_ref, f32[2]{0:T(128)} %multiply_power_fusion.slope_ref, s32[1,2048]{1,0:T(1,128)} %bitcast.213, f32[2,2048]{1,0:T(2,128)} %get-tuple-element.44.total_ref, f32[2,2048]{1,0:T(2,128)} %bitcast.214, ...), custom_call_target="tpu_custom_call" | custom-call | bytes 55924052 | tf_op jit(solution)/shard_map/attend_back/pallas_call | solution.py:178
  431.6 1.1 fusion.25
  432.7 1.1 fusion.26
  433.8 1.1 fusion.27
  435.1 0.7 copy-done.14
  435.9 9.2 %convolution_convert_fusion.5 = bf16[2048,384]{1,0:T(8,128)(2,1)} fusion(bf16[2048,2048]{1,0:T(8,128)(2,1)} %get-tuple-element.52, bf16[2048,128]{1,0:T(8,128)(2,1)S(1)} %bitcast.190, bf16[2048,128]{1,0:T(8,128)(2,1)S(1)} %bitcast.187, bf16[2048,128]{1,0:T(8,128)(2,1)S(1)} %bitcast.184), kind=kOutput, calls=%fused_computation.24 | convolution fusion | flops 3226730496 | bytes 11534336 | tf_op jit(solution)/shard_map/dot_general | solution.py:926
  445.1 4.1 reshape_reshape.11
  449.3 1.7 constant_dynamic-slice_fusion.1
  451.0 1.1 copy.141
  452.1 2.5 fusion.7
  454.6 4.2 all-to-all-start.4
  458.9 9.9 %convolution_convert_fusion.3 = bf16[512,2048]{1,0:T(8,128)(2,1)} fusion(bf16[2048,512]{1,0:T(8,128)(2,1)} %multiply_convert_fusion, bf16[2048,2048]{1,0:T(8,128)(2,1)} %all-gather.6.cloned.1.call-done), kind=kOutput, calls=%fused_computation.22 | convolution fusion | flops 4296015872 | bytes 12582912 | tf_op jit(solution)/shard_map/dot_general | solution.py:926
  468.8 2.4 dynamic-slice_bitcast_fusion
  471.2 2.0 collective-permute-start.3
  473.5 1.6 convert_reduce_fusion.1
  475.4 2.3 fusion.8
  477.7 10.4 %all-to-all-done.4 = bf16[16,64,1,512]{3,1,2,0:T(8,128)(2,1)S(1)} async-done(((bf16[16,64,1,512]{3,1,2,0:T(8,128)(2,1)}), bf16[16,64,1,512]{3,1,2,0:T(8,128)(2,1)S(1)}, u32[]{:S(2)}, u32[]{:S(2)}) %all-to-all-start.4) | async-done | bytes 1048608 | tf_op jit(solution)/shard_map/all_to_all | solution.py:936
  488.1 16.1 %all-to-all-start.3 = ((bf16[16,64,3,128]{3,1,2,0:T(8,128)(2,1)}), bf16[16,64,3,128]{3,1,2,0:T(8,128)(2,1)}, u32[]{:S(2)}, u32[]{:S(2)}) async-start(bf16[16,64,3,128]{3,1,2,0:T(8,128)(2,1)} %fusion.8), calls=%async_computation.4 | async-start | bytes 1572864 | tf_op jit(solution)/shard_map/all_to_all | solution.py:936
  504.2 9.6 %convolution_convert_fusion = bf16[2048,2048]{1,0:T(8,128)(2,1)} fusion(bf16[2048,384]{1,0:T(8,128)(2,1)} %bitcast.222, bf16[2048,128]{1,0:T(8,128)(2,1)} %bitcast.192, bf16[2048,128]{1,0:T(8,128)(2,1)} %bitcast.189, bf16[2048,128]{1,0:T(8,128)(2,1)S(1)} %bitcast.186), kind=kOutput, calls=%fused_computation | convolution fusion | flops 3230138368 | bytes 11534336 | tf_op jit(solution)/shard_map/dot_general | solution.py:1082
  513.8 76.6 %sum_rows.3 = f32[128,2048]{1,0:T(8,128)} custom-call(bf16[16,128,2048]{2,1,0:T(8,128)(2,1)} %bitcast.169), custom_call_target="tpu_custom_call" | custom-call | bytes 167772160 | tf_op jit(solution)/shard_map/sum_rows/pallas_call | solution.py:899
  590.5 3.3 convert_add_fusion
  594.1 1.5 copy.130
  595.6 1.3 convert_bitcast_fusion.1
  596.9 0.9 copy.116
  597.9 1.6 copy.140
  599.5 2.3 convert_element_type.159
  603.3 6.7 %all-to-all-start.2 = ((f32[32,8,128]{2,1,0:T(8,128)}), f32[32,8,128]{2,1,0:T(8,128)S(1)}, u32[]{:S(2)}, u32[]{:S(2)}) async-start(f32[32,8,128]{2,1,0:T(8,128)} %bitcast.85), calls=%async_computation.3 | async-start | bytes 262144 | tf_op jit(solution)/shard_map/all_to_all | solution.py:224
  610.1 2.7 fusion.18
  612.8 0.9 fusion.21
  613.8 4.9 all-to-all-done.2
  618.7 4.8 convolution_convert_fusion.6
  625.2 6.3 collective-permute-done.1
  631.4 0.8 convert_add_fusion.4
  (139 shorter events, 13.1 us)
Async XLA Ops:
  7.2 137.4 %copy-start.20 = (s32[1,8]{1,0:T(1,128)S(1)}, s32[1,8]{1,0:T(1,128)}, u32[]{:S(2)}) copy-start(s32[1,8]{1,0:T(1,128)} %param.17) | copy-start | bytes 100
  7.2 208.3 %all-gather.4.cloned.1.call-start = ((), (), s32[]{:S(2)}) async-start(), calls=%async_computation.6 | async-start | bytes 8650752 | tf_op jit(solution)/shard_map/all_gather | solution.py:1026
  7.9 283.2 %all-gather.6.cloned.1.call-start = ((), (), s32[]{:S(2)}) async-start(), calls=%async_computation.7 | async-start | bytes 8912896 | tf_op jit(solution)/shard_map/all_gather | solution.py:201
  144.9 16.8 %copy-start.17 = (s32[2048]{0:T(1024)}, s32[2048]{0:T(1024)S(1)}, u32[]{:S(2)}) copy-start(s32[2048]{0:T(1024)S(1)} %select_reduce_fusion) | copy-start | bytes 24580
  165.3 50.2 %copy-start.2 = (bf16[1,128,2048]{2,1,0:T(8,128)(2,1)S(1)}, bf16[1,128,2048]{2,1,0:T(8,128)(2,1)}, u32[]{:S(2)}) copy-start(bf16[1,128,2048]{2,1,0:T(8,128)(2,1)} %param.16) | copy-start | bytes 1572868
  187.3 27.9 %all-to-all-start = ((bf16[16,128,128]{2,1,0:T(8,128)(2,1)}), bf16[16,128,128]{2,1,0:T(8,128)(2,1)S(1)}, u32[]{:S(2)}, u32[]{:S(2)}) async-start(bf16[16,128,128]{2,1,0:T(8,128)(2,1)} %bitcast.15), calls=%async_computation | async-start | bytes 1048576 | tf_op jit(solution)/shard_map/all_to_all | solution.py:955
  192.1 407.4 %reduce-scatter.2.cloned.1.call-start = ((), (), s32[]{:S(2)}) async-start(), calls=%async_computation.8 | async-start | bytes 8912896 | tf_op jit(solution)/shard_map/reduce_scatter | solution.py:205
  220.2 1.0 copy-start
  291.2 17.8 %copy-start.9 = (f32[2048,512]{1,0:T(8,128)S(1)}, f32[2048,512]{1,0:T(8,128)}, u32[]{:S(2)}) copy-start(f32[2048,512]{1,0:T(8,128)} %fusion.34) | copy-start | bytes 12582916
  308.9 2.6 copy-start.21
  308.9 2.8 copy-start.19
  375.6 6.5 %copy-start.5 = (bf16[128,2048]{1,0:T(8,128)(2,1)}, bf16[128,2048]{1,0:T(8,128)(2,1)S(1)}, u32[]{:S(2)}) copy-start(bf16[128,2048]{1,0:T(8,128)(2,1)S(1)} %get-tuple-element.62) | copy-start | bytes 1572868
  375.6 6.5 %copy-start.16 = (bf16[2048,512]{1,0:T(8,128)(2,1)S(1)}, bf16[2048,512]{1,0:T(8,128)(2,1)}, u32[]{:S(2)}) copy-start(bf16[2048,512]{1,0:T(8,128)(2,1)} %multiply_convert_fusion) | copy-start | bytes 6291460
  375.6 6.5 %copy-start.18 = (bf16[2,256,2048]{2,1,0:T(8,128)(2,1)S(1)}, bf16[2,256,2048]{2,1,0:T(8,128)(2,1)}, u32[]{:S(2)}) copy-start(bf16[2,256,2048]{2,1,0:T(8,128)(2,1)} %get-tuple-element.42) | copy-start | bytes 6291460
  388.9 229.8 %all-gather.8.cloned.1.call-start = ((), (), s32[]{:S(2)}) async-start(), calls=%async_computation.9 | async-start | bytes 8912896 | tf_op jit(solution)/shard_map/all_gather | solution.py:201
  391.2 18.8 %all-to-all-start.1 = ((bf16[16,128,128]{2,1,0:T(8,128)(2,1)}), bf16[16,128,128]{2,1,0:T(8,128)(2,1)S(1)}, u32[]{:S(2)}, u32[]{:S(2)}) async-start(bf16[16,128,128]{2,1,0:T(8,128)(2,1)} %bitcast_bitcast_fusion), calls=%async_computation.2 | async-start | bytes 1048576 | tf_op jit(solution)/shard_map/all_to_all | solution.py:948
  405.3 1.3 copy-start.12
  405.3 4.8 copy-start.10
  407.7 44.4 %collective-permute-start.2 = (bf16[16,64,1,512]{3,1,2,0:T(8,128)(2,1)}, bf16[16,64,1,512]{3,1,2,0:T(8,128)(2,1)}, u32[]{:S(2)}, u32[]{:S(2)}) collective-permute-start(bf16[16,64,1,512]{3,1,2,0:T(8,128)(2,1)} %dynamic-slice_bitcast_fusion.1), channel_id=1, source_target_pairs={{0,1},{1,0},{2,3},{3,2},{4,5},{5,4},{6,7},{7,6},{8,9},{9,8},{10,11... | collective-permute-start | bytes 3145736 | tf_op jit(solution)/shard_map/ppermute | solution.py:209
  410.2 1.2 copy-start.4
  435.0 0.8 copy-start.14
  435.0 0.9 copy-start.15
  449.3 2.8 copy-start.13
  452.1 23.3 %collective-permute-start = (bf16[16,64,3,128]{3,1,2,0:T(8,128)(2,1)}, bf16[16,64,3,128]{3,1,2,0:T(8,128)(2,1)}, u32[]{:S(2)}, u32[]{:S(2)}) collective-permute-start(bf16[16,64,3,128]{3,1,2,0:T(8,128)(2,1)} %bitcast.165), channel_id=1, source_target_pairs={{0,1},{1,0},{2,3},{3,2},{4,5},{5,4},{6,7},{7,6},{8,9},{9,8},{10,11... | collective-permute-start | bytes 2359304 | tf_op jit(solution)/shard_map/ppermute | solution.py:209
  454.6 33.5 %all-to-all-start.4 = ((bf16[16,64,1,512]{3,1,2,0:T(8,128)(2,1)}), bf16[16,64,1,512]{3,1,2,0:T(8,128)(2,1)S(1)}, u32[]{:S(2)}, u32[]{:S(2)}) async-start(bf16[16,64,1,512]{3,1,2,0:T(8,128)(2,1)} %fusion.7), calls=%async_computation.5 | async-start | bytes 2097152 | tf_op jit(solution)/shard_map/all_to_all | solution.py:936
  468.8 6.6 %copy-start.8 = (bf16[16,1,64,3,128]{4,3,2,1,0:T(4,128)(2,1)S(1)}, bf16[16,1,64,3,128]{4,3,2,1,0:T(4,128)(2,1)}, u32[]{:S(2)}) copy-start(bf16[16,1,64,3,128]{4,3,2,1,0:T(4,128)(2,1)} %get-tuple-element.67) | copy-start | bytes 2359300
  471.2 119.3 %collective-permute-start.3 = (bf16[256,2048]{1,0:T(8,128)(2,1)}, bf16[256,2048]{1,0:T(8,128)(2,1)}, u32[]{:S(2)}, u32[]{:S(2)}) collective-permute-start(bf16[256,2048]{1,0:T(8,128)(2,1)} %dynamic-slice_bitcast_fusion), channel_id=1, source_target_pairs={{0,1},{1,0},{2,3},{3,2},{4,5},{5,4},{6,7},{7,6},{8,9},{9,8},{10,11... | collective-permute-start | bytes 3145736 | tf_op jit(solution)/shard_map/ppermute | solution.py:209
  488.1 25.7 %copy-start.6 = (bf16[16,64,1,512]{3,1,2,0:T(8,128)(2,1)}, bf16[16,64,1,512]{3,1,2,0:T(8,128)(2,1)S(1)}, u32[]{:S(2)}) copy-start(bf16[16,64,1,512]{3,1,2,0:T(8,128)(2,1)S(1)} %all-to-all-done.4) | copy-start | bytes 3145732
  488.1 107.5 %all-to-all-start.3 = ((bf16[16,64,3,128]{3,1,2,0:T(8,128)(2,1)}), bf16[16,64,3,128]{3,1,2,0:T(8,128)(2,1)}, u32[]{:S(2)}, u32[]{:S(2)}) async-start(bf16[16,64,3,128]{3,1,2,0:T(8,128)(2,1)} %fusion.8), calls=%async_computation.4 | async-start | bytes 1572864 | tf_op jit(solution)/shard_map/all_to_all | solution.py:936
  590.4 3.4 copy-start.7
  596.9 4.8 copy-start.3
  599.5 13.3 %copy-start.1 = (f32[128,2048]{1,0:T(8,128)S(1)}, f32[128,2048]{1,0:T(8,128)}, u32[]{:S(2)}) copy-start(f32[128,2048]{1,0:T(8,128)} %copy-done) | copy-start | bytes 3145732
  603.3 15.4 %all-to-all-start.2 = ((f32[32,8,128]{2,1,0:T(8,128)}), f32[32,8,128]{2,1,0:T(8,128)S(1)}, u32[]{:S(2)}, u32[]{:S(2)}) async-start(f32[32,8,128]{2,1,0:T(8,128)} %bitcast.85), calls=%async_computation.3 | async-start | bytes 262144 | tf_op jit(solution)/shard_map/all_to_all | solution.py:224
  610.1 2.8 copy-start.11
  623.6 7.8 %collective-permute-start.1 = (bf16[64,2048]{1,0:T(8,128)(2,1)S(1)}, bf16[64,2048]{1,0:T(8,128)(2,1)S(1)}, u32[]{:S(2)}, u32[]{:S(2)}) collective-permute-start(bf16[64,2048]{1,0:T(8,128)(2,1)S(1)} %dynamic-slice_bitcast_fusion.2), channel_id=1, source_target_pairs={{0,1},{1,0},{2,3},{3,2},{4,5},{5,4},{6,7},{7,6},{8,9},{9,8},{10,11... | collective-permute-start | bytes 786440 | tf_op jit(solution)/shard_map/ppermute | solution.py:209
Sparse Core Ops, SparseCore 0:
  11.1 126.4 all-gather.3
  144.7 82.5 all-gather.5
  389.1 114.2 reduce-scatter.1
  505.4 103.4 all-gather.7

commit v4 on v3

--- a/solution.py
+++ b/solution.py
@@ -1,4 +1,5 @@
 import functools
+import math
 
 import jax
 import jax.numpy as jnp
@@ -16,10 +17,6 @@
 F32 = jnp.float32
 BF16 = jnp.bfloat16
 BUSY = 160 * 2**20
-
-
-def gelu_exact(pre_activation):
-    return jax.nn.gelu(pre_activation, approximate=False)
 
 
 def norm_parts(values):
@@ -203,18 +200,6 @@
 
 def sum_beside(partial):
     return lax.psum_scatter(partial.astype(BF16), "ctx", scatter_dimension=0, tiled=True).astype(F32)
-
-
-def from_pair(mine):
-    return lax.ppermute(mine, "fsdp", [(0, 1), (1, 0)])
-
-
-def pair_reduce(grad, axis):
-    here = lax.axis_index("fsdp")
-    grad = grad.astype(BF16)
-    given = lax.dynamic_index_in_dim(grad, 1 - here, axis, keepdims=False)
-    kept = lax.dynamic_index_in_dim(grad, here, axis, keepdims=False)
-    return kept.astype(F32) + from_pair(given).astype(F32)
 
 
 def exchange(blocks):
@@ -737,9 +722,63 @@
     )(rows_in, gain[None], shift[None], weight, bias[None])
 
 
+def feed_kernel(
+    normed_ref, grad_ref, up_ref, down_ref, bias_ref,
+    activated_ref, grad_hidden_ref, terms_ref, branch_ref, sums_ref,
+):
+    hidden = jnp.dot(normed_ref[...], up_ref[...], preferred_element_type=F32) + bias_ref[...]
+    grad_activated = lax.dot_general(grad_ref[...], down_ref[...], NT, preferred_element_type=F32)
+    normal = 0.5 * (1.0 + lax.erf(hidden * 0.5**0.5))
+    density = jnp.exp(-0.5 * hidden * hidden) * (2.0 * math.pi) ** -0.5
+    activated = (hidden * normal).astype(BF16)
+    grad_hidden = (grad_activated * (normal + hidden * density)).astype(BF16)
+    activated_ref[...] = activated
+    grad_hidden_ref[...] = grad_hidden
+    terms = lax.dot_general(grad_hidden, up_ref[...], NT, preferred_element_type=F32)
+    terms_ref[...] = terms.astype(BF16)
+    branch = jnp.dot(activated, down_ref[...], preferred_element_type=F32)
+    branch_ref[...] = branch.astype(BF16)
+
+    @pl.when(pl.program_id(0) == 0)
+    def clear():
+        sums_ref[...] = jnp.zeros_like(sums_ref)
+
+    sums_ref[...] += jnp.sum(grad_hidden.astype(F32), axis=0, keepdims=True)
+
+
+def feed(normed, grads, w_up, w_down, bias, block=256):
+    total, width = normed.shape
+    hidden = w_up.shape[1]
+    wide = pl.BlockSpec((block, width), lambda i: (i, 0))
+    narrow_rows = pl.BlockSpec((block, hidden), lambda i: (i, 0))
+    return pl.pallas_call(
+        feed_kernel,
+        grid=(total // block,),
+        in_specs=[
+            wide,
+            wide,
+            pl.BlockSpec((width, hidden), lambda i: (0, 0)),
+            pl.BlockSpec((hidden, width), lambda i: (0, 0)),
+            pl.BlockSpec((1, hidden), lambda i: (0, 0)),
+        ],
+        out_specs=[narrow_rows, narrow_rows, wide, wide, pl.BlockSpec((1, hidden), lambda i: (0, 0))],
+        out_shape=[
+            jax.ShapeDtypeStruct((total, hidden), BF16),
+            jax.ShapeDtypeStruct((total, hidden), BF16),
+            jax.ShapeDtypeStruct((total, width), BF16),
+            jax.ShapeDtypeStruct((total, width), BF16),
+            jax.ShapeDtypeStruct((1, hidden), F32),
+        ],
+        cost_estimate=pl.CostEstimate(flops=0, bytes_accessed=BUSY // 3, transcendentals=0),
+        name="feed",
+    )(normed, grads, w_up, w_down, bias[None])
+
+
 def sum_kernel(
-    count, pieces, part_ref, out_ref, held, chip_in, across_in, line_in, load_sem,
+    count, pieces, part_ref, grad_ref, pair_ref, out_ref, got_ref, pair_out,
+    held, chip_in, across_in, line_in, grad_in, grad_sum, load_sem,
     chip_send, chip_recv, across_send, across_recv, line_send, line_recv,
+    pass_sem, passed_sem, give_sem, take_sem, pair_sem,
 ):
     lines = count // 4
     me, line, side, core = own_place()
@@ -775,7 +814,7 @@
 
         lax.fori_loop(0, pieces, step, 0)
 
-    def far_first(visit):
+    def far_first(visit, between=None):
         for hops in range(lines - 1, 0, -1):
             @pl.when(line + hops < lines)
             def ahead(hops=hops):
@@ -784,6 +823,53 @@
             @pl.when(line >= hops)
             def behind(hops=hops):
                 visit(line - hops, -1)
+
+            if between is not None:
+                between(lines - hops)
+
+    half = lax.axis_index("fsdp")
+    barrier = pltpu.get_barrier_semaphore()
+
+    def enter(step, carried):
+        pl.semaphore_signal(
+            barrier, inc=1, device_id={"ctx": lax.rem(me + step, count)}, device_id_type=MESH_ID
+        )
+        return carried
+
+    def hand(step):
+        goal = lax.rem(me + step, count)
+        return remote(
+            grad_ref.at[goal, 1 - half], grad_in.at[goal], pass_sem.at[step], passed_sem.at[step],
+            {"fsdp": 1 - half},
+        )
+
+    def give_grad(step):
+        goal = lax.rem(me + step, count)
+        return remote(
+            grad_sum.at[goal], got_ref.at[me], give_sem.at[step], take_sem.at[step], {"ctx": goal}
+        )
+
+    def take_grad(step):
+        source = lax.rem(me + count - step, count)
+        return remote(
+            grad_sum.at[source], got_ref.at[source], give_sem.at[step], take_sem.at[step], {"ctx": source}
+        )
+
+    def each_step(first, last, body):
+        def step_body(step, carried):
+            body(step)
+            return carried
+
+        lax.fori_loop(first, last, step_body, 0)
+
+    def pass_on(step):
+        goal = lax.rem(me + step, count)
+        hand(step).wait_recv()
+        grad_sum[goal] = (grad_ref[goal, half].astype(F32) + grad_in[goal].astype(F32)).astype(BF16)
+        give_grad(step).start()
+
+    def pair_copy():
+        return remote(pair_ref.at[1 - half], pair_out, pair_sem.at[0], pair_sem.at[1], {"fsdp": 1 - half})
 
     loads = [
         pltpu.make_async_copy(part_ref.at[pair * 2 + core], held.at[pair], load_sem.at[pair])
@@ -791,7 +877,9 @@
     ]
     for load in loads:
         load.start()
-    greet(lines)
+    lax.fori_loop(1, count, enter, 0)
+    pl.semaphore_signal(barrier, inc=1, device_id={"fsdp": 1 - half}, device_id_type=MESH_ID)
+    pl.semaphore_wait(barrier, count)
 
     def give(goal, way):
         each_piece(lambda k: to_partner(goal * 2 + 1 - side, k).start())
@@ -799,6 +887,9 @@
     def give_same(goal, way):
         each_piece(lambda k: to_partner(goal * 2 + side, k).start())
 
+    each_step(1, count, lambda step: hand(step).start())
+    hand(0).start()
+    pair_copy().start()
     far_first(give)
     give(line, 0)
     far_first(give_same)
@@ -855,7 +946,16 @@
 
         each_piece(one)
 
-    far_first(along)
+    def share_of_steps(turn):
+        each_step(
+            1 + (turn - 1) * (count - 1) // (lines - 1), 1 + turn * (count - 1) // (lines - 1), pass_on
+        )
+
+    far_first(along, share_of_steps)
+    hand(0).wait_recv()
+    grad_sum[me] = (grad_ref[me, half].astype(F32) + grad_in[me].astype(F32)).astype(BF16)
+    stay = pltpu.make_async_copy(grad_sum.at[me], got_ref.at[me], pair_sem.at[2])
+    stay.start()
 
     def last(k):
         span = pl.ds(pl.multiple_of(k * rows, rows), rows)
@@ -889,23 +989,38 @@
         return carried
 
     lax.fori_loop(0, lines, settle_line, 0)
-
-
-def sum_rows(partial, pieces=2):
+    each_step(1, count, lambda step: take_grad(step).wait_recv())
+    each_step(1, count, lambda step: give_grad(step).wait_send())
+    each_step(0, count, lambda step: hand(step).wait_send())
+    pair_copy().wait_recv()
+    pair_copy().wait_send()
+    stay.wait()
+
+
+def sum_rows(partial, grad, pair_grad, collective_id, pieces=2):
     count = lax.axis_size("ctx")
     lines = count // 4
     width = partial.shape[1]
     rows = partial.shape[0] // count
+    owned, columns = grad.shape[0] // (2 * count), grad.shape[1]
+    anywhere = pl.BlockSpec(memory_space=pl.ANY)
+    pair_shape = (pair_grad.shape[0] // 2, pair_grad.shape[1])
     return pl.pallas_call(
         functools.partial(sum_kernel, count, pieces),
-        out_shape=jax.ShapeDtypeStruct((rows, width), F32),
-        in_specs=[pl.BlockSpec(memory_space=pl.ANY)],
-        out_specs=pl.BlockSpec(memory_space=pltpu.VMEM),
+        out_shape=[
+            jax.ShapeDtypeStruct((rows, width), F32),
+            jax.ShapeDtypeStruct((count, owned, columns), BF16),
+            jax.ShapeDtypeStruct(pair_shape, BF16),
+        ],
+        in_specs=[anywhere, pl.BlockSpec(memory_space=pltpu.VMEM), anywhere],
+        out_specs=[pl.BlockSpec(memory_space=pltpu.VMEM), anywhere, anywhere],
         scratch_shapes=[
             pltpu.VMEM((count // 2, rows, width), BF16),
             pltpu.VMEM((count // 2, rows, width), BF16),
             pltpu.VMEM((lines, rows, width), BF16),
             pltpu.VMEM((lines + 1, rows, width), BF16),
+            pltpu.VMEM((count, owned, columns), BF16),
+            pltpu.VMEM((count, owned, columns), BF16),
             pltpu.SemaphoreType.DMA((count // 2,)),
             pltpu.SemaphoreType.DMA((count // 2, pieces)),
             pltpu.SemaphoreType.DMA((count // 2, pieces)),
@@ -913,40 +1028,38 @@
             pltpu.SemaphoreType.DMA((lines, pieces)),
             pltpu.SemaphoreType.DMA((lines, pieces)),
             pltpu.SemaphoreType.DMA((lines + 1, pieces)),
+            pltpu.SemaphoreType.DMA((count,)),
+            pltpu.SemaphoreType.DMA((count,)),
+            pltpu.SemaphoreType.DMA((count,)),
+            pltpu.SemaphoreType.DMA((count,)),
+            pltpu.SemaphoreType.DMA((3,)),
         ],
         compiler_params=pltpu.CompilerParams(
-            collective_id=1, has_side_effects=True, vmem_limit_bytes=63 * 2**20
+            collective_id=collective_id, has_side_effects=True, vmem_limit_bytes=63 * 2**20
         ),
         cost_estimate=pl.CostEstimate(flops=0, bytes_accessed=BUSY, transcendentals=0),
         name="sum_rows",
-    )(partial.astype(BF16).reshape(count, rows, width))
+    )(
+        partial.astype(BF16).reshape(count, rows, width),
+        grad.reshape(count, 2, owned, columns),
+        pair_grad.reshape(2, *pair_shape),
+    )
+
+
+def own_half(pair_grad, other):
+    half = pair_grad.shape[0] // 2
+    kept = lax.dynamic_slice_in_dim(pair_grad, lax.axis_index("fsdp") * half, half, 0)
+    return kept.astype(F32) + other.astype(F32)
+
+
+def in_order(got, parts):
+    count, owned, _ = got.shape
+    return got.reshape(count, owned, parts, -1).transpose(1, 2, 0, 3).reshape(owned, -1).astype(F32)
 
 
 def weight_grad(rows_in, grads):
     terms = lax.dot_general(rows_in, grads, TN, preferred_element_type=F32).astype(BF16)
     return lax.optimization_barrier(terms)
-
-
-def rows_of_columns(grad):
-    count = lax.axis_size("ctx")
-    pair = lax.axis_size("fsdp")
-    rows = grad.shape[0] // (count * pair)
-    pieces = grad.reshape(count, pair, rows, *grad.shape[1:])
-    summed = pair_reduce(pieces, 1).astype(BF16)
-    mine = lax.all_to_all(summed, "ctx", split_axis=0, concat_axis=0)
-    return mine.transpose(1, 2, 0, 3).reshape(rows, -1).astype(F32)
-
-
-def pair_sum(grad):
-    return pair_reduce(grad.reshape(2, grad.shape[0] // 2, *grad.shape[1:]), 0)
-
-
-def rows_to_columns(local):
-    count = lax.axis_size("ctx")
-    rows = local.shape[0]
-    split = local.reshape(rows, count, -1).transpose(1, 0, 2)
-    mine = lax.all_to_all(split, "ctx", split_axis=0, concat_axis=0)
-    return mine.reshape(count * rows, -1)
 
 
 def columns_to_rows(slice_in):
@@ -1046,29 +1159,29 @@
     unit_two, rate_two = norm_parts(middle)
     normed_two = (unit_two * gain_two + shift_two).astype(BF16)
     normed_two_all = gather_rows(normed_two)
-    hidden = jnp.dot(normed_two_all, w_up_own, preferred_element_type=F32) + b_up_own
-    activated, gelu_pull = jax.vjp(gelu_exact, hidden)
-    activated = activated.astype(BF16)
-
-    grad_activated = lax.dot_general(grad_out_all, w_down_own, NT, preferred_element_type=F32)
-    grad_hidden = gelu_pull(grad_activated)[0].astype(BF16)
-    grad_normed_two = sum_rows(
-        lax.dot_general(grad_hidden, w_up_own, NT, preferred_element_type=F32)
-    )
-    grad_w_down = pair_sum(weight_grad(activated, grad_out_all))
-    grad_w_up = weight_grad(normed_two_all, grad_hidden)
-    grad_w_up = rows_of_columns(grad_w_up[:, None])
+    activated, grad_hidden, terms, branch_terms, grad_hidden_sums = feed(
+        normed_two_all, grad_out_all, w_up_own, w_down_own, b_up_own
+    )
+    w_down_terms = weight_grad(activated, grad_out_all)
+    grad_normed_two, w_up_got, w_down_other = sum_rows(
+        terms,
+        weight_grad(normed_two_all, grad_hidden),
+        w_down_terms,
+        1,
+    )
+    grad_w_up = in_order(w_up_got, 1)
+    grad_w_down = own_half(w_down_terms, w_down_other)
 
     grad_middle = grad_out.astype(F32) + norm_back(unit_two, rate_two, gain_two, grad_normed_two)
     grad_branch = grad_middle.astype(BF16)
-    grad_attended = lax.dot_general(
-        grad_branch, w_out_all, NT, preferred_element_type=F32
+    grad_branch, branch_terms = lax.optimization_barrier((grad_branch, branch_terms))
+    branch = sum_beside(branch_terms)
+    grad_branch_all = gather_rows(grad_branch)
+    w_out_head = lax.dynamic_slice_in_dim(w_out_all, head_at, head_width, 0)
+    grad_heads = lax.dot_general(
+        grad_branch_all, w_out_head, NT, preferred_element_type=F32
     ).astype(BF16)
-    grad_attended, late = lax.optimization_barrier((grad_attended, activated))
-    grad_heads = to_sequence(widen(rows_to_columns(grad_attended), share), count)
-    grad_branch_all = gather_beside(grad_branch)
-    branch = sum_beside(jnp.dot(late, w_down_own, preferred_element_type=F32))
-    grad_w_out = pair_sum(weight_grad(attended_own, grad_branch_all))
+    grad_heads = to_sequence(grad_heads, count)
 
     delta = (grad_heads.astype(F32) * attended_full).reshape(seq_len, heads, HEAD_DIM)
     delta = jnp.sum(delta, axis=-1).T
@@ -1079,9 +1192,15 @@
         [narrow(to_layout(part, count), share) for part in grad_parts], axis=1
     )
     column_sums = jnp.sum(grad_qkv.astype(F32), axis=0)
-    grad_normed = sum_rows(lax.dot_general(grad_qkv, w_qkv_own, NT, preferred_element_type=F32))
-    grad_w_qkv = weight_grad(normed_all, grad_qkv)
-    grad_w_qkv = rows_of_columns(grad_w_qkv.reshape(width, 3, own_cols))
+    w_out_terms = weight_grad(attended_own, grad_branch_all)
+    grad_normed, w_qkv_got, w_out_other = sum_rows(
+        lax.dot_general(grad_qkv, w_qkv_own, NT, preferred_element_type=F32),
+        weight_grad(normed_all, grad_qkv),
+        w_out_terms,
+        2,
+    )
+    grad_w_qkv = in_order(w_qkv_got, 3)
+    grad_w_out = own_half(w_out_terms, w_out_other)
     branch, middle, grad_normed = lax.optimization_barrier((branch, middle, grad_normed))
     outputs = (middle + branch + b_down_all).astype(BF16)
     grad_inputs = grad_middle + norm_back(unit_one, rate_one, gain_one, grad_normed)
@@ -1102,7 +1221,7 @@
         [
             column_sums[:own_cols].reshape(pair, -1),
             column_sums[2 * own_cols :].reshape(pair, -1),
-            jnp.sum(grad_hidden.astype(F32), axis=0).reshape(pair, -1),
+            grad_hidden_sums.reshape(pair, -1),
         ],
         axis=1,
     )

time: 644 us -> 630 us (0.978)
  Pallas kernels: 370 us -> 471 us
  matrix products: 96.2 us -> 47.6 us
  starting transfers between devices: 38.9 us -> 10.1 us
  waiting for transfers between devices: 47.9 us -> 27.8 us
  other arithmetic: 33.6 us -> 23.5 us
  local copies, waits for them, and re-layouts: 38.3 us -> 29.5 us
    pallas_call x1 -> x2, Pallas kernels: 58.4 us -> 128 us  [gather_rows(): pl.pallas_call(functools.partial(gather_kernel, count, pieces), out_shape...]
    dot_general x5 -> x1, matrix products: 48.3 us -> 3.48 us  [on_device(): lax.dot_general(grad_branch_all, w_out_head, NT, preferred_element_type=F32)]
    pallas_call x2 -> x3, Pallas kernels: 128 us -> 160 us  [the longest x2 135 us: sum_rows(): pl.pallas_call(functools.partial(sum_kernel, count, pieces), out_shape=[j...]
    all_to_all x3 -> x0, starting transfers between devices: 24.8 us -> none  [the longest x2 20.3 us: rows_of_columns(): mine = lax.all_to_all(summed, 'ctx', split_axis=0, concat_axis=0)]
    all_to_all x3 -> x0, waiting for transfers between devices: 12.8 us -> none  [the longest x2 10.4 us: rows_of_columns(): mine = lax.all_to_all(summed, 'ctx', split_axis=0, concat_axis=0)]
  transfers between devices with their start and end apart: 13 -> 5, of which waited for: 5 -> 2; matrix products, arithmetic and copies ran while one was open for 18% -> 12% of each run, Pallas kernels for 50% -> 61%
where the time goes in v4:
time: 630 us; the launch traced here: 624 us
  Pallas kernels  471 us (75%)
  matrix products  47.6 us (8%)
  local copies, waits for them, and re-layouts  29.5 us (5%)
  waiting for transfers between devices  27.8 us (4%)
  other arithmetic  23.5 us (4%)
  between operations  14.6 us (2%)
  starting transfers between devices  10.1 us (2%)
    pallas_call x2, Pallas kernels, sum_rows(): pl.pallas_call(functools.partial(sum_kernel, count, pieces), out_shape=[j...  135 us
    pallas_call x1, Pallas kernels, begin(): pl.pallas_call(functools.partial(begin_kernel, count, pieces, tuple(share...  130 us
    pallas_call x2, Pallas kernels, gather_rows(): pl.pallas_call(functools.partial(gather_kernel, count, pieces), out_shape...  128 us
    dot_general x4, matrix products, weight_grad(): lax.dot_general(rows_in, grads, TN, preferred_element_type=F32).astype(BF16)  31.2 us
    pallas_call x1, Pallas kernels, feed(): pl.pallas_call(feed_kernel, grid=(total // block,), in_specs=[wide, wide,...  24.5 us
    all_to_all x1, waiting for transfers between devices, columns_to_rows(): lax.all_to_all(slice_in.reshape(count, rows, -1), 'ctx', split_axis=0, co...  22.1 us
    pallas_call x1, Pallas kernels, attend_back(): pl.pallas_call(functools.partial(attend_back_kernel, rows, heads), grid=(...  20.4 us
    pallas_call x1, Pallas kernels, attend(): pl.pallas_call(functools.partial(attend_kernel, rows, heads), grid=(seq_l...  19.7 us
  transfers between devices with their start and end apart: 5, of which 2 were waited for; matrix products, arithmetic and copies ran while one was open for 12% of the time, Pallas kernels for 61%

profile of v4, /device:TPU:0, one launch (start us, length us, event | category | flops | bytes accessed | tf_op | source)
XLA Modules:
  0.0 623.6 jit_solution(13616892209542667534)
XLA Ops:
  7.2 0.7 all-gather.3.cloned.1.call-update
  8.0 6.1 concatenate.23
  14.1 0.6 bitcast_convert_fusion.refs_3_
  14.7 129.9 %begin.1 = (bf16[16,128,2048]{2,1,0:T(8,128)(2,1)}, bf16[32,64,384]{2,1,0:T(8,128)(2,1)}, bf16[32,64,512]{2,1,0:T(8,128)(2,1)}, f32[32,8,128]{2,1,0:T(8,128)}, bf16[2,256,2048]{2,1,0:T(8,128)(2,1)}) custom-call(bf16[128,2048]{1,0:T(8,128)(2,1)} %bitcast.142, bf16[64,6144]{1,0:T(8,128)(2,1)} %refs_1_.1, bf16[64,8192]{1,0:T(8,128)(2,1)} %refs_2_.1, ...), custom_call_target="tpu_custom_call" | custom-call | bytes 167772160 | tf_op jit(solution)/shard_map/begin/pallas_call | solution.py:650
  145.0 0.9 copy.87
  146.0 0.7 broadcast_in_dim_reshape.4.gain_ref
  147.0 0.6 broadcast_in_dim.70.bias_ref
  147.6 0.7 broadcast_in_dim_reshape.5.shift_ref
  148.3 0.5 multiply_power_fusion.slope_ref
  148.8 12.9 %project.1 = (bf16[2048,2048]{1,0:T(8,128)(2,1)}, bf16[2048,384]{1,0:T(8,128)(2,1)}) custom-call(bf16[2048,2048]{1,0:T(8,128)(2,1)} %bitcast.190, f32[1,2048]{1,0:T(1,128)} %broadcast_in_dim_reshape.4.gain_ref, f32[1,2048]{1,0:T(1,128)} %broadcast_in_dim_reshape.5.shift_ref, bf16[2048,384]{1,0:T(8,128)(2,1)} %bitcast.191, f32[1,384]{1,0:T(1,128)} %broadcast_in_dim.70.bias_ref), custom_call_target="tpu_custom_call" | custom-call | flops 3221225472 | bytes 25165824 | tf_op jit(solution)/shard_map/project/pallas_call | solution.py:700
  161.7 1.5 slice_bitcast_fusion.1
  163.5 0.5 and_select_fusion.low_ref
  164.0 1.2 fusion.18
  165.3 19.7 %attend.1 = (f32[2048,128]{1,0:T(8,128)}, f32[2,2048]{1,0:T(2,128)}) custom-call(s32[8]{0:T(128)} %and_select_fusion.low_ref, f32[2]{0:T(128)} %multiply_power_fusion.slope_ref, s32[1,2048]{1,0:T(1,128)} %bitcast.185, bf16[2048,128]{1,0:T(8,128)(2,1)} %get-tuple-element.87.q_ref, bf16[2048,128]{1,0:T(8,128)(2,1)} %get-tuple-element.86.k_ref, ...), custom_call_target="tpu_custom_call" | custom-call | bytes 55924052 | tf_op jit(solution)/shard_map/attend/pallas_call | solution.py:153
  185.0 1.3 convert_element_type.104
  186.4 0.9 pad_maximum_fusion.2
  187.2 4.8 all-to-all-start
  192.4 0.7 dynamic_slice.20
  193.0 22.1 %all-to-all-done = bf16[16,128,128]{2,1,0:T(8,128)(2,1)S(1)} async-done(((bf16[16,128,128]{2,1,0:T(8,128)(2,1)}), bf16[16,128,128]{2,1,0:T(8,128)(2,1)S(1)}, u32[]{:S(2)}, u32[]{:S(2)}) %all-to-all-start) | async-done | bytes 524320 | tf_op jit(solution)/shard_map/all_to_all | solution.py:1068
  215.1 0.3 copy.62
  215.5 4.7 fusion.26
  220.2 0.3 multiply_reduce_fusion.2
  220.5 0.7 copy-done
  221.2 1.0 add_convert_fusion.1.own_ref
  222.2 59.0 %gather_rows.2 = bf16[16,128,2048]{2,1,0:T(8,128)(2,1)} custom-call(bf16[128,2048]{1,0:T(8,128)(2,1)} %add_convert_fusion.1.own_ref), custom_call_target="tpu_custom_call" | custom-call | bytes 167772160 | tf_op jit(solution)/shard_map/gather_rows/pallas_call | solution.py:388
  281.2 24.5 %feed.1 = (bf16[2048,512]{1,0:T(8,128)(2,1)}, bf16[2048,512]{1,0:T(8,128)(2,1)}, bf16[2048,2048]{1,0:T(8,128)(2,1)}, bf16[2048,2048]{1,0:T(8,128)(2,1)}, f32[1,512]{1,0:T(1,128)}) custom-call(bf16[2048,2048]{1,0:T(8,128)(2,1)} %bitcast.140, bf16[2048,2048]{1,0:T(8,128)(2,1)} %all-gather.5.cloned.1.call-done.grad_ref, bf16[2048,512]{1,0:T(8,128)(2,1)} %bitcast.165, ...), custom_call_target="tpu_custom_call" | custom-call | bytes 55924052 | tf_op jit(solution)/shard_map/feed/pallas_call | solution.py:754
  305.7 10.0 %convolution_convert_fusion.1 = bf16[512,2048]{1,0:T(8,128)(2,1)} fusion(bf16[2048,512]{1,0:T(8,128)(2,1)} %get-tuple-element.56, bf16[2048,2048]{1,0:T(8,128)(2,1)} %all-gather.5.cloned.1.call-done.grad_ref), kind=kOutput, calls=%fused_computation.2 | convolution fusion | flops 4296015872 | bytes 12582912 | tf_op jit(solution)/shard_map/dot_general | solution.py:1061
  315.8 5.7 convolution_convert_fusion.2
  321.5 68.5 %sum_rows.2 = (f32[128,2048]{1,0:T(8,128)}, bf16[16,64,512]{2,1,0:T(8,128)(2,1)}, bf16[256,2048]{1,0:T(8,128)(2,1)}) custom-call(bf16[16,128,2048]{2,1,0:T(8,128)(2,1)} %bitcast.144, bf16[16,2,64,512]{3,2,1,0:T(8,128)(2,1)} %bitcast.163, bf16[2,256,2048]{2,1,0:T(8,128)(2,1)} %bitcast.149), custom_call_target="tpu_custom_call" | custom-call | bytes 167772160 | tf_op jit(solution)/shard_map/sum_rows/pallas_call | solution.py:1008
  390.0 2.1 multiply_reduce_fusion
  392.2 2.9 fusion.17
  395.6 0.3 fusion.12
  395.9 0.5 broadcast.130
  396.4 0.7 reduce.3
  397.3 68.9 %gather_rows.3 = bf16[16,128,2048]{2,1,0:T(8,128)(2,1)} custom-call(bf16[128,2048]{1,0:T(8,128)(2,1)} %get-tuple-element.61.own_ref), custom_call_target="tpu_custom_call" | custom-call | bytes 167772160 | tf_op jit(solution)/shard_map/gather_rows/pallas_call | solution.py:388
  466.5 0.3 fusion.27
  466.8 1.5 copy.80
  468.3 6.3 %convolution_convert_fusion.4 = bf16[128,2048]{1,0:T(8,128)(2,1)} fusion(bf16[2048,128]{1,0:T(8,128)(2,1)} %bitcast.49, bf16[2048,2048]{1,0:T(8,128)(2,1)} %bitcast.136), kind=kOutput, calls=%fused_computation.7 | convolution fusion | flops 1074003968 | bytes 9437184 | tf_op jit(solution)/shard_map/dot_general | solution.py:1061
  474.6 3.5 convolution_convert_fusion.5
  478.2 1.1 copy-done.9
  479.3 1.1 convert_multiply_fusion
  480.5 1.6 copy.65
  482.1 0.7 bitcast_reduce_fusion
  482.7 20.4 %attend_back.1 = (bf16[2048,128]{1,0:T(8,128)(2,1)}, bf16[2048,128]{1,0:T(8,128)(2,1)}, bf16[2048,128]{1,0:T(8,128)(2,1)}) custom-call(s32[8]{0:T(128)} %and_select_fusion.low_ref, f32[2]{0:T(128)} %multiply_power_fusion.slope_ref, s32[1,2048]{1,0:T(1,128)} %bitcast.186, f32[2,2048]{1,0:T(2,128)} %get-tuple-element.60.total_ref, f32[2,2048]{1,0:T(2,128)} %bitcast.187, ...), custom_call_target="tpu_custom_call" | custom-call | bytes 55924052 | tf_op jit(solution)/shard_map/attend_back/pallas_call | solution.py:175
  503.2 1.1 fusion.19
  504.3 1.1 fusion.20
  505.7 9.1 %convolution_convert_fusion.3 = bf16[2048,384]{1,0:T(8,128)(2,1)} fusion(bf16[2048,2048]{1,0:T(8,128)(2,1)} %get-tuple-element.65, bf16[2048,128]{1,0:T(8,128)(2,1)S(1)} %bitcast.160, bf16[2048,128]{1,0:T(8,128)(2,1)S(1)} %bitcast.157, bf16[2048,128]{1,0:T(8,128)(2,1)S(1)} %bitcast.153), kind=kOutput, calls=%fused_computation.4 | convolution fusion | flops 3226730496 | bytes 11534336 | tf_op jit(solution)/shard_map/dot_general | solution.py:1061
  514.8 0.4 convert_reduce_fusion
  515.5 8.1 %convolution_convert_fusion = bf16[2048,2048]{1,0:T(8,128)(2,1)} fusion(bf16[2048,384]{1,0:T(8,128)(2,1)} %bitcast.192, bf16[2048,128]{1,0:T(8,128)(2,1)S(1)} %bitcast.162, bf16[2048,128]{1,0:T(8,128)(2,1)S(1)} %bitcast.159, bf16[2048,128]{1,0:T(8,128)(2,1)S(1)} %bitcast.155), kind=kOutput, calls=%fused_computation | convolution fusion | flops 3230138368 | bytes 11534336 | tf_op jit(solution)/shard_map/dot_general | solution.py:1197
  523.7 66.7 %sum_rows.3 = (f32[128,2048]{1,0:T(8,128)}, bf16[16,64,384]{2,1,0:T(8,128)(2,1)}, bf16[64,2048]{1,0:T(8,128)(2,1)}) custom-call(bf16[16,128,2048]{2,1,0:T(8,128)(2,1)} %bitcast.143, bf16[16,2,64,384]{3,2,1,0:T(8,128)(2,1)} %bitcast.167, bf16[2,64,2048]{2,1,0:T(8,128)(2,1)} %bitcast.151), custom_call_target="tpu_custom_call" | custom-call | bytes 167772160 | tf_op jit(solution)/shard_map/sum_rows/pallas_call | solution.py:1008
  590.4 2.4 reshape.299
  592.8 0.9 copy.69
  593.8 1.6 copy.85
  595.5 0.9 convert_add_fusion.2
  596.4 1.7 convert_add_fusion
  598.1 2.2 convert_element_type.109
  600.2 0.5 fusion.11
  601.1 0.7 copy.77
  601.8 5.2 all-to-all-start.1
  607.0 2.7 fusion.10
  609.8 0.9 fusion.13
  610.7 4.9 all-to-all-done.1
  615.7 0.6 slice.168
  616.2 0.6 fusion.24
  (116 shorter events, 3.8 us)
Async XLA Ops:
  7.2 137.4 %copy-start.20 = (s32[1,8]{1,0:T(1,128)S(1)}, s32[1,8]{1,0:T(1,128)}, u32[]{:S(2)}) copy-start(s32[1,8]{1,0:T(1,128)} %param.17) | copy-start | bytes 100
  7.2 208.2 %all-gather.3.cloned.1.call-start = ((), (), s32[]{:S(2)}) async-start(), calls=%async_computation.3 | async-start | bytes 8650752 | tf_op jit(solution)/shard_map/all_gather | solution.py:1139
  7.9 273.3 %all-gather.5.cloned.1.call-start = ((), (), s32[]{:S(2)}) async-start(), calls=%async_computation.4 | async-start | bytes 8912896 | tf_op jit(solution)/shard_map/all_gather | solution.py:198
  144.9 16.8 %copy-start.17 = (s32[2048]{0:T(1024)}, s32[2048]{0:T(1024)S(1)}, u32[]{:S(2)}) copy-start(s32[2048]{0:T(1024)S(1)} %select_reduce_fusion) | copy-start | bytes 24580
  186.3 29.1 %copy-start.4 = (bf16[1,128,2048]{2,1,0:T(8,128)(2,1)S(1)}, bf16[1,128,2048]{2,1,0:T(8,128)(2,1)}, u32[]{:S(2)}) copy-start(bf16[1,128,2048]{2,1,0:T(8,128)(2,1)} %param.16) | copy-start | bytes 1572868
  187.2 27.9 %all-to-all-start = ((bf16[16,128,128]{2,1,0:T(8,128)(2,1)}), bf16[16,128,128]{2,1,0:T(8,128)(2,1)S(1)}, u32[]{:S(2)}, u32[]{:S(2)}) async-start(bf16[16,128,128]{2,1,0:T(8,128)(2,1)} %bitcast.15), calls=%async_computation | async-start | bytes 1048576 | tf_op jit(solution)/shard_map/all_to_all | solution.py:1068
  192.1 406.0 %reduce-scatter.2.cloned.1.call-start = ((), (), s32[]{:S(2)}) async-start(), calls=%async_computation.5 | async-start | bytes 8912896 | tf_op jit(solution)/shard_map/reduce_scatter | solution.py:202
  220.2 1.0 copy-start
  305.7 10.1 %copy-start.3 = (bf16[16,128,2048]{2,1,0:T(8,128)(2,1)S(1)}, bf16[16,128,2048]{2,1,0:T(8,128)(2,1)}, u32[]{:S(2)}) copy-start(bf16[16,128,2048]{2,1,0:T(8,128)(2,1)} %gather_rows.2) | copy-start | bytes 25165828
  305.7 10.1 %copy-start.19 = (bf16[2048,512]{1,0:T(8,128)(2,1)S(1)}, bf16[2048,512]{1,0:T(8,128)(2,1)}, u32[]{:S(2)}) copy-start(bf16[2048,512]{1,0:T(8,128)(2,1)} %get-tuple-element.55) | copy-start | bytes 6291460
  390.0 2.1 copy-start.1
  390.0 2.2 copy-start.11
  395.1 1.3 copy-start.18
  397.2 69.0 %copy-start.7 = (bf16[128,2048]{1,0:T(8,128)(2,1)S(1)}, bf16[128,2048]{1,0:T(8,128)(2,1)}, u32[]{:S(2)}) copy-start(bf16[128,2048]{1,0:T(8,128)(2,1)} %get-tuple-element.61.own_ref) | copy-start | bytes 1572868
  397.2 69.2 %copy-start.14 = (bf16[16,64,512]{2,1,0:T(8,128)(2,1)S(1)}, bf16[16,64,512]{2,1,0:T(8,128)(2,1)}, u32[]{:S(2)}) copy-start(bf16[16,64,512]{2,1,0:T(8,128)(2,1)} %get-tuple-element.73) | copy-start | bytes 3145732
  466.7 7.9 %slice-start = ((s8[8388608]{0:T(1024)(128)(4,1)}), s8[4194304]{0:T(1024)(128)(4,1)S(1)}, s32[]{:S(2)}) async-start(s8[8388608]{0:T(1024)(128)(4,1)} %bitcast.137), calls=%async_computation.6 | async-start | bytes 8388608
  468.3 6.3 %slice-start.1 = ((s8[8388608]{0:T(1024)(128)(4,1)}), s8[4194304]{0:T(1024)(128)(4,1)S(1)}, s32[]{:S(2)}) async-start(s8[8388608]{0:T(1024)(128)(4,1)} %bitcast.137), calls=%async_computation.7 | async-start | bytes 8388608
  478.1 1.2 copy-start.9
  479.3 2.7 copy-start.5
  503.2 2.3 copy-start.15
  593.7 1.7 copy-start.12
  593.7 1.7 copy-start.16
  593.7 2.6 copy-start.6
  593.7 2.6 copy-start.13
  596.4 3.8 copy-start.8
  601.1 8.7 %copy-start.2 = (f32[128,2048]{1,0:T(8,128)S(1)}, f32[128,2048]{1,0:T(8,128)}, u32[]{:S(2)}) copy-start(f32[128,2048]{1,0:T(8,128)} %copy-done) | copy-start | bytes 3145732
  601.8 13.8 %all-to-all-start.1 = ((f32[32,8,128]{2,1,0:T(8,128)}), f32[32,8,128]{2,1,0:T(8,128)S(1)}, u32[]{:S(2)}, u32[]{:S(2)}) async-start(f32[32,8,128]{2,1,0:T(8,128)} %bitcast.74), calls=%async_computation.2 | async-start | bytes 262144 | tf_op jit(solution)/shard_map/all_to_all | solution.py:209
  607.0 2.7 copy-start.10
Sparse Core Ops, SparseCore 0:
  11.1 126.4 all-gather.2
  144.7 82.6 all-gather.4
  395.2 115.3 reduce-scatter.1

commit v5 on v4

--- a/solution.py
+++ b/solution.py
@@ -405,10 +405,11 @@
     return gathered.reshape(count * rows, width)
 
 
-def begin_kernel(count, pieces, shared, *refs):
+def supply_kernel(count, pieces, shared, *refs):
     inputs = len(shared) + 2
-    own_ref, sources, down_ref = refs[0], refs[1 : inputs - 1], refs[inputs - 1]
-    out_ref, targets, down_out = refs[inputs], refs[inputs + 1 : 2 * inputs - 1], refs[2 * inputs - 1]
+    own_ref, sources, pair_ref = refs[0], refs[1 : inputs - 1], refs[inputs - 1]
+    out_ref, targets = refs[inputs], refs[inputs + 1 : 2 * inputs - 1]
+    pair_out = refs[2 * inputs - 1]
     (
         keep_sem, up_sem, down_sem, across_sem, chip_sem, recv_sem,
         give_sem, take_sem, pass_sem, passed_sem, stay_sem, pair_sem,
@@ -482,10 +483,10 @@
 
         lax.fori_loop(first, last, step_body, 0)
 
-    down_stay = pltpu.make_async_copy(down_ref, down_out.at[half], stay_sem.at[len(moves)])
-
-    def down_pair(side_of):
-        return remote(down_ref, down_out.at[side_of], pair_sem.at[0], pair_sem.at[1], {"fsdp": 1 - half})
+    pair_stay = pltpu.make_async_copy(pair_ref, pair_out.at[half], stay_sem.at[len(moves)])
+
+    def pair_copy(side_of):
+        return remote(pair_ref, pair_out.at[side_of], pair_sem.at[0], pair_sem.at[1], {"fsdp": 1 - half})
 
     def part(block, k):
         return out_ref.at[block, pl.ds(pl.multiple_of(k * rows, rows), rows), :]
@@ -535,11 +536,11 @@
 
     each_piece(first)
     each_step(1, count, lambda step, m: give(step, m).start())
-    down_pair(half).start()
+    pair_copy(half).start()
     for m in range(len(moves)):
         hand_own(m).start()
     keep.start()
-    down_stay.start()
+    pair_stay.start()
     for m in range(len(moves)):
         stay(m).start()
 
@@ -625,39 +626,34 @@
     for m in range(len(moves)):
         hand_own(m).wait_send()
         stay(m).wait()
-    down_pair(1 - half).wait_recv()
-    down_pair(half).wait_send()
-    down_stay.wait()
+    pair_copy(1 - half).wait_recv()
+    pair_copy(half).wait_send()
+    pair_stay.wait()
     keep.wait()
 
 
-def begin(own, w_qkv, w_up, w_down, vectors, pieces=2):
+def supply(own, arrays, shared, pair_array, collective_id, name, pieces=2):
     count = lax.axis_size("ctx")
     lines = count // 4
     rows, width = own.shape
-    owned = w_qkv.shape[0]
-    qkv_cols = w_qkv.shape[1] // count
-    up_cols = w_up.shape[1] // count
-    if qkv_cols % 384 == 0:
-        shared = [(3, "columns")]
-    else:
-        w_qkv = w_qkv.reshape(owned, 3, count, -1).transpose(2, 0, 1, 3).reshape(count, owned, qkv_cols)
-        shared = [(1, "blocks")]
-    shared += [(1, "columns"), (1, "same")]
+    targets = []
+    for array, (_, kind) in zip(arrays, shared):
+        if kind == "columns":
+            block = (array.shape[0], array.shape[1] // count)
+        else:
+            block = array.shape if kind == "same" else array.shape[1:]
+        targets.append(jax.ShapeDtypeStruct((count * 2, *block), array.dtype))
     moves = sum(parts for parts, _ in shared)
-    in_vmem = pl.BlockSpec(memory_space=pltpu.VMEM)
-    anywhere = pl.BlockSpec(memory_space=pl.ANY)
-    rows_all, qkv, up, vectors_all, down = pl.pallas_call(
-        functools.partial(begin_kernel, count, pieces, tuple(shared)),
+    operands = [own, *arrays, pair_array]
+    rows_all, *got, pair_all = pl.pallas_call(
+        functools.partial(supply_kernel, count, pieces, tuple(shared)),
         out_shape=[
             jax.ShapeDtypeStruct((count, rows, width), own.dtype),
-            jax.ShapeDtypeStruct((count * 2, owned, qkv_cols), BF16),
-            jax.ShapeDtypeStruct((count * 2, owned, up_cols), BF16),
-            jax.ShapeDtypeStruct((count * 2, *vectors.shape), F32),
-            jax.ShapeDtypeStruct((2, *w_down.shape), BF16),
+            *targets,
+            jax.ShapeDtypeStruct((2, *pair_array.shape), pair_array.dtype),
         ],
-        in_specs=[in_vmem] * 5,
-        out_specs=[anywhere] * 5,
+        in_specs=[pl.BlockSpec(memory_space=pltpu.VMEM)] * len(operands),
+        out_specs=[pl.BlockSpec(memory_space=pl.ANY)] * len(operands),
         scratch_shapes=[
             pltpu.SemaphoreType.DMA,
             pltpu.SemaphoreType.DMA((lines, pieces)),
@@ -672,17 +668,11 @@
             pltpu.SemaphoreType.DMA((moves + 1,)),
             pltpu.SemaphoreType.DMA((2,)),
         ],
-        compiler_params=pltpu.CompilerParams(collective_id=3, has_side_effects=True),
+        compiler_params=pltpu.CompilerParams(collective_id=collective_id, has_side_effects=True),
         cost_estimate=pl.CostEstimate(flops=0, bytes_accessed=BUSY, transcendentals=0),
-        name="begin",
-    )(own, w_qkv, w_up, vectors, w_down)
-    return (
-        rows_all.reshape(count * rows, width),
-        qkv.reshape(-1, qkv_cols),
-        up.reshape(-1, up_cols),
-        down.reshape(-1, width),
-        vectors_all.reshape(count * 2, -1),
-    )
+        name=name,
+    )(*operands)
+    return rows_all.reshape(count * rows, width), got, pair_all.reshape(-1, pair_array.shape[1])
 
 
 def project_kernel(rows_ref, gain_ref, shift_ref, weight_ref, bias_ref, normed_ref, out_ref):
@@ -775,11 +765,20 @@
 
 
 def sum_kernel(
-    count, pieces, part_ref, grad_ref, pair_ref, out_ref, got_ref, pair_out,
-    held, chip_in, across_in, line_in, grad_in, grad_sum, load_sem,
-    chip_send, chip_recv, across_send, across_recv, line_send, line_recv,
-    pass_sem, passed_sem, give_sem, take_sem, pair_sem,
+    count, pieces, riders, *refs
 ):
+    if riders:
+        (
+            part_ref, grad_ref, pair_ref, out_ref, got_ref, pair_out,
+            held, chip_in, across_in, line_in, grad_in, grad_sum, load_sem,
+            chip_send, chip_recv, across_send, across_recv, line_send, line_recv,
+            pass_sem, passed_sem, give_sem, take_sem, pair_sem,
+        ) = refs
+    else:
+        (
+            part_ref, out_ref, held, chip_in, across_in, line_in, load_sem,
+            chip_send, chip_recv, across_send, across_recv, line_send, line_recv,
+        ) = refs
     lines = count // 4
     me, line, side, core = own_place()
     partner = place_of(line, side, 1 - core)
@@ -887,9 +886,10 @@
     def give_same(goal, way):
         each_piece(lambda k: to_partner(goal * 2 + side, k).start())
 
-    each_step(1, count, lambda step: hand(step).start())
-    hand(0).start()
-    pair_copy().start()
+    if riders:
+        each_step(1, count, lambda step: hand(step).start())
+        hand(0).start()
+        pair_copy().start()
     far_first(give)
     give(line, 0)
     far_first(give_same)
@@ -951,11 +951,12 @@
             1 + (turn - 1) * (count - 1) // (lines - 1), 1 + turn * (count - 1) // (lines - 1), pass_on
         )
 
-    far_first(along, share_of_steps)
-    hand(0).wait_recv()
-    grad_sum[me] = (grad_ref[me, half].astype(F32) + grad_in[me].astype(F32)).astype(BF16)
-    stay = pltpu.make_async_copy(grad_sum.at[me], got_ref.at[me], pair_sem.at[2])
-    stay.start()
+    far_first(along, share_of_steps if riders else None)
+    if riders:
+        hand(0).wait_recv()
+        grad_sum[me] = (grad_ref[me, half].astype(F32) + grad_in[me].astype(F32)).astype(BF16)
+        stay = pltpu.make_async_copy(grad_sum.at[me], got_ref.at[me], pair_sem.at[2])
+        stay.start()
 
     def last(k):
         span = pl.ds(pl.multiple_of(k * rows, rows), rows)
@@ -989,61 +990,55 @@
         return carried
 
     lax.fori_loop(0, lines, settle_line, 0)
-    each_step(1, count, lambda step: take_grad(step).wait_recv())
-    each_step(1, count, lambda step: give_grad(step).wait_send())
-    each_step(0, count, lambda step: hand(step).wait_send())
-    pair_copy().wait_recv()
-    pair_copy().wait_send()
-    stay.wait()
-
-
-def sum_rows(partial, grad, pair_grad, collective_id, pieces=2):
+    if riders:
+        each_step(1, count, lambda step: take_grad(step).wait_recv())
+        each_step(1, count, lambda step: give_grad(step).wait_send())
+        each_step(0, count, lambda step: hand(step).wait_send())
+        pair_copy().wait_recv()
+        pair_copy().wait_send()
+        stay.wait()
+
+
+def sum_rows(partial, collective_id, grad=None, pair_grad=None, pieces=2):
     count = lax.axis_size("ctx")
     lines = count // 4
     width = partial.shape[1]
     rows = partial.shape[0] // count
-    owned, columns = grad.shape[0] // (2 * count), grad.shape[1]
+    riders = grad is not None
     anywhere = pl.BlockSpec(memory_space=pl.ANY)
-    pair_shape = (pair_grad.shape[0] // 2, pair_grad.shape[1])
-    return pl.pallas_call(
-        functools.partial(sum_kernel, count, pieces),
-        out_shape=[
-            jax.ShapeDtypeStruct((rows, width), F32),
+    in_vmem = pl.BlockSpec(memory_space=pltpu.VMEM)
+    operands = [partial.astype(BF16).reshape(count, rows, width)]
+    results = [jax.ShapeDtypeStruct((rows, width), F32)]
+    buffers = [
+        pltpu.VMEM((count // 2, rows, width), BF16),
+        pltpu.VMEM((count // 2, rows, width), BF16),
+        pltpu.VMEM((lines, rows, width), BF16),
+        pltpu.VMEM((lines + 1, rows, width), BF16),
+    ]
+    semaphores = [(count // 2,)] + [(count // 2, pieces)] * 2 + [(lines, pieces)] * 3 + [(lines + 1, pieces)]
+    if riders:
+        owned, columns = grad.shape[0] // (2 * count), grad.shape[1]
+        pair_shape = (pair_grad.shape[0] // 2, pair_grad.shape[1])
+        operands += [grad.reshape(count, 2, owned, columns), pair_grad.reshape(2, *pair_shape)]
+        results += [
             jax.ShapeDtypeStruct((count, owned, columns), BF16),
             jax.ShapeDtypeStruct(pair_shape, BF16),
-        ],
-        in_specs=[anywhere, pl.BlockSpec(memory_space=pltpu.VMEM), anywhere],
-        out_specs=[pl.BlockSpec(memory_space=pltpu.VMEM), anywhere, anywhere],
-        scratch_shapes=[
-            pltpu.VMEM((count // 2, rows, width), BF16),
-            pltpu.VMEM((count // 2, rows, width), BF16),
-            pltpu.VMEM((lines, rows, width), BF16),
-            pltpu.VMEM((lines + 1, rows, width), BF16),
-            pltpu.VMEM((count, owned, columns), BF16),
-            pltpu.VMEM((count, owned, columns), BF16),
-            pltpu.SemaphoreType.DMA((count // 2,)),
-            pltpu.SemaphoreType.DMA((count // 2, pieces)),
-            pltpu.SemaphoreType.DMA((count // 2, pieces)),
-            pltpu.SemaphoreType.DMA((lines, pieces)),
-            pltpu.SemaphoreType.DMA((lines, pieces)),
-            pltpu.SemaphoreType.DMA((lines, pieces)),
-            pltpu.SemaphoreType.DMA((lines + 1, pieces)),
-            pltpu.SemaphoreType.DMA((count,)),
-            pltpu.SemaphoreType.DMA((count,)),
-            pltpu.SemaphoreType.DMA((count,)),
-            pltpu.SemaphoreType.DMA((count,)),
-            pltpu.SemaphoreType.DMA((3,)),
-        ],
+        ]
+        buffers += [pltpu.VMEM((count, owned, columns), BF16)] * 2
+        semaphores += [(count,)] * 4 + [(3,)]
+    done = pl.pallas_call(
+        functools.partial(sum_kernel, count, pieces, riders),
+        out_shape=results,
+        in_specs=[anywhere] + [in_vmem, anywhere] * riders,
+        out_specs=[in_vmem] + [anywhere] * (2 * riders),
+        scratch_shapes=buffers + [pltpu.SemaphoreType.DMA(shape) for shape in semaphores],
         compiler_params=pltpu.CompilerParams(
             collective_id=collective_id, has_side_effects=True, vmem_limit_bytes=63 * 2**20
         ),
         cost_estimate=pl.CostEstimate(flops=0, bytes_accessed=BUSY, transcendentals=0),
         name="sum_rows",
-    )(
-        partial.astype(BF16).reshape(count, rows, width),
-        grad.reshape(count, 2, owned, columns),
-        pair_grad.reshape(2, *pair_shape),
-    )
+    )(*operands)
+    return done if riders else done[0]
 
 
 def own_half(pair_grad, other):
@@ -1062,20 +1057,13 @@
     return lax.optimization_barrier(terms)
 
 
-def columns_to_rows(slice_in):
-    count = lax.axis_size("ctx")
-    rows = slice_in.shape[0] // count
-    mine = lax.all_to_all(slice_in.reshape(count, rows, -1), "ctx", split_axis=0, concat_axis=0)
-    return mine.transpose(1, 0, 2).reshape(rows, -1)
-
-
-def widen(columns, share):
+def widen(columns, share, axis=-1):
     if share == 1:
         return columns
     count = lax.axis_size("ctx")
     groups = [list(range(first, first + share)) for first in range(0, count, share)]
     return lax.all_gather(
-        columns, "ctx", axis=columns.ndim - 1, tiled=True, axis_index_groups=groups
+        columns, "ctx", axis=axis % columns.ndim, tiled=True, axis_index_groups=groups
     )
 
 
@@ -1119,9 +1107,16 @@
     own_vectors = jnp.concatenate([vector.astype(F32) for vector in vectors])
     tiles = -(-own_vectors.shape[0] // 1024) * 8
     own_vectors = jnp.pad(own_vectors, (0, tiles * 128 - own_vectors.shape[0])).reshape(tiles, 128)
-    tokens_all, w_qkv_own, w_up_own, w_down_own, everywhere = begin(
-        tokens[0], w_qkv, w_up, w_down, own_vectors
-    )
+    if own_cols % 128 == 0:
+        qkv_blocks, qkv_kind = w_qkv, (3, "columns")
+    else:
+        split = w_qkv.reshape(w_qkv.shape[0], 3, count, own_cols).transpose(2, 0, 1, 3)
+        qkv_blocks, qkv_kind = split.reshape(count, w_qkv.shape[0], -1), (1, "blocks")
+    tokens_all, (w_qkv_own, everywhere), w_out_own = supply(
+        tokens[0], [qkv_blocks, own_vectors], [qkv_kind, (1, "same")], w_out, 3, "begin"
+    )
+    w_qkv_own = w_qkv_own.reshape(width, -1)
+    everywhere = everywhere.reshape(devices, -1)
     at = 0
     whole_vectors = []
     for vector in vectors:
@@ -1136,7 +1131,7 @@
     b_up_own = lax.dynamic_slice_in_dim(whole_vectors[8], rank * ff_cols, ff_cols)
 
     w_qkv_head = widen(w_qkv_own.reshape(width, 3, -1), share).reshape(width, -1)
-    w_out_all = lax.all_gather(w_out, BOTH, axis=0, tiled=True)
+    w_out_head = widen(w_out_own, share, 0)
 
     inputs = tokens[0].astype(F32)
     unit_one, rate_one = norm_parts(inputs)
@@ -1153,31 +1148,28 @@
     )
     attended_full, log_total = attend(queries, keys, values, starts, low, slopes, rows)
     attended_own = narrow(to_layout(attended_full.astype(BF16), count), share)
-    attended = columns_to_rows(attended_own)
-    middle = inputs + jnp.dot(attended, w_out_all, preferred_element_type=F32) + b_out_all
+    attended_terms = jnp.dot(attended_own, w_out_own, preferred_element_type=F32)
+    middle = inputs + sum_rows(attended_terms, 4) + b_out_all
 
     unit_two, rate_two = norm_parts(middle)
     normed_two = (unit_two * gain_two + shift_two).astype(BF16)
-    normed_two_all = gather_rows(normed_two)
+    normed_two_all, (w_up_own,), w_down_own = supply(
+        normed_two, [w_up], [(1, "columns")], w_down, 5, "middle"
+    )
+    w_up_own = w_up_own.reshape(width, -1)
     activated, grad_hidden, terms, branch_terms, grad_hidden_sums = feed(
         normed_two_all, grad_out_all, w_up_own, w_down_own, b_up_own
     )
     w_down_terms = weight_grad(activated, grad_out_all)
     grad_normed_two, w_up_got, w_down_other = sum_rows(
-        terms,
-        weight_grad(normed_two_all, grad_hidden),
-        w_down_terms,
-        1,
-    )
-    grad_w_up = in_order(w_up_got, 1)
-    grad_w_down = own_half(w_down_terms, w_down_other)
+        terms, 1, weight_grad(normed_two_all, grad_hidden), w_down_terms
+    )
 
     grad_middle = grad_out.astype(F32) + norm_back(unit_two, rate_two, gain_two, grad_normed_two)
     grad_branch = grad_middle.astype(BF16)
     grad_branch, branch_terms = lax.optimization_barrier((grad_branch, branch_terms))
     branch = sum_beside(branch_terms)
     grad_branch_all = gather_rows(grad_branch)
-    w_out_head = lax.dynamic_slice_in_dim(w_out_all, head_at, head_width, 0)
     grad_heads = lax.dot_general(
         grad_branch_all, w_out_head, NT, preferred_element_type=F32
     ).astype(BF16)
@@ -1195,12 +1187,10 @@
     w_out_terms = weight_grad(attended_own, grad_branch_all)
     grad_normed, w_qkv_got, w_out_other = sum_rows(
         lax.dot_general(grad_qkv, w_qkv_own, NT, preferred_element_type=F32),
+        2,
         weight_grad(normed_all, grad_qkv),
         w_out_terms,
-        2,
-    )
-    grad_w_qkv = in_order(w_qkv_got, 3)
-    grad_w_out = own_half(w_out_terms, w_out_other)
+    )
     branch, middle, grad_normed = lax.optimization_barrier((branch, middle, grad_normed))
     outputs = (middle + branch + b_down_all).astype(BF16)
     grad_inputs = grad_middle + norm_back(unit_one, rate_one, gain_one, grad_normed)
@@ -1225,6 +1215,13 @@
         ],
         axis=1,
     )
+    full_sums, w_qkv_got, w_up_got, w_out_other, w_down_other = lax.optimization_barrier(
+        (full_sums, w_qkv_got, w_up_got, w_out_other, w_down_other)
+    )
+    grad_w_qkv = in_order(w_qkv_got, 3)
+    grad_w_up = in_order(w_up_got, 1)
+    grad_w_out = own_half(w_out_terms, w_out_other)
+    grad_w_down = own_half(w_down_terms, w_down_other)
     here = (jnp.arange(count) == rank)[:, None, None]
     own_sums = jnp.where(here, own_sums[None], 0.0).reshape(devices, -1)
     sums = jnp.sum(exchange(jnp.concatenate([full_sums, own_sums], axis=1)), axis=0)

time: 630 us -> 609 us (0.967)
  waiting for transfers between devices: 27.8 us -> 0.06 us
    pallas_call x3 -> x5, Pallas kernels: 265 us -> 335 us  [the longest x3 198 us: sum_rows(): pl.pallas_call(functools.partial(sum_kernel, count, pieces, riders), out_...]
    pallas_call x2 -> x1, Pallas kernels: 128 us -> 64.8 us  [gather_rows(): pl.pallas_call(functools.partial(gather_kernel, count, pieces), out_shape...]
    all_to_all x1 -> x0, waiting for transfers between devices: 22.1 us -> none  [columns_to_rows(): lax.all_to_all(slice_in.reshape(count, rows, -1), 'ctx', split_axis=0, co...]
  transfers between devices with their start and end apart: 5 -> 3, of which waited for: 2 -> 0; matrix products, arithmetic and copies ran while one was open for 12% -> 11% of each run, Pallas kernels for 61% -> 52%
where the time goes in v5:
time: 609 us; the launch traced here: 600 us
  Pallas kernels  477 us (78%)
  matrix products  46.7 us (8%)
  local copies, waits for them, and re-layouts  32 us (5%)
  other arithmetic  22.8 us (4%)
  between operations  14.8 us (2%)
  starting transfers between devices  6.36 us (1%)
    pallas_call x3, Pallas kernels, sum_rows(): pl.pallas_call(functools.partial(sum_kernel, count, pieces, riders), out_...  198 us
    pallas_call x2, Pallas kernels, supply(): pl.pallas_call(functools.partial(supply_kernel, count, pieces, tuple(shar...  136 us
    pallas_call x1, Pallas kernels, gather_rows(): pl.pallas_call(functools.partial(gather_kernel, count, pieces), out_shape...  64.8 us
    dot_general x4, matrix products, weight_grad(): lax.dot_general(rows_in, grads, TN, preferred_element_type=F32).astype(BF16)  30.6 us
    pallas_call x1, Pallas kernels, feed(): pl.pallas_call(feed_kernel, grid=(total // block,), in_specs=[wide, wide,...  24.5 us
    pallas_call x1, Pallas kernels, attend_back(): pl.pallas_call(functools.partial(attend_back_kernel, rows, heads), grid=(...  20.4 us
    pallas_call x1, Pallas kernels, attend(): pl.pallas_call(functools.partial(attend_kernel, rows, heads), grid=(seq_l...  19.7 us
    pallas_call x1, Pallas kernels, project(): pl.pallas_call(project_kernel, grid=(total // block,), in_specs=[pl.Block...  13 us
  transfers between devices with their start and end apart: 3, of which 0 were waited for; matrix products, arithmetic and copies ran while one was open for 11% of the time, Pallas kernels for 52%

profile of v5, /device:TPU:0, one launch (start us, length us, event | category | flops | bytes accessed | tf_op | source)
XLA Modules:
  0.0 600.0 jit_solution(4064483026406496972)
XLA Ops:
  7.2 6.1 %concatenate.23 = bf16[768]{0:T(1024)(128)(2,1)S(1)} concatenate(bf16[64]{0:T(256)(128)(2,1)} %param.18, bf16[64]{0:T(256)(128)(2,1)} %param.19, bf16[64]{0:T(256)(128)(2,1)} %param.24, bf16[64]{0:T(256)(128)(2,1)} %param.25, bf16[64]{0:T(256)(128)(2,1)} %param.26, bf16[64]{0:T(256)(128)(2,1)} %param.30, bf16[64]{0:T(256)(128)(2,1)} %param.21, bf16[64]{0:T(256)(128)(2,1)} %param.22, ...), dimensions={0} | concatenate | bytes 3072 | tf_op jit(solution)/shard_map/concatenate | solution.py:1107
  13.3 0.6 bitcast_convert_fusion.refs_2_
  13.9 68.3 %begin.1 = (bf16[16,128,2048]{2,1,0:T(8,128)(2,1)}, bf16[32,64,384]{2,1,0:T(8,128)(2,1)}, f32[32,8,128]{2,1,0:T(8,128)}, bf16[2,64,2048]{2,1,0:T(8,128)(2,1)}) custom-call(bf16[128,2048]{1,0:T(8,128)(2,1)} %bitcast.140, bf16[64,6144]{1,0:T(8,128)(2,1)} %refs_1_.2, f32[8,128]{1,0:T(8,128)} %bitcast_convert_fusion.refs_2_, bf16[64,2048]{1,0:T(8,128)(2,1)} %refs_3_.1), custom_call_target="tpu_custom_call" | custom-call | bytes 167772160 | tf_op jit(solution)/shard_map/begin/pallas_call | solution.py:648
  82.7 0.9 copy.84
  83.9 0.7 broadcast_in_dim_reshape.4.gain_ref
  85.0 0.6 broadcast_in_dim.70.bias_ref
  85.6 0.7 broadcast_in_dim_reshape.5.shift_ref
  86.2 0.5 multiply_power_fusion.slope_ref
  86.8 13.0 %project.1 = (bf16[2048,2048]{1,0:T(8,128)(2,1)}, bf16[2048,384]{1,0:T(8,128)(2,1)}) custom-call(bf16[2048,2048]{1,0:T(8,128)(2,1)} %bitcast.192, f32[1,2048]{1,0:T(1,128)} %broadcast_in_dim_reshape.4.gain_ref, f32[1,2048]{1,0:T(1,128)} %broadcast_in_dim_reshape.5.shift_ref, bf16[2048,384]{1,0:T(8,128)(2,1)} %bitcast.193, f32[1,384]{1,0:T(1,128)} %broadcast_in_dim.70.bias_ref), custom_call_target="tpu_custom_call" | custom-call | flops 3221225472 | bytes 25165824 | tf_op jit(solution)/shard_map/project/pallas_call | solution.py:690
  99.7 1.5 slice_bitcast_fusion.1
  101.6 0.5 and_select_fusion.low_ref
  102.1 1.2 fusion.18
  103.3 19.7 %attend.1 = (f32[2048,128]{1,0:T(8,128)}, f32[2,2048]{1,0:T(2,128)}) custom-call(s32[8]{0:T(128)} %and_select_fusion.low_ref, f32[2]{0:T(128)} %multiply_power_fusion.slope_ref, s32[1,2048]{1,0:T(1,128)} %bitcast.187, bf16[2048,128]{1,0:T(8,128)(2,1)} %get-tuple-element.103.q_ref, bf16[2048,128]{1,0:T(8,128)(2,1)} %get-tuple-element.102.k_ref, ...), custom_call_target="tpu_custom_call" | custom-call | bytes 55924052 | tf_op jit(solution)/shard_map/attend/pallas_call | solution.py:153
  123.0 1.3 convert_element_type.107
  124.5 5.5 convolution_convert_fusion.1
  130.1 65.0 %sum_rows.3 = f32[128,2048]{1,0:T(8,128)} custom-call(bf16[16,128,2048]{2,1,0:T(8,128)(2,1)} %bitcast.139), custom_call_target="tpu_custom_call" | custom-call | bytes 167772160 | tf_op jit(solution)/shard_map/sum_rows/pallas_call | solution.py:1029
  195.1 0.7 dynamic_slice.17
  195.9 1.6 fusion.16
  197.8 0.7 copy-done.1
  198.5 1.0 add_convert_fusion.1.refs_0_
  199.5 68.1 %middle.1 = (bf16[16,128,2048]{2,1,0:T(8,128)(2,1)}, bf16[32,64,512]{2,1,0:T(8,128)(2,1)}, bf16[2,256,2048]{2,1,0:T(8,128)(2,1)}) custom-call(bf16[128,2048]{1,0:T(8,128)(2,1)} %add_convert_fusion.1.refs_0_, bf16[64,8192]{1,0:T(8,128)(2,1)} %refs_1_.3, bf16[256,2048]{1,0:T(8,128)(2,1)} %refs_2_.1), custom_call_target="tpu_custom_call" | custom-call | bytes 167772160 | tf_op jit(solution)/shard_map/middle/pallas_call | solution.py:648
  267.7 24.5 %feed.1 = (bf16[2048,512]{1,0:T(8,128)(2,1)}, bf16[2048,512]{1,0:T(8,128)(2,1)}, bf16[2048,2048]{1,0:T(8,128)(2,1)}, bf16[2048,2048]{1,0:T(8,128)(2,1)}, f32[1,512]{1,0:T(1,128)}) custom-call(bf16[2048,2048]{1,0:T(8,128)(2,1)} %bitcast.146, bf16[2048,2048]{1,0:T(8,128)(2,1)} %all-gather.2.cloned.1.call-done.grad_ref, bf16[2048,512]{1,0:T(8,128)(2,1)} %bitcast.165, ...), custom_call_target="tpu_custom_call" | custom-call | bytes 55924052 | tf_op jit(solution)/shard_map/feed/pallas_call | solution.py:744
  292.3 10.1 %convolution_convert_fusion.2 = bf16[512,2048]{1,0:T(8,128)(2,1)} fusion(bf16[2048,512]{1,0:T(8,128)(2,1)} %get-tuple-element.65, bf16[2048,2048]{1,0:T(8,128)(2,1)} %all-gather.2.cloned.1.call-done.grad_ref), kind=kOutput, calls=%fused_computation.3 | convolution fusion | flops 4296015872 | bytes 12582912 | tf_op jit(solution)/shard_map/dot_general | solution.py:1056
  302.3 5.7 convolution_convert_fusion.3
  308.1 69.4 %sum_rows.4 = (f32[128,2048]{1,0:T(8,128)}, bf16[16,64,512]{2,1,0:T(8,128)(2,1)}, bf16[256,2048]{1,0:T(8,128)(2,1)}) custom-call(bf16[16,128,2048]{2,1,0:T(8,128)(2,1)} %bitcast.144, bf16[16,2,64,512]{3,2,1,0:T(8,128)(2,1)} %bitcast.163, bf16[2,256,2048]{2,1,0:T(8,128)(2,1)} %bitcast.151), custom_call_target="tpu_custom_call" | custom-call | bytes 167772160 | tf_op jit(solution)/shard_map/sum_rows/pallas_call | solution.py:1029
  377.5 2.1 multiply_reduce_fusion
  379.6 2.9 fusion.15
  382.8 0.5 broadcast.130
  383.4 0.7 reduce.3
  384.2 64.8 %gather_rows.1 = bf16[16,128,2048]{2,1,0:T(8,128)(2,1)} custom-call(bf16[128,2048]{1,0:T(8,128)(2,1)} %get-tuple-element.70.own_ref), custom_call_target="tpu_custom_call" | custom-call | bytes 167772160 | tf_op jit(solution)/shard_map/gather_rows/pallas_call | solution.py:388
  449.3 5.6 convolution_convert_fusion.5
  454.9 0.3 copy-done
  455.4 2.4 convolution_convert_fusion.6
  458.0 1.1 copy-done.14
  459.1 1.1 convert_multiply_fusion
  460.3 1.6 copy.62
  461.8 0.7 bitcast_reduce_fusion
  462.5 20.4 %attend_back.1 = (bf16[2048,128]{1,0:T(8,128)(2,1)}, bf16[2048,128]{1,0:T(8,128)(2,1)}, bf16[2048,128]{1,0:T(8,128)(2,1)}) custom-call(s32[8]{0:T(128)} %and_select_fusion.low_ref, f32[2]{0:T(128)} %multiply_power_fusion.slope_ref, s32[1,2048]{1,0:T(1,128)} %bitcast.188, f32[2,2048]{1,0:T(2,128)} %get-tuple-element.69.total_ref, f32[2,2048]{1,0:T(2,128)} %bitcast.189, ...), custom_call_target="tpu_custom_call" | custom-call | bytes 55924052 | tf_op jit(solution)/shard_map/attend_back/pallas_call | solution.py:175
  482.9 1.1 fusion.19
  484.1 1.1 fusion.20
  485.4 9.2 %convolution_convert_fusion.4 = bf16[2048,384]{1,0:T(8,128)(2,1)} fusion(bf16[2048,2048]{1,0:T(8,128)(2,1)} %get-tuple-element.74, bf16[2048,128]{1,0:T(8,128)(2,1)S(1)} %bitcast.160, bf16[2048,128]{1,0:T(8,128)(2,1)S(1)} %bitcast.157, bf16[2048,128]{1,0:T(8,128)(2,1)S(1)} %bitcast.154), kind=kOutput, calls=%fused_computation.5 | convolution fusion | flops 3226730496 | bytes 11534336 | tf_op jit(solution)/shard_map/dot_general | solution.py:1056
  494.6 0.4 convert_reduce_fusion
  495.3 8.2 %convolution_convert_fusion = bf16[2048,2048]{1,0:T(8,128)(2,1)} fusion(bf16[2048,384]{1,0:T(8,128)(2,1)} %bitcast.194, bf16[2048,128]{1,0:T(8,128)(2,1)S(1)} %bitcast.162, bf16[2048,128]{1,0:T(8,128)(2,1)S(1)} %bitcast.159, bf16[2048,128]{1,0:T(8,128)(2,1)S(1)} %bitcast.156), kind=kOutput, calls=%fused_computation | convolution fusion | flops 3230138368 | bytes 11534336 | tf_op jit(solution)/shard_map/dot_general | solution.py:1189
  503.5 64.0 %sum_rows.5 = (f32[128,2048]{1,0:T(8,128)}, bf16[16,64,384]{2,1,0:T(8,128)(2,1)}, bf16[64,2048]{1,0:T(8,128)(2,1)}) custom-call(bf16[16,128,2048]{2,1,0:T(8,128)(2,1)} %bitcast.143, bf16[16,2,64,384]{3,2,1,0:T(8,128)(2,1)} %bitcast.167, bf16[2,64,2048]{2,1,0:T(8,128)(2,1)} %bitcast.152), custom_call_target="tpu_custom_call" | custom-call | bytes 167772160 | tf_op jit(solution)/shard_map/sum_rows/pallas_call | solution.py:1029
  567.6 2.2 convert_element_type.113
  569.8 0.5 fusion.10
  570.7 0.7 copy.74
  571.4 6.3 %all-to-all-start = ((f32[32,8,128]{2,1,0:T(8,128)}), f32[32,8,128]{2,1,0:T(8,128)S(1)}, u32[]{:S(2)}, u32[]{:S(2)}) async-start(f32[32,8,128]{2,1,0:T(8,128)} %bitcast.73), calls=%async_computation.1 | async-start | bytes 262144 | tf_op jit(solution)/shard_map/all_to_all | solution.py:209
  577.7 2.4 reshape.303
  580.1 0.9 copy.66
  581.0 1.6 copy.82
  582.7 0.3 fusion.26
  583.0 1.5 copy.77
  584.5 0.8 copy-done.9
  585.3 0.3 copy-done.18
  585.6 1.7 convert_add_fusion
  587.3 0.4 copy-done.15
  587.7 0.9 fusion.13
  588.6 0.5 copy-done.12
  589.1 0.3 copy-done.13
  589.4 1.4 fusion.9
  590.9 0.9 convert_add_fusion.3
  591.8 0.6 slice.168
  592.3 0.6 fusion.24
  (120 shorter events, 4.2 us)
Async XLA Ops:
  7.2 75.1 %copy-start.27 = (s32[1,8]{1,0:T(1,128)S(1)}, s32[1,8]{1,0:T(1,128)}, u32[]{:S(2)}) copy-start(s32[1,8]{1,0:T(1,128)} %param.17) | copy-start | bytes 100
  7.2 260.5 %all-gather.2.cloned.1.call-start = ((), (), s32[]{:S(2)}) async-start(), calls=%async_computation.2 | async-start | bytes 8912896 | tf_op jit(solution)/shard_map/all_gather | solution.py:198
  82.3 485.4 %reduce-scatter.2.cloned.1.call-start = ((), (), s32[]{:S(2)}) async-start(), calls=%async_computation.3 | async-start | bytes 8912896 | tf_op jit(solution)/shard_map/reduce_scatter | solution.py:202
  82.6 17.1 %copy-start.24 = (s32[2048]{0:T(1024)}, s32[2048]{0:T(1024)S(1)}, u32[]{:S(2)}) copy-start(s32[2048]{0:T(1024)S(1)} %select_reduce_fusion) | copy-start | bytes 24580
  123.0 1.5 copy-start.21
  124.5 5.6 copy-start.5
  130.1 65.6 %copy-start.4 = (bf16[1,128,2048]{2,1,0:T(8,128)(2,1)S(1)}, bf16[1,128,2048]{2,1,0:T(8,128)(2,1)}, u32[]{:S(2)}) copy-start(bf16[1,128,2048]{2,1,0:T(8,128)(2,1)} %param.16) | copy-start | bytes 1572868
  197.5 1.0 copy-start.1
  292.2 10.1 %copy-start.7 = (bf16[16,128,2048]{2,1,0:T(8,128)(2,1)S(1)}, bf16[16,128,2048]{2,1,0:T(8,128)(2,1)}, u32[]{:S(2)}) copy-start(bf16[16,128,2048]{2,1,0:T(8,128)(2,1)} %get-tuple-element.59) | copy-start | bytes 25165828
  292.3 10.1 %copy-start.26 = (bf16[2048,512]{1,0:T(8,128)(2,1)S(1)}, bf16[2048,512]{1,0:T(8,128)(2,1)}, u32[]{:S(2)}) copy-start(bf16[2048,512]{1,0:T(8,128)(2,1)} %get-tuple-element.64) | copy-start | bytes 6291460
  377.5 2.1 copy-start.2
  377.5 2.2 copy-start.16
  382.5 0.9 copy-start.25
  384.2 64.8 %copy-start.10 = (bf16[128,2048]{1,0:T(8,128)(2,1)S(1)}, bf16[128,2048]{1,0:T(8,128)(2,1)}, u32[]{:S(2)}) copy-start(bf16[128,2048]{1,0:T(8,128)(2,1)} %get-tuple-element.70.own_ref) | copy-start | bytes 1572868
  384.2 65.1 %copy-start.6 = (bf16[16,2,64,128]{3,2,1,0:T(8,128)(2,1)S(1)}, bf16[16,2,64,128]{3,2,1,0:T(8,128)(2,1)}, u32[]{:S(2)}) copy-start(bf16[16,2,64,128]{3,2,1,0:T(8,128)(2,1)} %copy-done.5) | copy-start | bytes 1572868
  449.3 6.0 copy-start
  449.3 6.1 %copy-start.22 = (bf16[2,64,2048]{2,1,0:T(8,128)(2,1)S(1)}, bf16[2,64,2048]{2,1,0:T(8,128)(2,1)}, u32[]{:S(2)}) copy-start(bf16[2,64,2048]{2,1,0:T(8,128)(2,1)} %get-tuple-element.58) | copy-start | bytes 1572868
  457.9 1.3 copy-start.14
  459.1 2.7 copy-start.8
  482.9 2.3 copy-start.20
  567.5 2.3 copy-start.11
  571.4 20.3 %all-to-all-start = ((f32[32,8,128]{2,1,0:T(8,128)}), f32[32,8,128]{2,1,0:T(8,128)S(1)}, u32[]{:S(2)}, u32[]{:S(2)}) async-start(f32[32,8,128]{2,1,0:T(8,128)} %bitcast.73), calls=%async_computation.1 | async-start | bytes 262144 | tf_op jit(solution)/shard_map/all_to_all | solution.py:209
  581.0 1.6 copy-start.19
  582.9 2.4 copy-start.9
  583.0 2.6 copy-start.18
  585.6 1.7 copy-start.3
  585.6 2.1 copy-start.15
  587.7 1.4 copy-start.12
  587.7 1.7 copy-start.13
  588.6 2.2 copy-start.17
  588.6 2.2 copy-start.23
Sparse Core Ops, SparseCore 0:
  82.4 84.0 all-gather.1
  382.6 111.9 reduce-scatter.1

commit v6 on v5

--- a/solution.py
+++ b/solution.py
@@ -1183,6 +1183,7 @@
     grad_qkv = jnp.concatenate(
         [narrow(to_layout(part, count), share) for part in grad_parts], axis=1
     )
+    grad_qkv = lax.optimization_barrier(grad_qkv)
     column_sums = jnp.sum(grad_qkv.astype(F32), axis=0)
     w_out_terms = weight_grad(attended_own, grad_branch_all)
     grad_normed, w_qkv_got, w_out_other = sum_rows(

time: 609 us -> 610 us (level)
  no operation moved by 1% of the time
where the time goes in v6:
time: 610 us; the launch traced here: 600 us
  Pallas kernels  477 us (78%)
  matrix products  46.8 us (8%)
  local copies, waits for them, and re-layouts  32 us (5%)
  other arithmetic  22.9 us (4%)
  between operations  14.8 us (2%)
  starting transfers between devices  6.99 us (1%)
    pallas_call x3, Pallas kernels, sum_rows(): pl.pallas_call(functools.partial(sum_kernel, count, pieces, riders), out_...  203 us
    pallas_call x2, Pallas kernels, supply(): pl.pallas_call(functools.partial(supply_kernel, count, pieces, tuple(shar...  136 us
    pallas_call x1, Pallas kernels, gather_rows(): pl.pallas_call(functools.partial(gather_kernel, count, pieces), out_shape...  65.5 us
    dot_general x4, matrix products, weight_grad(): lax.dot_general(rows_in, grads, TN, preferred_element_type=F32).astype(BF16)  30.7 us
    pallas_call x1, Pallas kernels, feed(): pl.pallas_call(feed_kernel, grid=(total // block,), in_specs=[wide, wide,...  24.5 us
    pallas_call x1, Pallas kernels, attend_back(): pl.pallas_call(functools.partial(attend_back_kernel, rows, heads), grid=(...  17.2 us
    pallas_call x1, Pallas kernels, attend(): pl.pallas_call(functools.partial(attend_kernel, rows, heads), grid=(seq_l...  16.7 us
    pallas_call x1, Pallas kernels, project(): pl.pallas_call(project_kernel, grid=(total // block,), in_specs=[pl.Block...  13 us
  transfers between devices with their start and end apart: 3, of which 0 were waited for; matrix products, arithmetic and copies ran while one was open for 11% of the time, Pallas kernels for 52%

profile of v6, /device:TPU:0, one launch (start us, length us, event | category | flops | bytes accessed | tf_op | source)
XLA Modules:
  0.0 600.1 jit_solution(823770019231954479)
XLA Ops:
  7.2 6.1 %concatenate.23 = bf16[768]{0:T(1024)(128)(2,1)S(1)} concatenate(bf16[64]{0:T(256)(128)(2,1)} %param.18, bf16[64]{0:T(256)(128)(2,1)} %param.19, bf16[64]{0:T(256)(128)(2,1)} %param.24, bf16[64]{0:T(256)(128)(2,1)} %param.25, bf16[64]{0:T(256)(128)(2,1)} %param.26, bf16[64]{0:T(256)(128)(2,1)} %param.30, bf16[64]{0:T(256)(128)(2,1)} %param.21, bf16[64]{0:T(256)(128)(2,1)} %param.22, ...), dimensions={0} | concatenate | bytes 3072 | tf_op jit(solution)/shard_map/concatenate | solution.py:1107
  13.3 0.6 bitcast_convert_fusion.refs_2_
  13.9 68.3 %begin.1 = (bf16[16,128,2048]{2,1,0:T(8,128)(2,1)}, bf16[32,64,384]{2,1,0:T(8,128)(2,1)}, f32[32,8,128]{2,1,0:T(8,128)}, bf16[2,64,2048]{2,1,0:T(8,128)(2,1)}) custom-call(bf16[128,2048]{1,0:T(8,128)(2,1)} %bitcast.142, bf16[64,6144]{1,0:T(8,128)(2,1)} %refs_1_.2, f32[8,128]{1,0:T(8,128)} %bitcast_convert_fusion.refs_2_, bf16[64,2048]{1,0:T(8,128)(2,1)} %refs_3_.1), custom_call_target="tpu_custom_call" | custom-call | bytes 167772160 | tf_op jit(solution)/shard_map/begin/pallas_call | solution.py:648
  82.7 0.9 copy.84
  83.9 0.7 broadcast_in_dim_reshape.4.gain_ref
  85.0 0.6 broadcast_in_dim.70.bias_ref
  85.6 0.7 broadcast_in_dim_reshape.5.shift_ref
  86.2 0.5 multiply_power_fusion.slope_ref
  86.8 13.0 %project.1 = (bf16[2048,2048]{1,0:T(8,128)(2,1)}, bf16[2048,384]{1,0:T(8,128)(2,1)}) custom-call(bf16[2048,2048]{1,0:T(8,128)(2,1)} %bitcast.188, f32[1,2048]{1,0:T(1,128)} %broadcast_in_dim_reshape.4.gain_ref, f32[1,2048]{1,0:T(1,128)} %broadcast_in_dim_reshape.5.shift_ref, bf16[2048,384]{1,0:T(8,128)(2,1)} %bitcast.189, f32[1,384]{1,0:T(1,128)} %broadcast_in_dim.70.bias_ref), custom_call_target="tpu_custom_call" | custom-call | flops 3221225472 | bytes 25165824 | tf_op jit(solution)/shard_map/project/pallas_call | solution.py:690
  99.7 1.5 slice_bitcast_fusion.1
  101.6 0.5 and_select_fusion.low_ref
  102.1 1.2 fusion.18
  103.3 16.7 %attend.1 = (f32[2048,128]{1,0:T(8,128)}, f32[2,2048]{1,0:T(2,128)}) custom-call(s32[8]{0:T(128)} %and_select_fusion.low_ref, f32[2]{0:T(128)} %multiply_power_fusion.slope_ref, s32[1,2048]{1,0:T(1,128)} %bitcast.183, bf16[2048,128]{1,0:T(8,128)(2,1)} %get-tuple-element.103.q_ref, bf16[2048,128]{1,0:T(8,128)(2,1)} %get-tuple-element.102.k_ref, ...), custom_call_target="tpu_custom_call" | custom-call | bytes 55924052 | tf_op jit(solution)/shard_map/attend/pallas_call | solution.py:153
  120.1 1.3 convert_element_type.107
  121.6 5.5 convolution_convert_fusion.1
  127.1 68.3 %sum_rows.3 = f32[128,2048]{1,0:T(8,128)} custom-call(bf16[16,128,2048]{2,1,0:T(8,128)(2,1)} %bitcast.141), custom_call_target="tpu_custom_call" | custom-call | bytes 167772160 | tf_op jit(solution)/shard_map/sum_rows/pallas_call | solution.py:1029
  195.4 0.7 dynamic_slice.17
  196.3 1.6 fusion.16
  198.2 0.7 copy-done.1
  198.9 1.0 add_convert_fusion.1.refs_0_
  199.9 68.1 %middle.1 = (bf16[16,128,2048]{2,1,0:T(8,128)(2,1)}, bf16[32,64,512]{2,1,0:T(8,128)(2,1)}, bf16[2,256,2048]{2,1,0:T(8,128)(2,1)}) custom-call(bf16[128,2048]{1,0:T(8,128)(2,1)} %add_convert_fusion.1.refs_0_, bf16[64,8192]{1,0:T(8,128)(2,1)} %refs_1_.3, bf16[256,2048]{1,0:T(8,128)(2,1)} %refs_2_.1), custom_call_target="tpu_custom_call" | custom-call | bytes 167772160 | tf_op jit(solution)/shard_map/middle/pallas_call | solution.py:648
  268.1 24.5 %feed.1 = (bf16[2048,512]{1,0:T(8,128)(2,1)}, bf16[2048,512]{1,0:T(8,128)(2,1)}, bf16[2048,2048]{1,0:T(8,128)(2,1)}, bf16[2048,2048]{1,0:T(8,128)(2,1)}, f32[1,512]{1,0:T(1,128)}) custom-call(bf16[2048,2048]{1,0:T(8,128)(2,1)} %bitcast.148, bf16[2048,2048]{1,0:T(8,128)(2,1)} %all-gather.2.cloned.1.call-done.grad_ref, bf16[2048,512]{1,0:T(8,128)(2,1)} %bitcast.161, ...), custom_call_target="tpu_custom_call" | custom-call | bytes 55924052 | tf_op jit(solution)/shard_map/feed/pallas_call | solution.py:744
  292.6 10.1 %convolution_convert_fusion.2 = bf16[512,2048]{1,0:T(8,128)(2,1)} fusion(bf16[2048,512]{1,0:T(8,128)(2,1)} %get-tuple-element.65, bf16[2048,2048]{1,0:T(8,128)(2,1)} %all-gather.2.cloned.1.call-done.grad_ref), kind=kOutput, calls=%fused_computation.3 | convolution fusion | flops 4296015872 | bytes 12582912 | tf_op jit(solution)/shard_map/dot_general | solution.py:1056
  302.7 5.7 convolution_convert_fusion.3
  308.4 69.1 %sum_rows.4 = (f32[128,2048]{1,0:T(8,128)}, bf16[16,64,512]{2,1,0:T(8,128)(2,1)}, bf16[256,2048]{1,0:T(8,128)(2,1)}) custom-call(bf16[16,128,2048]{2,1,0:T(8,128)(2,1)} %bitcast.146, bf16[16,2,64,512]{3,2,1,0:T(8,128)(2,1)} %bitcast.159, bf16[2,256,2048]{2,1,0:T(8,128)(2,1)} %bitcast.153), custom_call_target="tpu_custom_call" | custom-call | bytes 167772160 | tf_op jit(solution)/shard_map/sum_rows/pallas_call | solution.py:1029
  377.6 2.1 multiply_reduce_fusion
  379.7 2.9 fusion.15
  383.0 0.5 broadcast.130
  383.5 0.7 reduce.3
  384.3 65.5 %gather_rows.1 = bf16[16,128,2048]{2,1,0:T(8,128)(2,1)} custom-call(bf16[128,2048]{1,0:T(8,128)(2,1)} %get-tuple-element.70.own_ref), custom_call_target="tpu_custom_call" | custom-call | bytes 167772160 | tf_op jit(solution)/shard_map/gather_rows/pallas_call | solution.py:388
  450.1 5.7 convolution_convert_fusion.5
  455.8 0.3 copy-done
  456.3 2.4 convolution_convert_fusion.6
  458.9 1.1 copy-done.14
  460.0 1.1 convert_multiply_fusion
  461.1 1.6 copy.62
  462.7 0.7 bitcast_reduce_fusion
  463.4 17.2 %attend_back.1 = (bf16[2048,128]{1,0:T(8,128)(2,1)}, bf16[2048,128]{1,0:T(8,128)(2,1)}, bf16[2048,128]{1,0:T(8,128)(2,1)}) custom-call(s32[8]{0:T(128)} %and_select_fusion.low_ref, f32[2]{0:T(128)} %multiply_power_fusion.slope_ref, s32[1,2048]{1,0:T(1,128)} %bitcast.184, f32[2,2048]{1,0:T(2,128)} %get-tuple-element.69.total_ref, f32[2,2048]{1,0:T(2,128)} %bitcast.185, ...), custom_call_target="tpu_custom_call" | custom-call | bytes 55924052 | tf_op jit(solution)/shard_map/attend_back/pallas_call | solution.py:175
  480.6 1.1 fusion.19
  481.7 1.1 fusion.20
  483.3 9.2 %convolution_convert_fusion.4 = bf16[2048,384]{1,0:T(8,128)(2,1)} fusion(bf16[2048,2048]{1,0:T(8,128)(2,1)} %get-tuple-element.74, bf16[2048,384]{1,0:T(8,128)(2,1)S(1)} %pad_maximum_fusion.1), kind=kOutput, calls=%fused_computation.5 | convolution fusion | flops 3222011904 | bytes 11534336 | tf_op jit(solution)/shard_map/dot_general | solution.py:1056
  492.5 0.3 convert_reduce_fusion
  493.1 8.2 %convolution_convert_fusion = bf16[2048,2048]{1,0:T(8,128)(2,1)} fusion(bf16[2048,384]{1,0:T(8,128)(2,1)S(1)} %pad_maximum_fusion.1, bf16[2048,384]{1,0:T(8,128)(2,1)} %bitcast.190), kind=kOutput, calls=%fused_computation | convolution fusion | flops 3225419776 | bytes 11534336 | tf_op jit(solution)/shard_map/dot_general | solution.py:1190
  501.3 65.8 %sum_rows.5 = (f32[128,2048]{1,0:T(8,128)}, bf16[16,64,384]{2,1,0:T(8,128)(2,1)}, bf16[64,2048]{1,0:T(8,128)(2,1)}) custom-call(bf16[16,128,2048]{2,1,0:T(8,128)(2,1)} %bitcast.145, bf16[16,2,64,384]{3,2,1,0:T(8,128)(2,1)} %bitcast.163, bf16[2,64,2048]{2,1,0:T(8,128)(2,1)} %bitcast.154), custom_call_target="tpu_custom_call" | custom-call | bytes 167772160 | tf_op jit(solution)/shard_map/sum_rows/pallas_call | solution.py:1029
  567.1 2.2 convert_element_type.113
  569.3 0.5 fusion.10
  570.2 0.7 copy.74
  570.9 6.9 %all-to-all-start = ((f32[32,8,128]{2,1,0:T(8,128)}), f32[32,8,128]{2,1,0:T(8,128)S(1)}, u32[]{:S(2)}, u32[]{:S(2)}) async-start(f32[32,8,128]{2,1,0:T(8,128)} %bitcast.73), calls=%async_computation.1 | async-start | bytes 262144 | tf_op jit(solution)/shard_map/all_to_all | solution.py:209
  577.8 2.4 reshape.303
  580.3 0.9 copy.66
  581.2 1.6 copy.82
  582.8 0.3 fusion.26
  583.1 1.5 copy.77
  584.6 0.8 copy-done.9
  585.4 0.3 copy-done.18
  585.7 1.7 convert_add_fusion
  587.4 0.4 copy-done.15
  587.8 0.9 fusion.13
  588.8 0.5 copy-done.12
  589.2 0.3 copy-done.13
  589.6 1.4 fusion.9
  591.0 0.9 convert_add_fusion.3
  591.9 0.6 slice.168
  592.5 0.6 fusion.24
  (121 shorter events, 4.4 us)
Async XLA Ops:
  7.2 75.1 %copy-start.27 = (s32[1,8]{1,0:T(1,128)S(1)}, s32[1,8]{1,0:T(1,128)}, u32[]{:S(2)}) copy-start(s32[1,8]{1,0:T(1,128)} %param.17) | copy-start | bytes 100
  7.2 260.9 %all-gather.2.cloned.1.call-start = ((), (), s32[]{:S(2)}) async-start(), calls=%async_computation.2 | async-start | bytes 8912896 | tf_op jit(solution)/shard_map/all_gather | solution.py:198
  82.3 484.9 %reduce-scatter.2.cloned.1.call-start = ((), (), s32[]{:S(2)}) async-start(), calls=%async_computation.3 | async-start | bytes 8912896 | tf_op jit(solution)/shard_map/reduce_scatter | solution.py:202
  82.6 17.1 %copy-start.24 = (s32[2048]{0:T(1024)}, s32[2048]{0:T(1024)S(1)}, u32[]{:S(2)}) copy-start(s32[2048]{0:T(1024)S(1)} %select_reduce_fusion) | copy-start | bytes 24580
  120.1 1.5 copy-start.21
  121.5 5.6 copy-start.5
  127.1 69.0 %copy-start.4 = (bf16[1,128,2048]{2,1,0:T(8,128)(2,1)S(1)}, bf16[1,128,2048]{2,1,0:T(8,128)(2,1)}, u32[]{:S(2)}) copy-start(bf16[1,128,2048]{2,1,0:T(8,128)(2,1)} %param.16) | copy-start | bytes 1572868
  197.9 1.0 copy-start.1
  292.6 10.1 %copy-start.7 = (bf16[16,128,2048]{2,1,0:T(8,128)(2,1)S(1)}, bf16[16,128,2048]{2,1,0:T(8,128)(2,1)}, u32[]{:S(2)}) copy-start(bf16[16,128,2048]{2,1,0:T(8,128)(2,1)} %get-tuple-element.59) | copy-start | bytes 25165828
  292.6 10.1 %copy-start.26 = (bf16[2048,512]{1,0:T(8,128)(2,1)S(1)}, bf16[2048,512]{1,0:T(8,128)(2,1)}, u32[]{:S(2)}) copy-start(bf16[2048,512]{1,0:T(8,128)(2,1)} %get-tuple-element.64) | copy-start | bytes 6291460
  377.6 2.1 copy-start.2
  377.6 2.2 copy-start.16
  382.6 0.9 copy-start.25
  384.3 65.5 %copy-start.10 = (bf16[128,2048]{1,0:T(8,128)(2,1)S(1)}, bf16[128,2048]{1,0:T(8,128)(2,1)}, u32[]{:S(2)}) copy-start(bf16[128,2048]{1,0:T(8,128)(2,1)} %get-tuple-element.70.own_ref) | copy-start | bytes 1572868
  384.3 65.8 %copy-start.6 = (bf16[16,2,64,128]{3,2,1,0:T(8,128)(2,1)S(1)}, bf16[16,2,64,128]{3,2,1,0:T(8,128)(2,1)}, u32[]{:S(2)}) copy-start(bf16[16,2,64,128]{3,2,1,0:T(8,128)(2,1)} %copy-done.5) | copy-start | bytes 1572868
  450.1 6.1 %copy-start = (bf16[16,128,2048]{2,1,0:T(8,128)(2,1)S(1)}, bf16[16,128,2048]{2,1,0:T(8,128)(2,1)}, u32[]{:S(2)}) copy-start(bf16[16,128,2048]{2,1,0:T(8,128)(2,1)} %gather_rows.1) | copy-start | bytes 25165828
  450.1 6.2 %copy-start.22 = (bf16[2,64,2048]{2,1,0:T(8,128)(2,1)S(1)}, bf16[2,64,2048]{2,1,0:T(8,128)(2,1)}, u32[]{:S(2)}) copy-start(bf16[2,64,2048]{2,1,0:T(8,128)(2,1)} %get-tuple-element.58) | copy-start | bytes 1572868
  458.8 1.2 copy-start.14
  460.0 2.7 copy-start.8
  480.6 2.3 copy-start.20
  567.1 2.3 copy-start.11
  570.9 20.9 %all-to-all-start = ((f32[32,8,128]{2,1,0:T(8,128)}), f32[32,8,128]{2,1,0:T(8,128)S(1)}, u32[]{:S(2)}, u32[]{:S(2)}) async-start(f32[32,8,128]{2,1,0:T(8,128)} %bitcast.73), calls=%async_computation.1 | async-start | bytes 262144 | tf_op jit(solution)/shard_map/all_to_all | solution.py:209
  581.2 1.6 copy-start.19
  583.1 2.4 copy-start.9
  583.1 2.6 copy-start.18
  585.7 1.7 copy-start.3
  585.7 2.1 copy-start.15
  587.8 1.4 copy-start.12
  587.8 1.7 copy-start.13
  588.8 2.2 copy-start.17
  588.8 2.2 copy-start.23
Sparse Core Ops, SparseCore 0:
  82.4 84.9 all-gather.1
  382.7 111.8 reduce-scatter.1
